TPU v7x, 32 devices: a whole 2x2x4 slice. The times are simulated.
32 devices in a mesh: dp: 8 (over z, x), tensor: 4 (over y, core).
Axes of the slice: x: 2, y: 2, z: 4, core: 2. Of those that a mesh axis runs over, the one named last changes fastest.
Arguments:
- tokens: bfloat16 [2048, 2048], P('dp'), may hold values from -6 to 6
- cotangent: bfloat16 [2048, 2048], P('dp'), may hold values from -6 to 6
- lengths: int32 [16], P('dp'), may hold values from 32 to 128, as said below
- master: float32 [4, 23389184], P('tensor', 'dp'), may hold values from -8 to 8
- moment_one: float32 [4, 23389184], P('tensor', 'dp'), may hold values from -60 to 60
- moment_two: float32 [4, 23389184], P('tensor', 'dp'), may hold values from 10 to 1000
Outputs:
- output: bfloat16 [2048, 2048], P('dp')
- input_grad: float32 [2048, 2048], P('dp')
- master_new: float32 [4, 23389184], P('tensor', 'dp')
- moment_one_new: float32 [4, 23389184], P('tensor', 'dp')
- moment_two_new: float32 [4, 23389184], P('tensor', 'dp')
- weights_copy: bfloat16 [4, 23389184], P('tensor', 'dp')
- weight_grads: float32 [4, 23389184], P('tensor', 'dp')
- norms: float32 [19, 2], replicated
Inputs may be any that keep to these rules, and one draw needn't show every extreme that they name: `lengths`: each slot's valid rows form a prefix of the slot; in every draw some slot is full.
All inputs are finite; a program needn't handle non-finite values.
Results may differ from a plain program's by a relative error of at most 0.038.
Values may be sent and summed in bfloat16 or wider, within the bound.
A program may use at most 576 MiB of HBM per device.

v0:
```python
import math

import jax
import jax.numpy as jnp
from jax import lax
from jax.sharding import PartitionSpec as P

D = 2048
INNER = 4096
NSTATE = 16
DTR = 128
HEADS = 32
HEAD_DIM = 64
FF = 4096
CONV = 4
WINDOW = 2048
SPAN = 16
MICRO = 2
SLOT = 128


EPS_NORM = 1e-05
TRUST_EPSILON = 1e-06
ROPE_BASE = 10000.0
BETA_ONE = 0.5
BETA_TWO = 0.55
ADAM_EPS = 1e-06
DECAY_W = 0.01
LEARN_RATE = 0.2
NEG_FILL = -1e30
PRECISE = lax.Precision.HIGHEST


def layout(d_model, e_in, f_in, h_width, n_state, conv_len, dt_rank, d_gain):
    entries = [
        ("gain", (4, d_gain)),
        ("w_in", (d_model, 2 * e_in)),
        ("conv_w", (conv_len, e_in)),
        ("conv_b", (e_in,)),
        ("dt_bias", (e_in,)),
        ("d_skip", (e_in,)),
        ("a_log", (n_state, e_in)),
        ("w_x", (e_in, dt_rank + 2 * n_state)),
        ("w_dt", (dt_rank, e_in)),
        ("w_out", (e_in, d_model)),
        ("w_gu1", (d_model, 2 * f_in)),
        ("w_down1", (f_in, d_model)),
        ("w_qkv", (d_model, 3 * h_width)),
        ("w_o", (h_width, d_model)),
        ("w_gu2", (d_model, 2 * f_in)),
        ("w_down2", (f_in, d_model)),
    ]
    placed = []
    offset = 0
    for entry_name, entry_shape in entries:
        placed.append((entry_name, entry_shape, offset))
        offset = offset + math.prod(entry_shape)
    return (placed, offset)


def group_bounds(placed):
    bounds = []
    for entry_name, entry_shape, offset in placed:
        if entry_name == "gain":
            for row_index in range(entry_shape[0]):
                bounds.append(
                    (offset + row_index * entry_shape[1], offset + (row_index + 1) * entry_shape[1])
                )
        else:
            bounds.append((offset, offset + math.prod(entry_shape)))
    return bounds


def silu(values):
    return values * jax.nn.sigmoid(values)


def softplus(values):
    return jnp.maximum(values, 0.0) + jnp.log1p(jnp.exp(-jnp.abs(values)))


def mat_nn(left, right):
    return jnp.dot(left, right, preferred_element_type=jnp.float32)


def mat_tn(left, right):
    return lax.dot_general(
        left, right, (((0,), (0,)), ((), ())), preferred_element_type=jnp.float32
    )


def mat_nt(left, right):
    return lax.dot_general(
        left, right, (((1,), (1,)), ((), ())), preferred_element_type=jnp.float32
    )


def rope_tables(length, head_dim):
    half_dim = head_dim // 2
    freq_index = jnp.arange(half_dim, dtype=jnp.float32)
    inv_freq = jnp.exp(-math.log(ROPE_BASE) * 2.0 * freq_index / head_dim)
    angles = jnp.arange(length, dtype=jnp.float32)[:, None] * inv_freq[None, :]
    return (jnp.cos(angles)[:, None, :], jnp.sin(angles)[:, None, :])


def rope_apply(values, cosine, sine):
    half_dim = values.shape[-1] // 2
    first_half = values[..., :half_dim]
    second_half = values[..., half_dim:]
    return jnp.concatenate(
        [first_half * cosine - second_half * sine, second_half * cosine + first_half * sine],
        axis=-1,
    )


def rms_apply(resid, gain_row):
    return resid * lax.rsqrt(jnp.mean(resid * resid, axis=-1, keepdims=True) + EPS_NORM) * gain_row


def conv_act(mix_x, conv_w, conv_b):
    length = mix_x.shape[0]
    tap_count = conv_w.shape[0]
    padded = jnp.pad(mix_x, ((tap_count - 1, 0), (0, 0)))
    summed = conv_b[None, :] + conv_w[0][None, :] * padded[0:length]
    for tap_index in range(1, tap_count):
        summed = summed + conv_w[tap_index][None, :] * padded[tap_index : tap_index + length]
    return silu(summed)


def span_scan(step_blk, unit_blk, rate_blk, b_in, c_out):
    length, width = step_blk.shape
    n_state = rate_blk.shape[0]
    span_len = min(SPAN, length)
    spans = length // span_len
    decay = (step_blk[:, None, :] * rate_blk[None]).reshape(spans, span_len, n_state * width)
    inject = ((step_blk * unit_blk)[:, None, :] * b_in[:, :, None]).reshape(
        spans, span_len, n_state * width
    )
    lower = (jnp.arange(span_len)[:, None] >= jnp.arange(span_len)[None, :]).astype(jnp.float32)
    cumul = jnp.einsum("ts,ksm->ktm", lower, decay, precision=PRECISE)
    local = jnp.exp(cumul) * jnp.einsum(
        "ts,ksm->ktm", lower, jnp.exp(-cumul) * inject, precision=PRECISE
    )

    def carry_step(state, pair):
        end_decay, end_local = pair
        return (end_decay * state + end_local, state)

    initial = jnp.zeros((n_state * width,), jnp.float32)
    final_state, starts = lax.scan(carry_step, initial, (jnp.exp(cumul[:, -1]), local[:, -1]))
    states = (local + jnp.exp(cumul) * starts[:, None, :]).reshape(length, n_state, width)
    return jnp.einsum("sn,snc->sc", c_out, states, precision=PRECISE)


def mixer_spanned(gate_z, unit_vals, proj, w_dt, dt_bias, a_log, d_skip):
    dt_rank = w_dt.shape[0]
    n_state = a_log.shape[0]
    length, e_in = unit_vals.shape
    step_size = softplus(jnp.dot(proj[:, :dt_rank], w_dt, precision=PRECISE) + dt_bias[None, :])
    b_in = proj[:, dt_rank : dt_rank + n_state]
    c_out = proj[:, dt_rank + n_state :]
    rates = -jnp.exp(a_log)
    width = min(256, e_in)
    blocks = e_in // width

    def per_block(inputs):
        step_blk, unit_blk, rate_blk = inputs
        return span_scan(step_blk, unit_blk, rate_blk, b_in, c_out)

    scanned = lax.map(
        jax.checkpoint(per_block),
        (
            step_size.reshape(length, blocks, width).transpose(1, 0, 2),
            unit_vals.reshape(length, blocks, width).transpose(1, 0, 2),
            rates.reshape(n_state, blocks, width).transpose(1, 0, 2),
        ),
    )
    scanned = scanned.transpose(1, 0, 2).reshape(length, e_in)
    return (scanned + d_skip[None, :] * unit_vals) * silu(gate_z)


def block_scores(query_blk, keys):
    rows = query_blk.shape[0]
    length = keys.shape[0]
    scale = query_blk.shape[-1] ** (-0.5)
    distance = jnp.arange(rows)[:, None] - jnp.arange(length)[None, :]
    allowed = (distance >= 0) & (distance < WINDOW)
    scores = jnp.einsum("qhd,khd->hqk", query_blk, keys, preferred_element_type=jnp.float32) * scale
    return jnp.where(allowed[None], scores, NEG_FILL)


def attend_forward(query, keys, values):
    scores = block_scores(query, keys)
    top = jnp.max(scores, axis=-1, keepdims=True)
    expo = jnp.exp(scores - top)
    summed = jnp.sum(expo, axis=-1, keepdims=True)
    probs_low = (expo / summed).astype(jnp.bfloat16)
    outs = jnp.einsum("hqk,khd->qhd", probs_low, values, preferred_element_type=jnp.float32)
    log_totals = [top + jnp.log(summed)]
    return (outs, log_totals)


def attend_backward(query, keys, values, log_totals, grad_out):
    scale = query.shape[-1] ** (-0.5)
    probs = jnp.exp(block_scores(query, keys) - log_totals[0])
    grad_values = jnp.einsum(
        "hqk,qhd->khd", probs.astype(jnp.bfloat16), grad_out, preferred_element_type=jnp.float32
    )
    grad_probs = jnp.einsum("qhd,khd->hqk", grad_out, values, preferred_element_type=jnp.float32)
    inner = jnp.sum(probs * grad_probs, axis=-1, keepdims=True)
    grad_scores = (probs * (grad_probs - inner)).astype(jnp.bfloat16)
    grad_query = (
        jnp.einsum("hqk,khd->qhd", grad_scores, keys, preferred_element_type=jnp.float32) * scale
    )
    grad_keys = (
        jnp.einsum("hqk,qhd->khd", grad_scores, query, preferred_element_type=jnp.float32) * scale
    )
    return (grad_query, grad_keys, grad_values)


def branch_total(partial_out):
    return lax.psum(partial_out.astype(jnp.bfloat16), "tensor").astype(jnp.float32)


def grad_total(partial_grad):
    return lax.psum(partial_grad.astype(jnp.bfloat16), "tensor").astype(jnp.float32)


def ffn_forward(hidden_low, w_gu, w_down):
    f_in = w_down.shape[0]
    pre_act = mat_nn(hidden_low, w_gu)
    activ_low = (silu(pre_act[:, :f_in]) * pre_act[:, f_in:]).astype(jnp.bfloat16)
    return (branch_total(mat_nn(activ_low, w_down)), (pre_act, activ_low))


def ffn_backward(hidden_low, kept, w_gu, w_down, grad_low):
    pre_act, activ_low = kept
    f_in = w_down.shape[0]
    gate_part = pre_act[:, :f_in]
    up_part = pre_act[:, f_in:]
    grad_down = mat_tn(activ_low, grad_low)
    grad_act = mat_nt(grad_low, w_down)
    sigmoid_gate = jax.nn.sigmoid(gate_part)
    grad_gate = grad_act * up_part * sigmoid_gate * (1.0 + gate_part * (1.0 - sigmoid_gate))
    grad_up = grad_act * gate_part * sigmoid_gate
    grad_pre = jnp.concatenate([grad_gate, grad_up], axis=1).astype(jnp.bfloat16)
    grad_gu = mat_tn(hidden_low, grad_pre)
    return (grad_total(mat_nt(grad_pre, w_gu)), grad_gu, grad_down)


def unpack(flat, placed):
    blocks = {}
    for entry_name, entry_shape, offset in placed:
        blocks[entry_name] = flat[offset : offset + math.prod(entry_shape)].reshape(entry_shape)
    blocks["gains"] = lax.all_gather(blocks["gain"], "tensor", axis=1, tiled=True).astype(
        jnp.float32
    )
    return blocks


def layer_pass(resid_in, grad_out, weights, cosine, sine):
    e_in = weights["conv_b"].shape[0]
    length = resid_in.shape[0]
    heads_rank = weights["w_o"].shape[0] // HEAD_DIM
    gains = weights["gains"]
    small = {}
    for entry_name in ("conv_w", "conv_b", "dt_bias", "d_skip", "a_log", "w_dt"):
        small[entry_name] = weights[entry_name].astype(jnp.float32)
    normed, norm_back_one = jax.vjp(rms_apply, resid_in, gains[0])
    hidden_one = normed.astype(jnp.bfloat16)
    mixed = mat_nn(hidden_one, weights["w_in"])
    unit_vals, conv_back = jax.vjp(conv_act, mixed[:, :e_in], small["conv_w"], small["conv_b"])
    unit_low = unit_vals.astype(jnp.bfloat16)
    proj_sum = lax.psum(mat_nn(unit_low, weights["w_x"]).astype(jnp.bfloat16), "tensor")
    proj_low = lax.optimization_barrier(proj_sum)
    gated, scan_back = jax.vjp(
        mixer_spanned,
        mixed[:, e_in:],
        unit_low.astype(jnp.float32),
        proj_low.astype(jnp.float32),
        small["w_dt"],
        small["dt_bias"],
        small["a_log"],
        small["d_skip"],
    )
    gated_low = gated.astype(jnp.bfloat16)
    resid_one = resid_in + branch_total(mat_nn(gated_low, weights["w_out"]))
    normed, norm_back_two = jax.vjp(rms_apply, resid_one, gains[1])
    hidden_two = normed.astype(jnp.bfloat16)
    branch, kept_two = ffn_forward(hidden_two, weights["w_gu1"], weights["w_down1"])
    resid_two = resid_one + branch
    normed, norm_back_three = jax.vjp(rms_apply, resid_two, gains[2])
    hidden_three = normed.astype(jnp.bfloat16)
    packed = mat_nn(hidden_three, weights["w_qkv"]).reshape(length, 3, heads_rank, HEAD_DIM)
    query = rope_apply(packed[:, 0], cosine, sine).astype(jnp.bfloat16)
    keys = rope_apply(packed[:, 1], cosine, sine).astype(jnp.bfloat16)
    values = packed[:, 2].astype(jnp.bfloat16)
    attended, log_totals = attend_forward(query, keys, values)
    attended_low = attended.reshape(length, heads_rank * HEAD_DIM).astype(jnp.bfloat16)
    resid_three = resid_two + branch_total(mat_nn(attended_low, weights["w_o"]))
    normed, norm_back_four = jax.vjp(rms_apply, resid_three, gains[3])
    hidden_four = normed.astype(jnp.bfloat16)
    branch, kept_four = ffn_forward(hidden_four, weights["w_gu2"], weights["w_down2"])
    resid_four = resid_three + branch
    grads = {}
    grad_hidden, grads["w_gu2"], grads["w_down2"] = ffn_backward(
        hidden_four, kept_four, weights["w_gu2"], weights["w_down2"], grad_out.astype(jnp.bfloat16)
    )
    grad_prev, gain_four = norm_back_four(grad_hidden)
    grad_res = grad_out + grad_prev
    grad_low = grad_res.astype(jnp.bfloat16)
    grads["w_o"] = mat_tn(attended_low, grad_low)
    grad_att = (
        mat_nt(grad_low, weights["w_o"]).astype(jnp.bfloat16).reshape(length, heads_rank, HEAD_DIM)
    )
    grad_query, grad_keys, grad_values = attend_backward(query, keys, values, log_totals, grad_att)
    grad_packed = (
        jnp.stack(
            [
                rope_apply(grad_query, cosine, -sine),
                rope_apply(grad_keys, cosine, -sine),
                grad_values,
            ],
            axis=1,
        )
        .reshape(length, 3 * heads_rank * HEAD_DIM)
        .astype(jnp.bfloat16)
    )
    grads["w_qkv"] = mat_tn(hidden_three, grad_packed)
    grad_prev, gain_three = norm_back_three(grad_total(mat_nt(grad_packed, weights["w_qkv"])))
    grad_res = grad_res + grad_prev
    grad_hidden, grads["w_gu1"], grads["w_down1"] = ffn_backward(
        hidden_two, kept_two, weights["w_gu1"], weights["w_down1"], grad_res.astype(jnp.bfloat16)
    )
    grad_prev, gain_two = norm_back_two(grad_hidden)
    grad_res = grad_res + grad_prev
    grad_low = grad_res.astype(jnp.bfloat16)
    grads["w_out"] = mat_tn(gated_low, grad_low)
    (
        grad_gate_z,
        grad_unit_scan,
        grad_proj_rank,
        grads["w_dt"],
        grads["dt_bias"],
        grads["a_log"],
        grads["d_skip"],
    ) = scan_back(mat_nt(grad_low, weights["w_out"]))
    grad_proj = lax.psum(grad_proj_rank.astype(jnp.bfloat16), "tensor")
    grads["w_x"] = mat_tn(unit_low, grad_proj)
    grad_mix_x, grads["conv_w"], grads["conv_b"] = conv_back(
        grad_unit_scan + mat_nt(grad_proj, weights["w_x"])
    )
    grad_mixed = jnp.concatenate([grad_mix_x, grad_gate_z], axis=1).astype(jnp.bfloat16)
    grads["w_in"] = mat_tn(hidden_one, grad_mixed)
    grad_prev, gain_one = norm_back_one(grad_total(mat_nt(grad_mixed, weights["w_in"])))
    grad_res = grad_res + grad_prev
    grads["gain"] = jnp.stack([gain_one, gain_two, gain_three, gain_four])
    return (resid_four.astype(jnp.bfloat16), grad_res, grads)


def pack(grads, placed, flat_len, dp_count):
    pieces = [grads[entry_name].reshape(-1) for entry_name, entry_shape, offset in placed]
    used = sum((math.prod(entry_shape) for entry_name, entry_shape, offset in placed))
    pieces.append(jnp.zeros((flat_len - used,), jnp.float32))
    return jnp.concatenate(pieces).reshape(dp_count, flat_len // dp_count)


def per_device(tokens, cotangent, lengths, master, moment_one, moment_two):
    tensor_count = lax.axis_size("tensor")
    dp_count = lax.axis_size("dp")
    e_in = INNER // tensor_count
    f_in = FF // tensor_count
    heads_rank = HEADS // tensor_count
    d_gain = D // tensor_count
    placed, raw_count = layout(D, e_in, f_in, heads_rank * HEAD_DIM, NSTATE, CONV, DTR, d_gain)
    shard_len = master.shape[1]
    flat_len = shard_len * dp_count
    cosine, sine = rope_tables(SLOT, HEAD_DIM)
    own_copy = master[0].astype(jnp.bfloat16)
    gain_start = lax.axis_index("tensor") * d_gain
    weights_kept = unpack(lax.all_gather(own_copy, "dp", axis=0, tiled=True), placed)
    grads_summed = {}
    outputs_list = []
    grads_in_list = []
    for micro_index in range(MICRO):
        row_start = micro_index * SLOT
        slot_tokens = tokens[row_start : row_start + SLOT].astype(jnp.float32)
        valid = (jnp.arange(SLOT, dtype=jnp.int32) < lengths[micro_index]).astype(jnp.float32)
        slot_grad = cotangent[row_start : row_start + SLOT].astype(jnp.float32) * valid[:, None]
        slot_out, slot_in_grad, grads = layer_pass(
            slot_tokens, slot_grad, weights_kept, cosine, sine
        )
        grads["gain"] = lax.dynamic_slice_in_dim(grads["gain"], gain_start, d_gain, 1)
        outputs_list.append(slot_out)
        grads_in_list.append(slot_in_grad)
        if micro_index == 0:
            grads_summed = grads
        else:
            grads_summed = jax.tree.map(jnp.add, grads_summed, grads)
    received = lax.all_to_all(
        pack(grads_summed, placed, flat_len, dp_count).astype(jnp.bfloat16),
        "dp",
        split_axis=0,
        concat_axis=0,
        tiled=True,
    ).astype(jnp.float32)
    grad_shard = jnp.sum(received, axis=0)
    weights_old = master[0]
    first = BETA_ONE * moment_one[0] + (1.0 - BETA_ONE) * grad_shard
    second = BETA_TWO * moment_two[0] + (1.0 - BETA_TWO) * grad_shard * grad_shard
    trust_ratio = first / (jnp.sqrt(second) + ADAM_EPS) + DECAY_W * weights_old
    columns = lax.axis_index("dp") * shard_len + jnp.arange(shard_len, dtype=jnp.int32)
    bounds = group_bounds(placed)
    pieces = []
    for lower_end, upper_end in bounds:
        within_bounds = (columns >= lower_end) & (columns < upper_end)
        pieces.append(
            jnp.stack(
                [
                    jnp.sum(jnp.where(within_bounds, weights_old * weights_old, 0.0)),
                    jnp.sum(jnp.where(within_bounds, trust_ratio * trust_ratio, 0.0)),
                ]
            )
        )
    squares = lax.psum(jnp.stack(pieces), ("dp", "tensor"))
    trust_factor = jnp.sqrt(squares[:, 0] + TRUST_EPSILON) * lax.rsqrt(
        squares[:, 1] + TRUST_EPSILON
    )
    column_trust = jnp.zeros((shard_len,), jnp.float32)
    for group_index in range(len(bounds)):
        lower_end, upper_end = bounds[group_index]
        within_bounds = (columns >= lower_end) & (columns < upper_end)
        column_trust = jnp.where(within_bounds, trust_factor[group_index], column_trust)
    master_new = weights_old - LEARN_RATE * column_trust * trust_ratio
    return (
        jnp.concatenate(outputs_list, axis=0),
        jnp.concatenate(grads_in_list, axis=0),
        master_new[None, :],
        first[None, :],
        second[None, :],
        master_new.astype(jnp.bfloat16)[None, :],
        grad_shard[None, :],
        jnp.sqrt(squares),
    )


def solution(mesh):
    in_specs = (
        P("dp", None),
        P("dp", None),
        P("dp"),
        P("tensor", "dp"),
        P("tensor", "dp"),
        P("tensor", "dp"),
    )
    out_specs = (
        P("dp", None),
        P("dp", None),
        P("tensor", "dp"),
        P("tensor", "dp"),
        P("tensor", "dp"),
        P("tensor", "dp"),
        P("tensor", "dp"),
        P(),
    )
    return jax.shard_map(
        per_device, mesh=mesh, in_specs=in_specs, out_specs=out_specs, check_vma=False
    )
```

profile of v0, /device:TPU:2, one launch (start us, length us, event | category | flops | bytes accessed | tf_op | source)
XLA Modules:
  0.0 6914.6 jit_solution(3868949039324920960)
XLA Ops:
  7.2 141.3 %multiply_reduce_fusion.6 = (f32[2923648]{0:T(1024)}, f32[2923648]{0:T(1024)}, bf16[1,2923648]{1,0:T(2,128)(2,1)}) fusion(f32[1,2923648]{1,0:T(1,128)} %param.29), kind=kLoop, calls=%fused_computation.311 | loop fusion | flops 8770944 | bytes 40931072 | tf_op jit(solution)/shard_map/mul | solution.py:420
  152.7 1758.9 %all-gather.3.cloned.1.call-done = bf16[1,23389184]{1,0:T(2,128)(2,1)} async-done(((bf16[1,2923648]{1,0:T(2,128)(2,1)}), bf16[1,23389184]{1,0:T(2,128)(2,1)}) %all-gather.3.cloned.1.call-update) | async-done | bytes 46778384 | tf_op jit(solution)/shard_map/all_gather | solution.py:381
  1918.2 245.3 %slice_reduce_fusion = (bf16[4194304]{0:T(1024)(128)(2,1)}, bf16[4194304]{0:T(1024)(128)(2,1)}, bf16[4194304]{0:T(1024)(128)(2,1)}) fusion(bf16[1,23389184]{1,0:T(2,128)(2,1)} %all-gather.3.cloned.1.call-done), kind=kLoop, calls=%fused_computation.196 | loop fusion | bytes 50331648 | tf_op jit(solution)/shard_map/slice | solution.py:254
  2200.2 125.6 %slice_reduce_fusion.4 = (bf16[2097152]{0:T(1024)(128)(2,1)}, bf16[2097152]{0:T(1024)(128)(2,1)}, bf16[2097152]{0:T(1024)(128)(2,1)}) fusion(bf16[1,23389184]{1,0:T(2,128)(2,1)} %all-gather.3.cloned.1.call-done), kind=kLoop, calls=%fused_computation.312 | loop fusion | bytes 25165824 | tf_op jit(solution)/shard_map/slice | solution.py:254
  2345.9 144.0 %while.234 = (s32[]{:T(128)}, f32[4,128,256]{2,1,0:T(8,128)}, f32[4,128,256]{2,1,0:T(8,128)}, f32[4,16,256]{2,1,0:T(8,128)}, f32[4,128,256]{2,1,0:T(8,128)S(1)},...) while((s32[]{:T(128)}, f32[4,128,256]{2,1,0:T(8,128)}, ...), condition=%wide.region_20.21_spmd.clone.clone, body=%wide.region_17.20_spmd.clone.clone.sunk | while | flops 211334144 | bytes 46826292 | solution.py:170
  2495.5 105.7 %while.232 = (s32[]{:T(128)}, f32[4,128,256]{2,1,0:T(8,128)}, f32[4,128,256]{2,1,0:T(8,128)}, f32[4,16,256]{2,1,0:T(8,128)}, f32[4,128,256]{2,1,0:T(8,128)S(1)},...) while((s32[]{:T(128)}, f32[4,128,256]{2,1,0:T(8,128)}, ...), condition=%wide.region_5.6_spmd.clone.clone, body=%wide.region_2.5_spmd.clone.clone.sunk | while | flops 211334144 | bytes 46826292 | solution.py:170
  2608.1 109.2 %slice_reduce_fusion.3 = bf16[3145728]{0:T(1024)(128)(2,1)} fusion(bf16[1,23389184]{1,0:T(2,128)(2,1)} %all-gather.3.cloned.1.call-done), kind=kLoop, calls=%fused_computation.202 | loop fusion | bytes 12582912 | tf_op jit(solution)/shard_map/slice | solution.py:254
  3144.1 299.9 %while.237 = (s32[]{:T(128)}, f32[128,16]{1,0:T(8,128)}, f32[128,16]{0,1:T(8,128)}, f32[4,128,256]{2,1,0:T(8,128)}, f32[4,128,256]{2,1,0:T(8,128)}, /*index=5*/f...) while((s32[]{:T(128)}, f32[128,16]{1,0:T(8,128)}, ...), condition=%wide.region_47.48_spmd.clone, body=%wide.region_37.47_spmd.clone.sunk | while | flops 426867712 | bytes 157197360 | solution.py:170
  3454.9 261.7 %while.240 = (s32[]{:T(128)}, f32[128,16]{1,0:T(8,128)}, f32[128,16]{0,1:T(8,128)}, f32[4,128,256]{2,1,0:T(8,128)}, f32[4,128,256]{2,1,0:T(8,128)}, /*index=5*/f...) while((s32[]{:T(128)}, f32[128,16]{1,0:T(8,128)}, ...), condition=%wide.region_68.69_spmd.clone, body=%wide.region_58.68_spmd.clone.sunk | while | flops 426867712 | bytes 157164576 | solution.py:170
  3877.1 582.6 %while.241 = (u32[]{:T(128)}, bf16[23389184]{0:T(1024)(128)(2,1)}, bf16[8,1,2923648]{2,1,0:T(2,128)(2,1)}, u32[]{}, u32[]{}) while((u32[]{:T(128)}, bf16[23389184]{0:T(1024)(128)(2,1)}, bf16[8,1,2923648]{2,1,0:T(2,128)(2,1)}, u32[]{}, u32[]{}) %tuple.621), condition=%wide.cond, body=%wide.body.sunk | while | flops 9 | bytes 29236636
  3882.3 67.6 reshape_dynamic-update-slice_fusion.2
  3955.1 67.6 reshape_dynamic-update-slice_fusion.2
  4100.8 67.6 reshape_dynamic-update-slice_fusion.2
  4173.6 67.6 reshape_dynamic-update-slice_fusion.2
  4319.2 67.6 reshape_dynamic-update-slice_fusion.2
  4392.1 67.6 reshape_dynamic-update-slice_fusion.2
  4460.2 275.6 %reduce.50 = bf16[8,2923648]{1,0:T(8,128)(2,1)} reduce(bf16[8,1,2923648]{2,1,0:T(2,128)(2,1)} %get-tuple-element.1544, bf16[]{:T(256)} %broadcast.1659), dimensions={1}, to_apply=%get-tuple-element.1544.reduce_sub_computation | reduce | bytes 93556736 | tf_op jit(solution)/shard_map/convert_element_type | solution.py:401
  4735.8 240.5 %reshape.1274 = bf16[8,2,1461824]{2,1,0:T(2,128)(2,1)} reshape(bf16[8,2923648]{1,0:T(8,128)(2,1)} %reduce.50) | data formatting | bytes 93556736
  4985.3 115.0 %reduce.30 = f32[2923648]{0:T(1024)} reduce(f32[1,2923648]{1,0:T(1,128)} %param.30, f32[]{:T(128)} %constant.443), dimensions={0}, to_apply=%param.30.reduce_sub_computation | reduce | bytes 23389188 | tf_op args[4]
  5100.3 126.0 %multiply_reduce_fusion.8 = f32[2923648]{0:T(1024)} fusion(f32[1,2923648]{1,0:T(1,128)} %param.31), kind=kLoop, calls=%fused_computation.319 | loop fusion | flops 2923648 | bytes 23389184 | tf_op jit(solution)/shard_map/mul | solution.py:410
  5270.2 720.5 %all-to-all-done = bf16[8,2,1461824]{2,1,0:T(2,128)(2,1)} async-done(((bf16[8,2,1461824]{2,1,0:T(2,128)(2,1)}), bf16[8,2,1461824]{2,1,0:T(2,128)(2,1)}, u32[]{:S(2)}, u32[]{:S(2)}) %all-to-all-start) | async-done | bytes 46778400 | tf_op jit(solution)/shard_map/all_to_all | solution.py:400
  5990.6 147.3 %reshape.1275 = bf16[8,1,2923648]{2,1,0:T(2,128)(2,1)} reshape(bf16[8,2,1461824]{2,1,0:T(2,128)(2,1)} %all-to-all-done) | data formatting | bytes 93556736
  6137.9 248.8 %convert_reduce_fusion = f32[2923648]{0:T(1024)} fusion(bf16[8,1,2923648]{2,1,0:T(2,128)(2,1)} %reshape.1275), kind=kLoop, calls=%fused_computation.174 | loop fusion | flops 43854720 | bytes 58472960 | tf_op jit(solution)/shard_map/reduce_sum | solution.py:407
  6545.4 362.1 %fusion.331 = (bf16[1,2923648]{1,0:T(2,128)(2,1)}, f32[1,2923648]{1,0:T(1,128)}, f32[1,2923648]{1,0:T(1,128)}, f32[1,2923648]{1,0:T(1,128)}) fusion(f32[1,2923648]{1,0:T(1,128)} %param.29, f32[]{:T(128)} %bitcast.155, f32[]{:T(128)} %bitcast.154, f32[]{:T(128)} %bitcast.153, f32[]{:T(128)} %bitcast.152, f32[]{:T(128)} %bitcast.151, f32[]{:T(128)} %bitcast.150, ...), kind=kLoop, calls=%fused_computation.801 | loop fusion | flops 266051968 | bytes 87709520 | tf_op jit(solution)/shard_map/convert_element_type | solution.py:441
  (2304 shorter events, 1973.7 us)
Async XLA Ops:
  7.2 1904.4 %all-gather.3.cloned.1.call-start = ((), (), s32[]{:S(2)}) async-start(), calls=%async_computation.1 | async-start | bytes 105251328 | tf_op jit(solution)/shard_map/all_gather | solution.py:381
  148.5 2186.7 %all-reduce.49.cloned.1.call-start = ((), (), s32[]{:S(2)}) async-start(), calls=%async_computation.3 | async-start | bytes 163840 | tf_op jit(solution)/shard_map/psum | solution.py:274
  151.9 1760.5 %copy-start.212 = (f32[128]{0:T(128)}, f32[128]{0:T(128)S(1)}, u32[]{:S(2)}) copy-start(f32[128]{0:T(128)S(1)} %get-tuple-element.1620) | copy-start | bytes 1540
  151.9 2024.8 %copy-start.195 = (f32[128]{0:T(128)}, f32[128]{0:T(128)S(1)}, u32[]{:S(2)}) copy-start(f32[128]{0:T(128)S(1)} %fusion.298) | copy-start | bytes 1540
  151.9 2029.7 %copy-start.174 = (f32[128]{0:T(128)}, f32[128]{0:T(128)S(1)}, u32[]{:S(2)}) copy-start(f32[128]{0:T(128)S(1)} %fusion.294) | copy-start | bytes 1540
  1918.2 263.5 %copy-start.118 = (f32[1,2048]{1,0:T(1,128)}, f32[1,2048]{1,0:T(1,128)S(1)}, u32[]{:S(2)}) copy-start(f32[1,2048]{1,0:T(1,128)S(1)} %get-tuple-element.1945) | copy-start | bytes 24580
  2183.9 141.9 %copy-start.111 = (f32[128,1024]{1,0:T(8,128)}, f32[128,1024]{1,0:T(8,128)S(1)}, u32[]{:S(2)}) copy-start(f32[128,1024]{1,0:T(8,128)S(1)} %slice.571) | copy-start | bytes 1572868
  2184.9 141.0 %copy-start.187 = (f32[1,1024]{1,0:T(1,128)}, f32[1,1024]{1,0:T(1,128)S(1)}, u32[]{:S(2)}) copy-start(f32[1,1024]{1,0:T(1,128)S(1)} %get-tuple-element.1946) | copy-start | bytes 12292
  2184.9 141.0 %copy-start.189 = (f32[1,1024]{1,0:T(1,128)}, f32[1,1024]{1,0:T(1,128)S(1)}, u32[]{:S(2)}) copy-start(f32[1,1024]{1,0:T(1,128)S(1)} %get-tuple-element.1947) | copy-start | bytes 12292
  2184.9 141.0 %copy-start.191 = (f32[1,1024]{1,0:T(1,128)}, f32[1,1024]{1,0:T(1,128)S(1)}, u32[]{:S(2)}) copy-start(f32[1,1024]{1,0:T(1,128)S(1)} %get-tuple-element.1948) | copy-start | bytes 12292
  2184.9 141.0 %copy-start.193 = (f32[1,1024]{1,0:T(1,128)}, f32[1,1024]{1,0:T(1,128)S(1)}, u32[]{:S(2)}) copy-start(f32[1,1024]{1,0:T(1,128)S(1)} %get-tuple-element.1949) | copy-start | bytes 12292
  2192.0 133.9 %copy-start.62 = (bf16[1024,160]{1,0:T(8,128)(2,1)}, bf16[1024,160]{1,0:T(8,128)(2,1)S(1)}, u32[]{:S(2)}) copy-start(bf16[1024,160]{1,0:T(8,128)(2,1)S(1)} %reshape.1127) | copy-start | bytes 983044
  2197.6 561.3 %all-reduce.63.cloned.1.call-start = ((), (), s32[]{:S(2)}) async-start(), calls=%async_computation.10 | async-start | bytes 2097152 | tf_op jit(solution)/shard_map/psum | solution.py:222
  2608.0 205.3 %all-reduce.61.cloned.1.call-start = ((), (), s32[]{:S(2)}) async-start(), calls=%async_computation.9 | async-start | bytes 2097152 | tf_op jit(solution)/shard_map/psum | solution.py:222
  2772.9 93.6 %all-reduce.59.cloned.1.call-start = ((), (), s32[]{:S(2)}) async-start(), calls=%async_computation.8 | async-start | bytes 2097152 | tf_op jit(solution)/shard_map/psum | solution.py:222
  2828.9 122.5 %all-reduce.57.cloned.1.call-start = ((), (), s32[]{:S(2)}) async-start(), calls=%async_computation.7 | async-start | bytes 2097152 | tf_op jit(solution)/shard_map/psum | solution.py:226
  2914.5 139.6 %all-reduce.55.cloned.1.call-start = ((), (), s32[]{:S(2)}) async-start(), calls=%async_computation.6 | async-start | bytes 2097152 | tf_op jit(solution)/shard_map/psum | solution.py:226
  3017.1 113.0 %all-reduce.53.cloned.1.call-start = ((), (), s32[]{:S(2)}) async-start(), calls=%async_computation.5 | async-start | bytes 2097152 | tf_op jit(solution)/shard_map/psum | solution.py:226
  3093.1 672.8 %all-reduce.47.cloned.1.call-start = ((), (), s32[]{:S(2)}) async-start(), calls=%async_computation.2 | async-start | bytes 163840 | tf_op jit(solution)/shard_map/psum | solution.py:348
  3735.0 103.4 %all-reduce.51.cloned.1.call-start = ((), (), s32[]{:S(2)}) async-start(), calls=%async_computation.4 | async-start | bytes 4194304 | tf_op jit(solution)/shard_map/psum | solution.py:222
  4976.4 1014.3 %all-to-all-start = ((bf16[8,2,1461824]{2,1,0:T(2,128)(2,1)}), bf16[8,2,1461824]{2,1,0:T(2,128)(2,1)}, u32[]{:S(2)}, u32[]{:S(2)}) async-start(bf16[8,2,1461824]{2,1,0:T(2,128)(2,1)} %reshape.1274), calls=%async_computation | async-start | bytes 93560832 | tf_op jit(solution)/shard_map/all_to_all | solution.py:400
  6498.8 46.6 slice-start.8
  6499.4 46.0 slice-start.9
  6499.4 46.0 slice-start.10
  (323 other events, 2183.3 us)
Sparse Core Ops, SparseCore 0:
  148.6 1762.8 all-gather.2
  2197.7 31.3 all-reduce.48
  2608.2 37.4 all-reduce.62
  2773.0 37.4 all-reduce.60
  2829.0 37.3 all-reduce.58
  2914.6 36.7 all-reduce.56
  3017.2 36.8 all-reduce.54
  3093.2 36.7 all-reduce.52
  3735.1 30.7 all-reduce.46
  3785.6 52.8 all-reduce.50
where the time goes:
time: 6930 us; the launch traced here: 6910 us
  waiting for transfers between devices  2600 us (38%)
  local copies, waits for them, and re-layouts  2120 us (31%)
  other arithmetic  1670 us (24%)
  matrix products  400 us (6%)
    all_gather x1, waiting for transfers between devices, per_device(): lax.all_gather(own_copy, 'dp', axis=0, tiled=True)  1760 us
    unnamed x471, local copies, waits for them, and re-layouts  1070 us
    all_to_all x1, waiting for transfers between devices, per_device(): lax.all_to_all(pack(grads_summed, placed, flat_len, dp_count).astype(jnp....  720 us
    slice x9, local copies, waits for them, and re-layouts, unpack(): flat[offset:offset + math.prod(entry_shape)].reshape(entry_shape)  528 us
    convert_element_type x1, other arithmetic, per_device(): master_new.astype(jnp.bfloat16)[None, :]  362 us
    convert_element_type x1, other arithmetic, per_device(): pack(grads_summed, placed, flat_len, dp_count).astype(jnp.bfloat16)  276 us
    reduce_sum x1, other arithmetic, per_device(): grad_shard = jnp.sum(received, axis=0)  249 us
    mul x1, other arithmetic, per_device(): weights_old * weights_old  141 us
  transfers between devices with their start and end apart: 11, of which 8 were waited for; matrix products, arithmetic and copies ran while one was open for 11% of the time, Pallas kernels for 0%

commit v1 on v0

v1 whole, which is shorter than its diff:
```python
import functools
import math

import jax
import jax.numpy as jnp
from jax import lax
from jax.experimental import pallas as pl
from jax.experimental.pallas import tpu as pltpu
from jax.sharding import PartitionSpec as P

D = 2048
INNER = 4096
NSTATE = 16
DTR = 128
HEADS = 32
HEAD_DIM = 64
FF = 4096
CONV = 4
WINDOW = 2048
SLOT = 128
LANES = 128

EPS_NORM = 1e-05
TRUST_EPSILON = 1e-06
ROPE_BASE = 10000.0
BETA_ONE = 0.5
BETA_TWO = 0.55
ADAM_EPS = 1e-06
DECAY_W = 0.01
LEARN_RATE = 0.2
NEG_FILL = -1e30
LOG2E = 1.4426950408889634
MESH = pl.DeviceIdType.MESH
BF = jnp.bfloat16
F32 = jnp.float32

EI = INNER // 4
FI = FF // 4
HW = HEADS * HEAD_DIM // 4
DG = D // 4

SMALL = [
    ("conv_w", (CONV, EI)),
    ("conv_b", (EI,)),
    ("dt_bias", (EI,)),
    ("d_skip", (EI,)),
    ("a_log", (NSTATE, EI)),
    ("w_x", (EI, DTR + 2 * NSTATE)),
    ("w_dt", (DTR, EI)),
]
SMALL_ROWS = sum(math.prod(s) for _, s in SMALL) // LANES
GAIN_ROWS = 4 * DG // LANES
BIG = [
    ("w_in", D),
    ("w_out", EI),
    ("w_gu1", D),
    ("w_down1", FI),
    ("w_qkv", D * 3 * HW // D),
    ("w_o", HW),
    ("w_gu2", D),
    ("w_down2", FI),
]
BIG_OFF = {}
_at = 0
for _name, _rows in BIG:
    BIG_OFF[_name] = _at
    _at += _rows
BIG_ROWS = _at
LINES = D // LANES
FIRST = BIG_OFF["w_out"] * LINES
LEAD = GAIN_ROWS


def group_bounds():
    bounds = []
    for k in range(4):
        bounds.append((k * DG, (k + 1) * DG))
    at = 4 * DG
    entries = [("w_in", D * 2 * EI)]
    entries += [(name, math.prod(shape)) for name, shape in SMALL]
    entries += [
        ("w_out", EI * D),
        ("w_gu1", D * 2 * FI),
        ("w_down1", FI * D),
        ("w_qkv", D * 3 * HW),
        ("w_o", HW * D),
        ("w_gu2", D * 2 * FI),
        ("w_down2", FI * D),
    ]
    for _, count in entries:
        bounds.append((at, at + count))
        at += count
    return bounds


def silu(v):
    return v * jax.nn.sigmoid(v)


def softplus(v):
    return jnp.maximum(v, 0.0) + jnp.log1p(jnp.exp(-jnp.abs(v)))


def mat_nn(a, b):
    return jnp.dot(a, b, preferred_element_type=F32)


def mat_tn(a, b):
    return lax.dot_general(a, b, (((0,), (0,)), ((), ())), preferred_element_type=F32)


def mat_nt(a, b):
    return lax.dot_general(a, b, (((1,), (1,)), ((), ())), preferred_element_type=F32)


def ring_pos(d, n):
    return jnp.where(lax.rem(d, 2) == 0, lax.div(d, 2), n - 1 - lax.div(d, 2))


def ring_dev(p, n):
    return jnp.where(p < n // 2, 2 * p, 2 * (n - 1 - p) + 1)


def ring_neighbours(n):
    d = lax.axis_index("dp")
    p = ring_pos(d, n)
    right = ring_dev(lax.rem(p + 1, n), n)
    left = ring_dev(lax.rem(p + n - 1, n), n)
    return d, p, right, left


def ring_barrier(left, right, t):
    barrier = pltpu.get_barrier_semaphore()
    for nb in (left, right):
        pl.semaphore_signal(barrier, inc=1, device_id=(nb, t), device_id_type=MESH)
    pl.semaphore_wait(barrier, 2)


def gather_kernel(n, subs, own_ref, out_ref, hold, local_sem, ssem, rsem):
    t = lax.axis_index("tensor")
    d, p, right, left = ring_neighbours(n)
    rows = own_ref.shape[0]
    half = rows // 2
    sub = half // subs
    fetch = pltpu.make_async_copy(own_ref, hold, local_sem.at[0])
    fetch.start()
    ring_barrier(left, right, t)

    def copy(way, step, c, from_own):
        target = right if way == 0 else left
        owner = ring_dev(lax.rem(p + (n - step if way == 0 else step), n), n)
        at = pl.multiple_of(owner * rows + way * half + c * sub, 8)
        src = own_ref.at[pl.ds(way * half + c * sub, sub)] if from_own else out_ref.at[pl.ds(at, sub)]
        return pltpu.make_async_remote_copy(
            src_ref=src,
            dst_ref=out_ref.at[pl.ds(at, sub)],
            send_sem=ssem.at[way, step, c],
            recv_sem=rsem.at[way, step, c],
            device_id=(target, t),
            device_id_type=MESH,
        )

    for c in range(subs):
        for way in (0, 1):
            copy(way, 0, c, True).start()
    fetch.wait()
    store = pltpu.make_async_copy(
        hold, out_ref.at[pl.ds(pl.multiple_of(d * rows, 8), rows)], local_sem.at[1]
    )
    store.start()
    for step in range(1, n - 1):
        for c in range(subs):
            for way in (0, 1):
                copy(way, step - 1, c, step == 1).wait_recv()
                copy(way, step, c, False).start()
    for c in range(subs):
        for way in (0, 1):
            copy(way, n - 2, c, n == 2).wait_recv()
    store.wait()
    for step in range(n - 1):
        for c in range(subs):
            for way in (0, 1):
                copy(way, step, c, step == 0).wait_send()


def ring_gather(own, n):
    rows, cols = own.shape
    subs = 2
    return pl.pallas_call(
        functools.partial(gather_kernel, n, subs),
        out_shape=jax.ShapeDtypeStruct((n * rows, cols), own.dtype),
        in_specs=[pl.BlockSpec(memory_space=pl.ANY)],
        out_specs=pl.BlockSpec(memory_space=pl.ANY),
        scratch_shapes=[
            pltpu.VMEM((rows, cols), own.dtype),
            pltpu.SemaphoreType.DMA((2,)),
            pltpu.SemaphoreType.DMA((2, n - 1, subs)),
            pltpu.SemaphoreType.DMA((2, n - 1, subs)),
        ],
        compiler_params=pltpu.CompilerParams(
            collective_id=0, has_side_effects=True, vmem_limit_bytes=32 << 20
        ),
        name="ring_gather",
    )(own)


def piece_of(half):
    for size in (64, 32, 16):
        if half % size == 0:
            return size


def reduce_kernel(n, left_ref, right_refs, qkv_ref, out_ref, slots, ssem, rsem, out_sem):
    t = lax.axis_index("tensor")
    d, p, right, left = ring_neighbours(n)
    rows = out_ref.shape[0]
    half = rows // 2
    SUB = piece_of(half)
    subs = half // SUB
    ring_barrier(left, right, t)
    qkv_at = BIG_OFF["w_qkv"]
    qkv_rows = dict(BIG)["w_qkv"]

    def own_into(at, put):
        in_qkv = jnp.logical_and(at >= qkv_at, at < qkv_at + qkv_rows)
        which = jnp.int32(0)
        for name, _ in BIG[1:]:
            if name != "w_qkv":
                which = which + jnp.where(at >= BIG_OFF[name], 1, 0)

        @pl.when(in_qkv)
        def _():
            put(qkv_ref[pl.ds(pl.multiple_of(at - qkv_at, SUB), SUB), :].astype(F32))

        @pl.when(jnp.logical_not(in_qkv))
        def _():
            row = jnp.where(at >= qkv_at + qkv_rows, at - qkv_rows, at)
            lt = left_ref[pl.ds(pl.multiple_of(row, SUB), SUB), :]
            put(jnp.dot(lt, right_refs[which], preferred_element_type=F32))

    def owner_of(way, step):
        return ring_dev(lax.rem(p + (n - 1 - step if way == 0 else 1 + step), n), n)

    def copy(way, step, c):
        target = right if way == 0 else left
        return pltpu.make_async_remote_copy(
            src_ref=slots.at[way, step, pl.ds(pl.multiple_of(c * SUB, SUB), SUB)],
            dst_ref=slots.at[way, step + 1, pl.ds(pl.multiple_of(c * SUB, SUB), SUB)],
            send_sem=ssem.at[way, step, c],
            recv_sem=rsem.at[way, step, c],
            device_id=(target, t),
            device_id_type=MESH,
        )

    def run(step):
        @pl.loop(0, subs)
        def _(c):
            here = pl.ds(pl.multiple_of(c * SUB, SUB), SUB)
            for way in (0, 1):
                at = owner_of(way, step) * rows + way * half + c * SUB
                if step > 0:
                    copy(way, step - 1, c).wait_recv()

                def put(value):
                    if step > 0:
                        value = value + slots[way, step, here, :].astype(F32)
                    slots[way, step, here, :] = value.astype(BF)

                own_into(at, put)
                if step < n - 1:
                    copy(way, step, c).start()
                else:
                    pltpu.make_async_copy(
                        slots.at[way, step, here],
                        out_ref.at[pl.ds(pl.multiple_of(way * half + c * SUB, SUB), SUB)],
                        out_sem.at[way, c],
                    ).start()

    for step in range(n):
        run(step)

    @pl.loop(0, subs)
    def _(c):
        here = pl.ds(pl.multiple_of(c * SUB, SUB), SUB)
        for way in (0, 1):
            for step in range(n - 1):
                copy(way, step, c).wait_send()
            pltpu.make_async_copy(
                slots.at[way, n - 1, here],
                out_ref.at[pl.ds(pl.multiple_of(way * half + c * SUB, SUB), SUB)],
                out_sem.at[way, c],
            ).wait()


def ring_reduce(left_t, rights, qkv_grad, n):
    rows = BIG_ROWS // n
    subs = rows // 2 // piece_of(rows // 2)
    vm = pl.BlockSpec(memory_space=pltpu.VMEM)
    return pl.pallas_call(
        functools.partial(reduce_kernel, n),
        out_shape=jax.ShapeDtypeStruct((rows, D), BF),
        in_specs=[vm, vm, vm],
        out_specs=pl.BlockSpec(memory_space=pl.ANY),
        scratch_shapes=[
            pltpu.VMEM((2, n, rows // 2, D), BF),
            pltpu.SemaphoreType.DMA((2, n - 1, subs)),
            pltpu.SemaphoreType.DMA((2, n - 1, subs)),
            pltpu.SemaphoreType.DMA((2, subs)),
        ],
        compiler_params=pltpu.CompilerParams(
            collective_id=1, has_side_effects=True, vmem_limit_bytes=67043328
        ),
        name="ring_reduce",
    )(left_t, rights, qkv_grad)


def spread(ref, value):
    rows = value.shape[0]
    for j in range(EI // LANES):
        ref[pl.ds(j, rows, stride=EI // LANES), :] = value[:, j * LANES : (j + 1) * LANES]


def collect(ref, rows):
    return jnp.concatenate(
        [ref[pl.ds(j, rows, stride=EI // LANES), :] for j in range(EI // LANES)], axis=1
    )


SUBL = EI // LANES


def scan_kernel(slots, proj_ref, bc_ref, unit_ref, gate_ref, w_dt_ref, bias_ref, skip_ref, alog_ref,
                gated_ref, step_s, su_s, y_s, rate_s):
    pre = jnp.dot(proj_ref[:, :DTR], w_dt_ref[...], preferred_element_type=F32) + bias_ref[...]
    step = softplus(pre)
    unit = unit_ref[...].astype(F32)
    spread(step_s, step)
    spread(su_s, step * unit)
    rate_s[...] = -jnp.exp(alog_ref[...]) * LOG2E

    def body(t, states):
        new = []
        for m in range(slots):
            r = m * SLOT + t
            row = pl.ds(pl.multiple_of(r * SUBL, SUBL), SUBL)
            st = step_s[row, :]
            su = su_s[row, :]
            y = jnp.zeros((SUBL, LANES), F32)
            for k in range(NSTATE):
                dec = jnp.exp2(rate_s[k * SUBL : (k + 1) * SUBL, :] * st)
                s = dec * states[m * NSTATE + k] + bc_ref[r, k] * su
                y = y + bc_ref[r, NSTATE + k] * s
                new.append(s)
            y_s[row, :] = y
        return tuple(new)

    init = tuple(jnp.zeros((SUBL, LANES), F32) for _ in range(slots * NSTATE))
    lax.fori_loop(0, SLOT, body, init)
    y = collect(y_s, slots * SLOT) + skip_ref[...] * unit
    z = gate_ref[...]
    gated_ref[...] = (y * silu(z)).astype(BF)


def scan_forward(proj, bc, unit, gate, w_dt, dt_bias, d_skip, a_log):
    rows = unit.shape[0]
    vm = pl.BlockSpec(memory_space=pltpu.VMEM)
    sm = pl.BlockSpec(memory_space=pltpu.SMEM)
    return pl.pallas_call(
        functools.partial(scan_kernel, rows // SLOT),
        out_shape=jax.ShapeDtypeStruct((rows, EI), BF),
        in_specs=[vm, sm, vm, vm, vm, vm, vm, vm],
        out_specs=vm,
        scratch_shapes=[
            pltpu.VMEM((rows * SUBL, LANES), F32),
            pltpu.VMEM((rows * SUBL, LANES), F32),
            pltpu.VMEM((rows * SUBL, LANES), F32),
            pltpu.VMEM((NSTATE * SUBL, LANES), F32),
        ],
        compiler_params=pltpu.CompilerParams(vmem_limit_bytes=60 << 20),
        name="scan_forward",
    )(proj, bc, unit, gate, w_dt, dt_bias, d_skip, a_log)


def adjoint_kernel(slots, proj_ref, bc_ref, unit_ref, gate_ref, w_dt_ref, bias_ref, skip_ref, alog_ref,
                   grad_ref, gz_ref, gunit_ref, gproj_ref, gdt_ref, gbias_ref, gskip_ref, galog_ref,
                   step_s, su_s, unit_s, y_s, gy_s, gs_s, lb_s, rate_s, hist, lams):
    rows = slots * SLOT
    pre = jnp.dot(proj_ref[:, :DTR], w_dt_ref[...], preferred_element_type=F32) + bias_ref[...]
    step = softplus(pre)
    unit = unit_ref[...].astype(F32)
    spread(step_s, step)
    spread(unit_s, unit)
    spread(su_s, step * unit)
    z = gate_ref[...]
    sig = jax.nn.sigmoid(z)
    gg = grad_ref[...]
    gy = gg * z * sig
    spread(gy_s, gy)
    rate_s[...] = -jnp.exp(alog_ref[...])
    galog_ref[...] = jnp.zeros_like(galog_ref)
    zero = jnp.zeros((SUBL, LANES), F32)
    span = SLOT + 1

    def hist_at(k, t):
        return pl.ds(pl.multiple_of((k * span + t) * SUBL, SUBL), SUBL)

    def lam_at(k, t):
        return pl.ds(pl.multiple_of((k * SLOT + t) * SUBL, SUBL), SUBL)

    for m in range(slots):
        for k in range(NSTATE):
            hist[hist_at(k, 0), :] = zero

        def forward(t, states):
            r = m * SLOT + t
            row = pl.ds(pl.multiple_of(r * SUBL, SUBL), SUBL)
            st = step_s[row, :] * LOG2E
            su = su_s[row, :]
            y = zero
            new = []
            for k in range(NSTATE):
                dec = jnp.exp2(rate_s[k * SUBL : (k + 1) * SUBL, :] * st)
                s = dec * states[k] + bc_ref[r, k] * su
                y = y + bc_ref[r, NSTATE + k] * s
                hist[hist_at(k, t + 1), :] = s
                new.append(s)
            y_s[row, :] = y
            return tuple(new)

        lax.fori_loop(0, SLOT, forward, tuple(zero for _ in range(NSTATE)))

        def backward(i, carry):
            t = SLOT - 1 - i
            r = m * SLOT + t
            row = pl.ds(pl.multiple_of(r * SUBL, SUBL), SUBL)
            st = step_s[row, :]
            st2 = st * LOG2E
            gyt = gy_s[row, :]
            lb = zero
            gs = zero
            new = []
            for k in range(NSTATE):
                rate = rate_s[k * SUBL : (k + 1) * SUBL, :]
                dec = jnp.exp2(rate * st2)
                lam = bc_ref[r, NSTATE + k] * gyt + carry[k]
                ld = dec * lam
                new.append(ld)
                lams[lam_at(k, t), :] = lam
                lb = lb + bc_ref[r, k] * lam
                x = ld * hist[hist_at(k, t), :]
                gs = gs + rate * x
                at = slice(k * SUBL, (k + 1) * SUBL)
                galog_ref[at, :] = galog_ref[at, :] + st * x
            lb_s[row, :] = lb
            gs_s[row, :] = gs + unit_s[row, :] * lb
            return tuple(new)

        lax.fori_loop(0, SLOT, backward, tuple(zero for _ in range(NSTATE)))
        out = slice(m * SLOT, (m + 1) * SLOT)
        base = m * SLOT * SUBL

        lane = lax.broadcasted_iota(jnp.int32, (SLOT, LANES), 1)

        def reduce_state(k, acc):
            ab = jnp.zeros((SLOT, LANES), F32)
            ac = jnp.zeros((SLOT, LANES), F32)
            for j in range(SUBL):
                cols = slice(j * LANES, (j + 1) * LANES)
                lam = lams[pl.ds(k * SLOT * SUBL + j, SLOT, stride=SUBL), :]
                h = hist[pl.ds((k * span + 1) * SUBL + j, SLOT, stride=SUBL), :]
                sj = su_s[pl.ds(base + j, SLOT, stride=SUBL), :]
                gj = gy_s[pl.ds(base + j, SLOT, stride=SUBL), :]
                ab = ab + lam * sj
                ac = ac + h * gj
            sb = jnp.sum(ab, axis=1, keepdims=True)
            sc = jnp.sum(ac, axis=1, keepdims=True)
            return acc + jnp.where(lane == k, sb, 0.0) + jnp.where(lane == NSTATE + k, sc, 0.0)

        sums = lax.fori_loop(0, NSTATE, reduce_state, jnp.zeros((SLOT, LANES), F32))
        gproj_ref[out, DTR : DTR + LANES] = sums.astype(BF)
    galog_ref[...] = galog_ref[...] * rate_s[...]
    y = collect(y_s, rows) + skip_ref[...] * unit
    gz_ref[...] = (gg * y * sig * (1.0 + z * (1.0 - sig))).astype(BF)
    gunit_ref[...] = gy * skip_ref[...] + step * collect(lb_s, rows)
    gskip_ref[...] = jnp.sum(gy * unit, axis=0, keepdims=True)
    q = collect(gs_s, rows) * jax.nn.sigmoid(pre)
    gbias_ref[...] = jnp.sum(q, axis=0, keepdims=True)
    ql = q.astype(BF)
    gdt_ref[...] = mat_tn(proj_ref[:, :DTR], ql)
    gproj_ref[:, :DTR] = mat_nt(ql, w_dt_ref[...]).astype(BF)


def scan_backward(proj, bc, unit, gate, w_dt, dt_bias, d_skip, a_log, grad):
    rows = unit.shape[0]
    vm = pl.BlockSpec(memory_space=pltpu.VMEM)
    sm = pl.BlockSpec(memory_space=pltpu.SMEM)
    sds = jax.ShapeDtypeStruct
    flat = pltpu.VMEM((rows * SUBL, LANES), F32)
    return pl.pallas_call(
        functools.partial(adjoint_kernel, rows // SLOT),
        out_shape=(
            sds((rows, EI), BF),
            sds((rows, EI), F32),
            sds((rows, DTR + LANES), BF),
            sds((DTR, EI), F32),
            sds((1, EI), F32),
            sds((1, EI), F32),
            sds((NSTATE * SUBL, LANES), F32),
        ),
        in_specs=[vm, sm, vm, vm, vm, vm, vm, vm, vm],
        out_specs=(vm,) * 7,
        scratch_shapes=[flat] * 7
        + [
            pltpu.VMEM((NSTATE * SUBL, LANES), F32),
            pltpu.VMEM((NSTATE * (SLOT + 1) * SUBL, LANES), F32),
            pltpu.VMEM((NSTATE * SLOT * SUBL, LANES), F32),
        ],
        compiler_params=pltpu.CompilerParams(vmem_limit_bytes=60 << 20),
        name="scan_backward",
    )(proj, bc, unit, gate, w_dt, dt_bias, d_skip, a_log, grad)


def rope_tables(length, head_dim):
    half_dim = head_dim // 2
    freq_index = jnp.arange(half_dim, dtype=F32)
    inv_freq = jnp.exp(-math.log(ROPE_BASE) * 2.0 * freq_index / head_dim)
    angles = jnp.arange(length, dtype=F32)[:, None] * inv_freq[None, :]
    return (jnp.cos(angles)[None, :, None, :], jnp.sin(angles)[None, :, None, :])


def rope_apply(values, cosine, sine):
    half_dim = values.shape[-1] // 2
    a = values[..., :half_dim]
    b = values[..., half_dim:]
    return jnp.concatenate([a * cosine - b * sine, b * cosine + a * sine], axis=-1)


def rms_parts(v, g):
    s = lax.rsqrt(jnp.mean(v * v, axis=-1, keepdims=True) + EPS_NORM)
    return s, v * s


def rms_back(v, g, gh):
    s, nrm = rms_parts(v, g)
    gg = jnp.sum(gh * nrm, axis=0)
    gv = s * (gh * g - nrm * jnp.mean(gh * g * nrm, axis=-1, keepdims=True))
    return gv, gg


def total(partial_out):
    return lax.psum(partial_out.astype(BF), "tensor").astype(F32)


def shift_down(v, by):
    if by == 0:
        return v
    return jnp.pad(v, ((0, 0), (by, 0), (0, 0)))[:, : v.shape[1]]


def shift_up(v, by):
    if by == 0:
        return v
    return jnp.pad(v, ((0, 0), (0, by), (0, 0)))[:, by:]


def attend(query, keys, values):
    scale = HEAD_DIM ** (-0.5)
    distance = jnp.arange(SLOT)[:, None] - jnp.arange(SLOT)[None, :]
    allowed = (distance >= 0) & (distance < WINDOW)
    scores = jnp.einsum("mqhd,mkhd->mhqk", query, keys, preferred_element_type=F32) * scale
    scores = jnp.where(allowed, scores, NEG_FILL)
    expo = jnp.exp(scores - jnp.max(scores, axis=-1, keepdims=True))
    return expo / jnp.sum(expo, axis=-1, keepdims=True)


def ffn_forward(h, w_gu, w_down):
    pre = mat_nn(h, w_gu)
    act = (silu(pre[:, :FI]) * pre[:, FI:]).astype(BF)
    return total(mat_nn(act, w_down)), pre, act


def ffn_backward(pre, w_gu, w_down, grad_low):
    gate = pre[:, :FI]
    up = pre[:, FI:]
    ga = mat_nt(grad_low, w_down)
    sig = jax.nn.sigmoid(gate)
    grad_gate = ga * up * sig * (1.0 + gate * (1.0 - sig))
    grad_up = ga * gate * sig
    gp = jnp.concatenate([grad_gate, grad_up], axis=1).astype(BF)
    return total(mat_nt(gp, w_gu)), gp


def layer(x, grad_out, w, small, gains, n):
    rows = x.shape[0]
    m = rows // SLOT
    hr = HW // HEAD_DIM
    cosine, sine = rope_tables(SLOT, HEAD_DIM)
    s1, n1 = rms_parts(x, gains[0])
    h1 = (n1 * gains[0]).astype(BF)
    mixed = mat_nn(h1, w["w_in"])
    mix_x = mixed[:, :EI].reshape(m, SLOT, EI)
    gate_z = mixed[:, EI:]
    conv_w = small["conv_w"].astype(F32)
    pre_conv = small["conv_b"].astype(F32)[None, None, :]
    for j in range(CONV):
        pre_conv = pre_conv + conv_w[j] * shift_down(mix_x, CONV - 1 - j)
    unit = silu(pre_conv).astype(BF).reshape(rows, EI)
    proj = lax.psum(mat_nn(unit, small["w_x"]).astype(BF), "tensor")
    bc = proj[:, DTR:].astype(F32)
    scan_args = (
        proj[:, :DTR],
        bc,
        unit,
        gate_z,
        small["w_dt"],
        small["dt_bias"].astype(F32)[None],
        small["d_skip"].astype(F32)[None],
        small["a_log"].astype(F32).reshape(NSTATE * SUBL, LANES),
    )
    gated = scan_forward(*scan_args)
    x1 = x + total(mat_nn(gated, w["w_out"]))
    h2 = (rms_parts(x1, 0)[1] * gains[1]).astype(BF)
    branch, pre1, act1 = ffn_forward(h2, w["w_gu1"], w["w_down1"])
    x2 = x1 + branch
    h3 = (rms_parts(x2, 0)[1] * gains[2]).astype(BF)
    packed = mat_nn(h3, w["w_qkv"]).reshape(m, SLOT, 3, hr, HEAD_DIM)
    query = rope_apply(packed[:, :, 0], cosine, sine).astype(BF)
    keys = rope_apply(packed[:, :, 1], cosine, sine).astype(BF)
    values = packed[:, :, 2].astype(BF)
    probs = attend(query, keys, values)
    probs_low = probs.astype(BF)
    attended = jnp.einsum("mhqk,mkhd->mqhd", probs_low, values, preferred_element_type=F32)
    attended = attended.reshape(rows, HW).astype(BF)
    x3 = x2 + total(mat_nn(attended, w["w_o"]))
    h4 = (rms_parts(x3, 0)[1] * gains[3]).astype(BF)
    branch, pre2, act2 = ffn_forward(h4, w["w_gu2"], w["w_down2"])
    x4 = x3 + branch

    gb4 = grad_out.astype(BF)
    gh, gp2 = ffn_backward(pre2, w["w_gu2"], w["w_down2"], gb4)
    gv, gg4 = rms_back(x3, gains[3], gh)
    g3 = grad_out + gv
    gb3 = g3.astype(BF)
    gatt = mat_nt(gb3, w["w_o"]).astype(BF).reshape(m, SLOT, hr, HEAD_DIM)
    grad_p = jnp.einsum("mqhd,mkhd->mhqk", gatt, values, preferred_element_type=F32)
    inner = jnp.sum(probs * grad_p, axis=-1, keepdims=True)
    gs = (probs * (grad_p - inner)).astype(BF)
    scale = HEAD_DIM ** (-0.5)
    gq = jnp.einsum("mhqk,mkhd->mqhd", gs, keys, preferred_element_type=F32) * scale
    gk = jnp.einsum("mhqk,mqhd->mkhd", gs, query, preferred_element_type=F32) * scale
    gvv = jnp.einsum("mhqk,mqhd->mkhd", probs_low, gatt, preferred_element_type=F32)
    gpk = (
        jnp.stack([rope_apply(gq, cosine, -sine), rope_apply(gk, cosine, -sine), gvv], axis=2)
        .reshape(rows, 3 * HW)
        .astype(BF)
    )
    gv, gg3 = rms_back(x2, gains[2], total(mat_nt(gpk, w["w_qkv"])))
    g2 = g3 + gv
    gb2 = g2.astype(BF)
    gh, gp1 = ffn_backward(pre1, w["w_gu1"], w["w_down1"], gb2)
    gv, gg2 = rms_back(x1, gains[1], gh)
    g1 = g2 + gv
    gb1 = g1.astype(BF)
    ggated = mat_nt(gb1, w["w_out"])
    gz, gunit, gproj, g_dt, g_bias, g_skip, g_alog = scan_backward(*scan_args, ggated)
    gproj = lax.psum(gproj[:, : DTR + 2 * NSTATE], "tensor")
    g_wx = mat_tn(unit, gproj)
    gu = gunit + mat_nt(gproj, small["w_x"])
    sig = jax.nn.sigmoid(pre_conv)
    gpre = gu.reshape(m, SLOT, EI) * sig * (1.0 + pre_conv * (1.0 - sig))
    g_conv_b = jnp.sum(gpre, axis=(0, 1))
    g_conv_w = jnp.stack(
        [jnp.sum(gpre * shift_down(mix_x, CONV - 1 - j), axis=(0, 1)) for j in range(CONV)]
    )
    gmx = sum(conv_w[j] * shift_up(gpre, CONV - 1 - j) for j in range(CONV))
    gmixed = jnp.concatenate([gmx.reshape(rows, EI).astype(BF), gz], axis=1)
    gv, gg1 = rms_back(x, gains[0], total(mat_nt(gmixed, w["w_in"])))
    g0 = g1 + gv

    left_t = jnp.concatenate([h1, gated, h2, act1, attended, h4, act2], axis=1).T
    rights = jnp.stack([gmixed, gb1, gp1, gb2, gb3, gp2, gb4])
    g_qkv = mat_tn(h3, gpk).astype(BF).reshape(-1, D)
    slab = ring_reduce(left_t, rights, g_qkv, n)
    start = lax.axis_index("tensor") * DG
    g_gain = lax.dynamic_slice_in_dim(jnp.stack([gg1, gg2, gg3, gg4]), start, DG, 1)
    pieces = [g_gain, g_conv_w, g_conv_b, g_bias, g_skip, g_alog, g_wx, g_dt]
    small_grads = jnp.concatenate([p.reshape(-1) for p in pieces])
    return x4.astype(BF), g0, slab, small_grads


def extents(n, shard_rows):
    slab = BIG_ROWS * LINES // n
    before = 0
    after = 0
    back_before = 0
    back_after = 0
    for d in range(n):
        lo, hi = slab * d, slab * (d + 1) - 1
        qs = [p + LEAD + (SMALL_ROWS if p >= FIRST else 0) - shard_rows * d for p in (lo, hi)]
        before = max(before, -qs[0])
        after = max(after, qs[1] + 1 - shard_rows)
    return before, after


def shift_perm(n, by):
    return [(i, i + by) for i in range(n) if 0 <= i + by < n]


def stack_own(flat, n):
    lines = flat.shape[0] // LANES
    before, after = extents(n, lines)
    d = lax.axis_index("dp")
    slab = BIG_ROWS * LINES // n
    nxt = lax.ppermute(flat[: after * LANES], "dp", shift_perm(n, -1))
    prv = lax.ppermute(flat[-before * LANES :], "dp", shift_perm(n, 1))
    ext = jnp.concatenate([prv, flat, nxt])
    at = before + slab * d + LEAD - lines * d
    limit = before + lines + after - slab

    def take(a):
        return lax.dynamic_slice_in_dim(ext, jnp.clip(a, 0, limit) * LANES, slab * LANES, 0).reshape(-1, D)

    one = take(at)
    two = take(at + SMALL_ROWS)
    row = lax.broadcasted_iota(jnp.int32, (BIG_ROWS // n, 1), 0) + d * (BIG_ROWS // n)
    return jnp.where(row < FIRST // LINES, one, two)


def window(values, shift, size):
    length = values.shape[0]
    if length >= size:
        s = jnp.clip(shift, 0, length - size)
        got = lax.dynamic_slice_in_dim(values, s, size, 0)
        room = jnp.zeros((3 * size,), values.dtype)
        room = lax.dynamic_update_slice_in_dim(room, got, size + jnp.clip(s - shift, -size, size), 0)
        return room[size : 2 * size]
    padded = jnp.concatenate([jnp.zeros((size,), values.dtype), values, jnp.zeros((size,), values.dtype)])
    return lax.dynamic_slice_in_dim(padded, jnp.clip(shift + size, 0, length + size), size, 0)


def per_device(n, tokens, cotangent, lengths, master, moment_one, moment_two):
    d = lax.axis_index("dp")
    shard = master.shape[1]
    lines = shard // LANES
    own = master[0].astype(BF)
    base = d * shard
    small_own = jnp.concatenate(
        [
            window(own, -base, GAIN_ROWS * LANES),
            window(own, (LEAD + FIRST) * LANES - base, SMALL_ROWS * LANES),
        ]
    )
    small_flat = lax.psum(small_own, "dp")
    gains = lax.all_gather(small_flat[: GAIN_ROWS * LANES].reshape(4, DG), "tensor", axis=1, tiled=True)
    gains = gains.astype(F32)
    small = {}
    at = GAIN_ROWS * LANES
    for name, shape in SMALL:
        count = math.prod(shape)
        small[name] = small_flat[at : at + count].reshape(shape)
        at += count
    weights = ring_gather(stack_own(own, n), n)
    w = {}
    for name, rows in BIG:
        w[name] = weights[BIG_OFF[name] : BIG_OFF[name] + rows]
    w["w_qkv"] = w["w_qkv"].reshape(D, 3 * HW)
    x = tokens.astype(F32)
    pos = lax.broadcasted_iota(jnp.int32, (tokens.shape[0] // SLOT, SLOT), 1)
    valid = (pos < lengths[:, None]).astype(F32).reshape(-1, 1)
    grad = cotangent.astype(F32) * valid
    out, grad_in, slab, small_grads = layer(x, grad, w, small, gains, n)

    small_sum = lax.psum(small_grads.astype(BF), "dp").astype(F32)
    slab_lines = BIG_ROWS * LINES // n
    before, after = extents(n, lines)
    flat = slab.astype(F32).reshape(-1)
    tail = lax.ppermute(slab.reshape(-1)[-after * LANES :], "dp", shift_perm(n, 1)).astype(F32)
    head = lax.ppermute(slab.reshape(-1)[: before * LANES], "dp", shift_perm(n, -1)).astype(F32)
    pad = jnp.zeros((2 * SMALL_ROWS * LANES,), F32)
    ext = jnp.concatenate([pad, tail, flat, head, pad])
    first_at = (2 * SMALL_ROWS + after) * LANES + base - LEAD * LANES - d * slab_lines * LANES
    limit = ext.shape[0] - shard
    one = lax.dynamic_slice_in_dim(ext, jnp.clip(first_at, 0, limit), shard, 0)
    two = lax.dynamic_slice_in_dim(ext, jnp.clip(first_at - SMALL_ROWS * LANES, 0, limit), shard, 0)
    index = base + jnp.arange(shard, dtype=jnp.int32)
    mid = (LEAD + FIRST) * LANES
    end = mid + SMALL_ROWS * LANES
    grad_shard = jnp.where(index < mid, one, two)
    grad_shard = jnp.where(
        index < LEAD * LANES,
        window(small_sum[: LEAD * LANES], base, shard),
        jnp.where((index >= mid) & (index < end), window(small_sum[LEAD * LANES :], base - mid, shard), grad_shard),
    )
    used = end + (BIG_ROWS * LINES - FIRST) * LANES
    grad_shard = jnp.where(index < used, grad_shard, 0.0)

    weights_old = master[0]
    first = BETA_ONE * moment_one[0] + (1.0 - BETA_ONE) * grad_shard
    second = BETA_TWO * moment_two[0] + (1.0 - BETA_TWO) * grad_shard * grad_shard
    trust_ratio = first / (jnp.sqrt(second) + ADAM_EPS) + DECAY_W * weights_old
    bounds = group_bounds()
    pieces = []
    for lower_end, upper_end in bounds:
        within = (index >= lower_end) & (index < upper_end)
        pieces.append(
            jnp.stack(
                [
                    jnp.sum(jnp.where(within, weights_old * weights_old, 0.0)),
                    jnp.sum(jnp.where(within, trust_ratio * trust_ratio, 0.0)),
                ]
            )
        )
    squares = lax.psum(jnp.stack(pieces), ("dp", "tensor"))
    trust_factor = jnp.sqrt(squares[:, 0] + TRUST_EPSILON) * lax.rsqrt(squares[:, 1] + TRUST_EPSILON)
    column_trust = jnp.zeros((shard,), F32)
    for g, (lower_end, upper_end) in enumerate(bounds):
        within = (index >= lower_end) & (index < upper_end)
        column_trust = jnp.where(within, trust_factor[g], column_trust)
    master_new = weights_old - LEARN_RATE * column_trust * trust_ratio
    return (
        out,
        grad_in,
        master_new[None, :],
        first[None, :],
        second[None, :],
        master_new.astype(BF)[None, :],
        grad_shard[None, :],
        jnp.sqrt(squares),
    )


def solution(mesh):
    row = P("dp", None)
    flat = P("tensor", "dp")
    return jax.shard_map(
        functools.partial(per_device, mesh.shape["dp"]),
        mesh=mesh,
        in_specs=(row, row, P("dp"), flat, flat, flat),
        out_specs=(row, row, flat, flat, flat, flat, flat, P()),
        check_vma=False,
    )
```

time: 6930 us -> 2540 us (0.37)
  waiting for transfers between devices: 2600 us -> 248 us
  local copies, waits for them, and re-layouts: 2120 us -> 519 us
  other arithmetic: 1670 us -> 646 us
  Pallas kernels: 0 us -> 941 us
  matrix products: 400 us -> 90.2 us
    all_gather x1 -> x0, waiting for transfers between devices: 1760 us -> none  [per_device(): lax.all_gather(own_copy, 'dp', axis=0, tiled=True)]
    pallas_call x0 -> x4, Pallas kernels: none -> 941 us  [the longest x1 446 us: ring_reduce(): pl.pallas_call(functools.partial(reduce_kernel, n), out_shape=jax.ShapeDt...]
    unnamed x471 -> x240, local copies, waits for them, and re-layouts: 1070 us -> 127 us
    all_to_all x1 -> x0, waiting for transfers between devices: 720 us -> none  [per_device(): lax.all_to_all(pack(grads_summed, placed, flat_len, dp_count).astype(jnp....]
    convert_element_type x20 -> x10, other arithmetic: 652 us -> 52.9 us  [the longest x1 45.5 us: per_device(): master_new.astype(BF)[None, :]]
    slice x25 -> x21, local copies, waits for them, and re-layouts: 533 us -> 17.5 us  [the longest x1 6.61 us: per_device(): w[name] = weights[BIG_OFF[name]:BIG_OFF[name] + rows]]
    dot_general x136 -> x25, matrix products: 400 us -> 89.6 us  [the longest x9 42.6 us: mat_nt(): lax.dot_general(a, b, (((1,), (1,)), ((), ())), preferred_element_type=F32)]
    broadcast_in_dim x2 -> x9, local copies, waits for them, and re-layouts: 0.7 us -> 261 us  [the longest x1 56.9 us: per_device(): master_new.astype(BF)[None, :]]
  transfers between devices with their start and end apart: 11 -> 15, of which waited for: 8 -> 8; matrix products, arithmetic and copies ran while one was open for 11% -> 21% of each run, Pallas kernels for 0% -> 18%
where the time goes in v1:
time: 2540 us; the launch traced here: 2520 us
  Pallas kernels  941 us (37%)
  other arithmetic  646 us (25%)
  local copies, waits for them, and re-layouts  519 us (20%)
  waiting for transfers between devices  248 us (10%)
  matrix products  90.2 us (4%)
  blocking collectives  47 us (2%)
    pallas_call x1, Pallas kernels, ring_reduce(): pl.pallas_call(functools.partial(reduce_kernel, n), out_shape=jax.ShapeDt...  446 us
    pallas_call x1, Pallas kernels, ring_gather(): pl.pallas_call(functools.partial(gather_kernel, n, subs), out_shape=jax.S...  443 us
    unnamed x20, other arithmetic  251 us
    unnamed x240, local copies, waits for them, and re-layouts  127 us
    mul x1, other arithmetic, per_device(): BETA_TWO * moment_two[0] + (1.0 - BETA_TWO) * grad_shard * grad_shard  126 us
    psum x7, waiting for transfers between devices, total(): return lax.psum(partial_out.astype(BF), 'tensor').astype(F32)  120 us
    reduce_sum x1, other arithmetic, per_device(): jnp.sum(jnp.where(within, trust_ratio * trust_ratio, 0.0))  91.3 us
    psum x1, waiting for transfers between devices, per_device(): small_sum = lax.psum(small_grads.astype(BF), 'dp').astype(F32)  67.9 us
  transfers between devices with their start and end apart: 15, of which 8 were waited for; matrix products, arithmetic and copies ran while one was open for 21% of the time, Pallas kernels for 18%

profile of v1, /device:TPU:2, one launch (start us, length us, event | category | flops | bytes accessed | tf_op | source)
XLA Modules:
  0.0 2521.5 jit_solution(12317646914558438689)
XLA Ops:
  7.2 114.9 %reduce = f32[2923648]{0:T(1024)} reduce(f32[1,2923648]{1,0:T(1,128)} %param.9, f32[]{:T(128)} %constant.179), dimensions={0}, to_apply=%param.9.reduce_sub_computation | reduce | bytes 23389188 | tf_op args[3]
  122.1 39.8 %select_reduce_fusion.1 = (f32[]{:T(128)}, f32[]{:T(128)}, f32[]{:T(128)}, f32[]{:T(128)}, f32[]{:T(128)}, /*index=5*/f32[]{:T(128)}, f32[]{:T(128)}, f32[]{:T(1...) fusion(s32[]{:T(128)S(6)} %mul.733, f32[2923648]{0:T(1024)} %reduce), kind=kLoop, calls=%fused_computation.18 | loop fusion | flops 286517504 | bytes 17541968 | tf_op jit(solution)/shard_map/reduce_sum | solution.py:808
  187.6 17.0 pad_maximum_fusion
  237.0 443.3 %ring_gather.1 = bf16[11264,2048]{1,0:T(8,128)(2,1)} custom-call(bf16[1408,2048]{1,0:T(8,128)(2,1)S(1)} %broadcast_select_fusion.own_ref), custom_call_target="tpu_custom_call" | custom-call | tf_op jit(solution)/shard_map/ring_gather/pallas_call | solution.py:189
  702.4 29.1 %all-reduce.21.cloned.1.call-done = bf16[256,160]{1,0:T(8,128)(2,1)} async-done(((bf16[256,160]{1,0:T(8,128)(2,1)}), bf16[256,160]{1,0:T(8,128)(2,1)}) %all-reduce.21.cloned.1.call-update) | async-done | bytes 81936 | tf_op jit(solution)/shard_map/psum | solution.py:608
  752.5 34.3 %all-reduce.23.cloned.1.call-done = bf16[256,2048]{1,0:T(8,128)(2,1)} async-done(((bf16[256,2048]{1,0:T(8,128)(2,1)}), bf16[256,2048]{1,0:T(8,128)(2,1)}) %all-reduce.23.cloned.1.call-update) | async-done | bytes 1048592 | tf_op jit(solution)/shard_map/psum | solution.py:551
  853.6 34.6 %all-reduce.27.cloned.1.call-done = bf16[256,2048]{1,0:T(8,128)(2,1)} async-done(((bf16[256,2048]{1,0:T(8,128)(2,1)}), bf16[256,2048]{1,0:T(8,128)(2,1)}) %all-reduce.27.cloned.1.call-update) | async-done | bytes 1048592 | tf_op jit(solution)/shard_map/psum | solution.py:551
  909.9 126.1 %multiply_reduce_fusion = f32[2923648]{0:T(1024)} fusion(f32[1,2923648]{1,0:T(1,128)} %param.11), kind=kLoop, calls=%fused_computation.116 | loop fusion | flops 2923648 | bytes 23389184 | tf_op jit(solution)/shard_map/mul | solution.py:799
  1036.0 115.2 %reduce.1 = f32[2923648]{0:T(1024)} reduce(f32[1,2923648]{1,0:T(1,128)} %param.10, f32[]{:T(128)} %constant.179), dimensions={0}, to_apply=%param.10.reduce_sub_computation | reduce | bytes 23389188 | tf_op args[4]
  1176.1 33.5 %all-reduce.31.cloned.1.call-done = bf16[256,2048]{1,0:T(8,128)(2,1)} async-done(((bf16[256,2048]{1,0:T(8,128)(2,1)}), bf16[256,2048]{1,0:T(8,128)(2,1)}) %all-reduce.31.cloned.1.call-update) | async-done | bytes 1048592 | tf_op jit(solution)/shard_map/psum | solution.py:551
  1272.7 40.8 %scan_backward.1 = (bf16[256,1024]{1,0:T(8,128)(2,1)}, f32[256,1024]{1,0:T(8,128)}, bf16[256,256]{1,0:T(8,128)(2,1)}, f32[128,1024]{1,0:T(8,128)}, f32[1,1024]{1...) custom-call(bf16[256,128]{1,0:T(8,128)(2,1)} %slice.407.proj_ref, f32[256,32]{1,0:T(8,128)} %slice_convert_fusion.1.bc_ref, ...), custom_call_target="tpu_custom_call" | custom-call | tf_op jit(solution)/shard_map/scan_backward/pallas_call | solution.py:499
  1315.8 30.2 %all-reduce.35.cloned.1.call-done = bf16[256,160]{1,0:T(8,128)(2,1)} async-done(((bf16[256,160]{1,0:T(8,128)(2,1)}), bf16[256,160]{1,0:T(8,128)(2,1)}) %all-reduce.35.cloned.1.call-update) | async-done | bytes 81936 | tf_op jit(solution)/shard_map/psum | solution.py:666
  1365.7 445.6 %ring_reduce.1 = bf16[1408,2048]{1,0:T(8,128)(2,1)} custom-call(bf16[9728,256]{1,0:T(8,128)(2,1)} %copy.90.left_ref, bf16[7,256,2048]{2,1,0:T(8,128)(2,1)} %bitcast_dynamic-update-slice_fusion.right_refs, bf16[1536,2048]{1,0:T(8,128)(2,1)} %reshape.421.qkv_ref), custom_call_target="tpu_custom_call" | custom-call | tf_op jit(solution)/shard_map/ring_reduce/pallas_call | solution.py:299
  1839.1 97.9 %dynamic-update-slice.2 = f32[4435840]{0:T(1024)} dynamic-update-slice(f32[4435840]{0:T(1024)} %convert_dynamic-update-slice_fusion, f32[2883584]{0:T(1024)} %reshape.423, s32[]{} %constant.205) | dynamic-update-slice | bytes 23068676
  1940.2 22.5 dynamic-update-slice.4
  1978.7 67.9 %all-reduce.37.cloned.1.call-done = bf16[320512]{0:T(1024)(128)(2,1)} async-done(((bf16[320512]{0:T(1024)(128)(2,1)}), bf16[320512]{0:T(1024)(128)(2,1)}) %all-reduce.37.cloned.1.call-update) | async-done | bytes 641040 | tf_op jit(solution)/shard_map/psum | solution.py:773
  2049.2 91.3 %select_reduce_fusion = (f32[]{:T(128)}, f32[]{:T(128)}, f32[]{:T(128)}, f32[]{:T(128)}, f32[]{:T(128)}, /*index=5*/f32[]{:T(128)}, f32[]{:T(128)}, f32[]{:T(128...) fusion(s32[]{:T(128)S(6)} %mul.733, ...), kind=kLoop, calls=%fused_computation.17 | loop fusion | flops 336219520 | bytes 118228064 | tf_op jit(solution)/shard_map/reduce_sum | solution.py:809
  2167.7 41.6 %psum.103 = f32[19,2]{0,1:T(2,128)S(1)} all-reduce(f32[19,2]{0,1:T(2,128)S(1)} %stack.394), channel_id=1, replica_groups=mesh['dp'=8,'tensor'=4] {'dp','tensor'}, use_global_device_ids=true, to_apply=%region_70.71 | all-reduce | flops 38 | bytes 304 | tf_op jit(solution)/shard_map/psum | solution.py:813
  2210.7 45.5 %fusion.205 = (bf16[2923648]{0:T(1024)(128)(2,1)}, f32[2923648]{0:T(1024)S(1)}) fusion(f32[2923648]{0:T(1024)} %reduce, f32[2923648]{0:T(1024)} %get-tuple-element.93, f32[]{:T(128)} %bitcast.119, f32[]{:T(128)} %bitcast.118, f32[]{:T(128)} %bitcast.117, f32[]{:T(128)} %bitcast.116, f32[]{:T(128)} %bitcast.115, f32[]{:T(128)} %bitcast.114, f32[]{:T(128)} %bitcast.113, ...), kind=kLoop, calls=%fused_computation.384 | loop fusion | flops 236815488 | bytes 40931152 | tf_op jit(solution)/shard_map/convert_element_type | solution.py:826
  2256.2 55.5 %broadcast_in_dim.203 = f32[1,2923648]{1,0:T(1,128)} reshape(f32[2923648]{0:T(1024)S(1)} %get-tuple-element.92) | data formatting | bytes 23389184 | tf_op jit(solution)/shard_map/broadcast_in_dim | solution.py:823
  2311.7 56.9 %broadcast_in_dim.206 = bf16[1,2923648]{1,0:T(2,128)(2,1)} reshape(bf16[2923648]{0:T(1024)(128)(2,1)} %get-tuple-element.91) | data formatting | bytes 11694592 | tf_op jit(solution)/shard_map/broadcast_in_dim | solution.py:826
  2368.7 45.1 %broadcast_in_dim.204 = f32[1,2923648]{1,0:T(1,128)} reshape(f32[2923648]{0:T(1024)} %get-tuple-element.95) | data formatting | bytes 23389184 | tf_op jit(solution)/shard_map/broadcast_in_dim | solution.py:824
  2413.8 45.1 %broadcast_in_dim.205 = f32[1,2923648]{1,0:T(1,128)} reshape(f32[2923648]{0:T(1024)} %get-tuple-element.94) | data formatting | bytes 23389184 | tf_op jit(solution)/shard_map/broadcast_in_dim | solution.py:825
  2458.9 55.8 %broadcast_in_dim.207 = f32[1,2923648]{1,0:T(1,128)} reshape(f32[2923648]{0:T(1024)S(1)} %bitcast.222) | data formatting | bytes 23389184 | tf_op jit(solution)/shard_map/broadcast_in_dim | solution.py:827
  (457 shorter events, 376.5 us)
Async XLA Ops:
  7.2 673.2 %all-reduce.19.cloned.1.call-start = ((), (), s32[]{:S(2)}) async-start(), calls=%async_computation | async-start | bytes 1282048 | tf_op jit(solution)/shard_map/psum | solution.py:753
  162.8 24.8 collective-permute-start.1
  165.4 22.2 collective-permute-start
  186.7 544.8 %all-reduce.21.cloned.1.call-start = ((), (), s32[]{:S(2)}) async-start(), calls=%async_computation.1 | async-start | bytes 262144 | tf_op jit(solution)/shard_map/psum | solution.py:608
  187.6 562.8 %copy-start.86 = (f32[256]{0:T(256)}, f32[256]{0:T(256)S(1)}, u32[]{:S(2)}) copy-start(f32[256]{0:T(256)S(1)} %add_rsqrt_fusion.3) | copy-start | bytes 3076
  687.0 63.4 %copy-start.66 = (f32[1,2048]{1,0:T(1,128)}, f32[1,2048]{1,0:T(1,128)S(1)}, u32[]{:S(2)}) copy-start(f32[1,2048]{1,0:T(1,128)S(1)} %get-tuple-element.137) | copy-start | bytes 24580
  687.0 107.6 %copy-start.68 = (f32[1,2048]{1,0:T(1,128)}, f32[1,2048]{1,0:T(1,128)S(1)}, u32[]{:S(2)}) copy-start(f32[1,2048]{1,0:T(1,128)S(1)} %get-tuple-element.136) | copy-start | bytes 24580
  687.0 153.7 %copy-start.70 = (f32[1,2048]{1,0:T(1,128)}, f32[1,2048]{1,0:T(1,128)S(1)}, u32[]{:S(2)}) copy-start(f32[1,2048]{1,0:T(1,128)S(1)} %get-tuple-element.135) | copy-start | bytes 24580
  700.1 86.7 %all-reduce.23.cloned.1.call-start = ((), (), s32[]{:S(2)}) async-start(), calls=%async_computation.2 | async-start | bytes 2097152 | tf_op jit(solution)/shard_map/psum | solution.py:551
  750.3 88.4 %all-reduce.25.cloned.1.call-start = ((), (), s32[]{:S(2)}) async-start(), calls=%async_computation.3 | async-start | bytes 2097152 | tf_op jit(solution)/shard_map/psum | solution.py:551
  801.9 86.3 %all-reduce.27.cloned.1.call-start = ((), (), s32[]{:S(2)}) async-start(), calls=%async_computation.4 | async-start | bytes 2097152 | tf_op jit(solution)/shard_map/psum | solution.py:551
  851.3 302.4 %all-reduce.29.cloned.1.call-start = ((), (), s32[]{:S(2)}) async-start(), calls=%async_computation.5 | async-start | bytes 2097152 | tf_op jit(solution)/shard_map/psum | solution.py:551
  890.4 282.3 %copy-start.2 = (f32[256,2048]{1,0:T(8,128)}, f32[256,2048]{1,0:T(8,128)S(1)}, u32[]{:S(2)}) copy-start(f32[256,2048]{1,0:T(8,128)S(1)} %get-tuple-element.103) | copy-start | bytes 6291460
  909.4 300.2 %all-reduce.31.cloned.1.call-start = ((), (), s32[]{:S(2)}) async-start(), calls=%async_computation.6 | async-start | bytes 2097152 | tf_op jit(solution)/shard_map/psum | solution.py:551
  1172.7 90.6 %all-reduce.33.cloned.1.call-start = ((), (), s32[]{:S(2)}) async-start(), calls=%async_computation.7 | async-start | bytes 2097152 | tf_op jit(solution)/shard_map/psum | solution.py:551
  1226.4 119.6 %all-reduce.35.cloned.1.call-start = ((), (), s32[]{:S(2)}) async-start(), calls=%async_computation.8 | async-start | bytes 262144 | tf_op jit(solution)/shard_map/psum | solution.py:666
  1272.7 73.2 %copy-start.28 = (f32[256,1024]{1,0:T(8,128)S(1)}, f32[256,1024]{1,0:T(8,128)}, u32[]{:S(2)}) copy-start(f32[256,1024]{1,0:T(8,128)} %copy-done.27) | copy-start | bytes 3145732
  1272.7 73.2 %copy-start.41 = (f32[256,2048]{1,0:T(8,128)S(1)}, f32[256,2048]{1,0:T(8,128)}, u32[]{:S(2)}) copy-start(f32[256,2048]{1,0:T(8,128)} %copy-done.40) | copy-start | bytes 6291460
  1313.6 649.2 %all-reduce.39.cloned.1.call-start = ((), (), s32[]{:S(2)}) async-start(), calls=%async_computation.10 | async-start | bytes 4194304 | tf_op jit(solution)/shard_map/psum | solution.py:551
  1818.7 18.2 collective-permute-start.2
  1822.4 224.2 %all-reduce.37.cloned.1.call-start = ((), (), s32[]{:S(2)}) async-start(), calls=%async_computation.9 | async-start | bytes 1282048 | tf_op jit(solution)/shard_map/psum | solution.py:773
  1834.0 102.9 %collective-permute-start.3 = (bf16[38016]{0:T(1024)(128)(2,1)S(1)}, bf16[38016]{0:T(1024)(128)(2,1)S(1)}, u32[]{:S(2)}, u32[]{:S(2)}) collective-permute-start(bf16[38016]{0:T(1024)(128)(2,1)S(1)} %slice.435), channel_id=1, source_target_pairs={{4,0},{8,4},{12,8},{16,12},{20,16},{24,20},{28,24},{5,1},{9,5},{13... | collective-permute-start | bytes 228104 | tf_op jit(solution)/shard_map/ppermute | solution.py:778
  2368.6 90.3 %slice-start = ((s8[11698176]{0:T(1024)(128)(4,1)}), s8[4194304]{0:T(1024)(128)(4,1)S(1)}, s32[]{:S(2)}) async-start(s8[11698176]{0:T(1024)(128)(4,1)} %bitcast.221), calls=%async_computation.11 | async-start | bytes 8388608
  2368.7 90.3 %slice-start.1 = ((s8[11698176]{0:T(1024)(128)(4,1)}), s8[4194304]{0:T(1024)(128)(4,1)S(1)}, s32[]{:S(2)}) async-start(s8[11698176]{0:T(1024)(128)(4,1)} %bitcast.221), calls=%async_computation.12 | async-start | bytes 8388608
  (106 other events, 770.7 us)
Sparse Core Ops, SparseCore 0:
  186.8 77.0 all-reduce.18
  700.2 31.2 all-reduce.20
  750.5 36.2 all-reduce.22
  802.0 36.7 all-reduce.24
  851.4 36.7 all-reduce.26
  909.5 36.7 all-reduce.28
  1172.8 36.7 all-reduce.30
  1226.5 36.7 all-reduce.32
  1313.7 32.2 all-reduce.34
  1822.5 49.8 all-reduce.38
  1974.2 72.3 all-reduce.36

commit v2 on v1

--- a/solution.py
+++ b/solution.py
@@ -69,6 +69,8 @@
 LINES = D // LANES
 FIRST = BIG_OFF["w_out"] * LINES
 LEAD = GAIN_ROWS
+CHUNK = 1024
+SLACK = -(-(SMALL_ROWS + GAIN_ROWS) // CHUNK) * CHUNK
 
 
 def group_bounds():
@@ -197,6 +199,7 @@
             pltpu.SemaphoreType.DMA((2, n - 1, subs)),
             pltpu.SemaphoreType.DMA((2, n - 1, subs)),
         ],
+        cost_estimate=pl.CostEstimate(flops=10**9, bytes_accessed=1500 * 10**6, transcendentals=0),
         compiler_params=pltpu.CompilerParams(
             collective_id=0, has_side_effects=True, vmem_limit_bytes=32 << 20
         ),
@@ -210,10 +213,10 @@
             return size
 
 
-def reduce_kernel(n, left_ref, right_refs, qkv_ref, out_ref, slots, ssem, rsem, out_sem):
+def reduce_kernel(n, shard_lines, left_ref, right_refs, qkv_ref, out_ref, slots, lines, ssem, rsem, out_sem):
     t = lax.axis_index("tensor")
     d, p, right, left = ring_neighbours(n)
-    rows = out_ref.shape[0]
+    rows = BIG_ROWS // n
     half = rows // 2
     SUB = piece_of(half)
     subs = half // SUB
@@ -264,49 +267,61 @@
                 def put(value):
                     if step > 0:
                         value = value + slots[way, step, here, :].astype(F32)
-                    slots[way, step, here, :] = value.astype(BF)
+                    if step < n - 1:
+                        slots[way, step, here, :] = value.astype(BF)
+                    else:
+                        for j in range(LINES):
+                            lines[way, pl.ds(j, SUB, stride=LINES), :] = value[:, j * LANES : (j + 1) * LANES]
+
+                if step == n - 1:
+
+                    @pl.when(c > 0)
+                    def _():
+                        leave(way, c - 1).wait()
 
                 own_into(at, put)
                 if step < n - 1:
                     copy(way, step, c).start()
                 else:
-                    pltpu.make_async_copy(
-                        slots.at[way, step, here],
-                        out_ref.at[pl.ds(pl.multiple_of(way * half + c * SUB, SUB), SUB)],
-                        out_sem.at[way, c],
-                    ).start()
+                    leave(way, c).start()
+
+    def leave(way, c):
+        row = d * rows + way * half + c * SUB
+        to = row * LINES + LEAD + jnp.where(row >= FIRST // LINES, SMALL_ROWS, 0) - d * shard_lines + SLACK
+        return pltpu.make_async_copy(
+            lines.at[way], out_ref.at[pl.ds(to, SUB * LINES), 0], out_sem.at[way]
+        )
 
     for step in range(n):
         run(step)
+    for way in (0, 1):
+        leave(way, subs - 1).wait()
 
     @pl.loop(0, subs)
     def _(c):
-        here = pl.ds(pl.multiple_of(c * SUB, SUB), SUB)
         for way in (0, 1):
             for step in range(n - 1):
                 copy(way, step, c).wait_send()
-            pltpu.make_async_copy(
-                slots.at[way, n - 1, here],
-                out_ref.at[pl.ds(pl.multiple_of(way * half + c * SUB, SUB), SUB)],
-                out_sem.at[way, c],
-            ).wait()
-
-
-def ring_reduce(left_t, rights, qkv_grad, n):
+
+
+def ring_reduce(left_t, rights, qkv_grad, n, shard_lines):
     rows = BIG_ROWS // n
-    subs = rows // 2 // piece_of(rows // 2)
+    sub = piece_of(rows // 2)
+    subs = rows // 2 // sub
     vm = pl.BlockSpec(memory_space=pltpu.VMEM)
     return pl.pallas_call(
-        functools.partial(reduce_kernel, n),
-        out_shape=jax.ShapeDtypeStruct((rows, D), BF),
+        functools.partial(reduce_kernel, n, shard_lines),
+        out_shape=jax.ShapeDtypeStruct((shard_lines + 2 * SLACK, 1, LANES), F32),
         in_specs=[vm, vm, vm],
         out_specs=pl.BlockSpec(memory_space=pl.ANY),
         scratch_shapes=[
             pltpu.VMEM((2, n, rows // 2, D), BF),
+            pltpu.VMEM((2, sub * LINES, LANES), F32),
             pltpu.SemaphoreType.DMA((2, n - 1, subs)),
             pltpu.SemaphoreType.DMA((2, n - 1, subs)),
-            pltpu.SemaphoreType.DMA((2, subs)),
+            pltpu.SemaphoreType.DMA((2,)),
         ],
+        cost_estimate=pl.CostEstimate(flops=10**9, bytes_accessed=1500 * 10**6, transcendentals=0),
         compiler_params=pltpu.CompilerParams(
             collective_id=1, has_side_effects=True, vmem_limit_bytes=67043328
         ),
@@ -680,12 +695,12 @@
     left_t = jnp.concatenate([h1, gated, h2, act1, attended, h4, act2], axis=1).T
     rights = jnp.stack([gmixed, gb1, gp1, gb2, gb3, gp2, gb4])
     g_qkv = mat_tn(h3, gpk).astype(BF).reshape(-1, D)
-    slab = ring_reduce(left_t, rights, g_qkv, n)
     start = lax.axis_index("tensor") * DG
     g_gain = lax.dynamic_slice_in_dim(jnp.stack([gg1, gg2, gg3, gg4]), start, DG, 1)
     pieces = [g_gain, g_conv_w, g_conv_b, g_bias, g_skip, g_alog, g_wx, g_dt]
-    small_grads = jnp.concatenate([p.reshape(-1) for p in pieces])
-    return x4.astype(BF), g0, slab, small_grads
+    small_grads = jnp.concatenate([p.reshape(-1, LANES).astype(BF) for p in pieces])
+    small_grads, left_t = lax.optimization_barrier((small_grads, left_t))
+    return x4.astype(BF), g0, (left_t, rights, g_qkv), small_grads
 
 
 def extents(n, shard_rows):
@@ -706,60 +721,284 @@
     return [(i, i + by) for i in range(n) if 0 <= i + by < n]
 
 
-def stack_own(flat, n):
-    lines = flat.shape[0] // LANES
-    before, after = extents(n, lines)
+def stack_kernel(n, shard_lines, before, per, top_ref, own_ref, bottom_ref, out_ref, hold, sem):
     d = lax.axis_index("dp")
-    slab = BIG_ROWS * LINES // n
-    nxt = lax.ppermute(flat[: after * LANES], "dp", shift_perm(n, -1))
-    prv = lax.ppermute(flat[-before * LANES :], "dp", shift_perm(n, 1))
-    ext = jnp.concatenate([prv, flat, nxt])
-    at = before + slab * d + LEAD - lines * d
-    limit = before + lines + after - slab
-
-    def take(a):
-        return lax.dynamic_slice_in_dim(ext, jnp.clip(a, 0, limit) * LANES, slab * LANES, 0).reshape(-1, D)
-
-    one = take(at)
-    two = take(at + SMALL_ROWS)
-    row = lax.broadcasted_iota(jnp.int32, (BIG_ROWS // n, 1), 0) + d * (BIG_ROWS // n)
-    return jnp.where(row < FIRST // LINES, one, two)
+    i = pl.program_id(0)
+    steps = BIG_ROWS // n // per
+    size = per * LINES
+
+    def fetch(k, slot):
+        row = d * (BIG_ROWS // n) + k * per
+        a = row * LINES + LEAD + jnp.where(row >= FIRST // LINES, SMALL_ROWS, 0) - d * shard_lines
+        high = a < 0
+        low = a + size > shard_lines
+
+        @pl.when(high)
+        def _():
+            pltpu.make_async_copy(top_ref.at[pl.ds(a + before, size), 0], hold.at[slot], sem.at[slot]).start()
+
+        @pl.when(low)
+        def _():
+            pltpu.make_async_copy(
+                bottom_ref.at[pl.ds(a + size - shard_lines, size), 0], hold.at[slot], sem.at[slot]
+            ).start()
+
+        @pl.when(jnp.logical_not(jnp.logical_or(high, low)))
+        def _():
+            pltpu.make_async_copy(own_ref.at[pl.ds(a, size), 0], hold.at[slot], sem.at[slot]).start()
+
+    @pl.when(i == 0)
+    def _():
+        for k in range(min(3, steps)):
+            fetch(k, k)
+
+    @pl.when(i + 3 < steps)
+    def _():
+        fetch(i + 3, lax.rem(i + 3, 4))
+
+    slot = lax.rem(i, 4)
+    pltpu.make_async_copy(own_ref.at[pl.ds(0, size), 0], hold.at[slot], sem.at[slot]).wait()
+    for j in range(LINES):
+        out_ref[:, j * LANES : (j + 1) * LANES] = hold[slot, pl.ds(j, per, stride=LINES), :].astype(BF)
+
+
+def stack_own(lines3, n):
+    shard_lines = lines3.shape[0]
+    before, after = extents(n, shard_lines)
+    rows = BIG_ROWS // n
+    per = 64 if rows % 64 == 0 else 32
+    size = per * LINES
+    nxt = lax.ppermute(lines3[:after], "dp", shift_perm(n, -1))
+    prv = lax.ppermute(lines3[shard_lines - before :], "dp", shift_perm(n, 1))
+    top = jnp.concatenate([prv, lines3[:size]])
+    bottom = jnp.concatenate([lines3[shard_lines - size :], nxt])
+    hbm = pl.BlockSpec(memory_space=pl.ANY)
+    return pl.pallas_call(
+        functools.partial(stack_kernel, n, shard_lines, before, per),
+        grid=(rows // per,),
+        out_shape=jax.ShapeDtypeStruct((rows, D), BF),
+        in_specs=[hbm] * 3,
+        out_specs=pl.BlockSpec((per, D), lambda i: (i, 0)),
+        scratch_shapes=[pltpu.VMEM((4, size, LANES), F32), pltpu.SemaphoreType.DMA((4,))],
+        compiler_params=pltpu.CompilerParams(vmem_limit_bytes=24 << 20),
+        name="stack_own",
+    )(top, lines3, bottom)
 
 
 def window(values, shift, size):
     length = values.shape[0]
-    if length >= size:
-        s = jnp.clip(shift, 0, length - size)
-        got = lax.dynamic_slice_in_dim(values, s, size, 0)
-        room = jnp.zeros((3 * size,), values.dtype)
-        room = lax.dynamic_update_slice_in_dim(room, got, size + jnp.clip(s - shift, -size, size), 0)
-        return room[size : 2 * size]
-    padded = jnp.concatenate([jnp.zeros((size,), values.dtype), values, jnp.zeros((size,), values.dtype)])
-    return lax.dynamic_slice_in_dim(padded, jnp.clip(shift + size, 0, length + size), size, 0)
-
-
-def per_device(n, tokens, cotangent, lengths, master, moment_one, moment_two):
+    s = jnp.clip(shift, 0, length - size)
+    got = lax.dynamic_slice_in_dim(values, s, size, 0)
+    room = jnp.zeros((3 * size,) + values.shape[1:], values.dtype)
+    room = lax.dynamic_update_slice_in_dim(room, got, size + jnp.clip(s - shift, -size, size), 0)
+    return room[size : 2 * size]
+
+
+def moments_kernel(groups, shard, bounds_ref, grad_ref, w_ref, one_ref, two_ref,
+                   first_ref, second_ref, grad_out, sums_ref, hold):
+    i = pl.program_id(0)
+    size = CHUNK * LANES
+
+    @pl.when(i == 0)
+    def _():
+        @pl.loop(0, 2 * groups)
+        def _(g):
+            sums_ref[g] = 0.0
+
+    grad = grad_ref[...]
+    w = w_ref[...]
+    first = BETA_ONE * one_ref[...] + (1.0 - BETA_ONE) * grad
+    second = BETA_TWO * two_ref[...] + (1.0 - BETA_TWO) * grad * grad
+    first_ref[...] = first
+    second_ref[...] = second
+    grad_out[...] = grad
+    hold[...] = first / (jnp.sqrt(second) + ADAM_EPS) + DECAY_W * w
+    d = lax.axis_index("dp")
+    start = d * shard + i * size
+    stop = jnp.minimum(start + size, (d + 1) * shard)
+
+    @pl.loop(0, groups)
+    def _(g):
+        low = jnp.maximum(bounds_ref[2 * g], start)
+        high = jnp.minimum(bounds_ref[2 * g + 1], stop)
+
+        @pl.when(low < high)
+        def _():
+            index = start + lax.broadcasted_iota(jnp.int32, (1, size), 1)
+            inside = (index >= low) & (index < high)
+            wv = w_ref[...]
+            rv = hold[...]
+            sums_ref[2 * g] = sums_ref[2 * g] + jnp.sum(jnp.where(inside, wv * wv, 0.0))
+            sums_ref[2 * g + 1] = sums_ref[2 * g + 1] + jnp.sum(jnp.where(inside, rv * rv, 0.0))
+
+
+def moments(bounds, lines, master, one, two):
+    shard = master.shape[1]
+    size = CHUNK * LANES
+    groups = bounds.shape[0] // 2
+    block = pl.BlockSpec((1, size), lambda i: (0, i))
+    ahead = SLACK // CHUNK
+    flat = jax.ShapeDtypeStruct((1, shard), F32)
+    smem = pl.BlockSpec(memory_space=pltpu.SMEM)
+    return pl.pallas_call(
+        functools.partial(moments_kernel, groups, shard),
+        grid=(pl.cdiv(shard, size),),
+        out_shape=(flat, flat, flat, jax.ShapeDtypeStruct((2 * groups,), F32)),
+        in_specs=[smem, pl.BlockSpec((1, size), lambda i: (0, i + ahead)), block, block, block],
+        out_specs=(block, block, block, smem),
+        scratch_shapes=[pltpu.VMEM((1, size), F32)],
+        compiler_params=pltpu.CompilerParams(vmem_limit_bytes=40 << 20),
+        name="moments",
+    )(bounds, lines.reshape(1, -1), master, one, two)
+
+
+def update_kernel(groups, shard, bounds_ref, trust_ref, w_ref, first_ref, second_ref, new_ref, low_ref, hold):
+    i = pl.program_id(0)
+    size = CHUNK * LANES
+    d = lax.axis_index("dp")
+    start = d * shard + i * size
+    hold[...] = jnp.zeros_like(hold)
+
+    @pl.loop(0, groups)
+    def _(g):
+        low = jnp.maximum(bounds_ref[2 * g], start)
+        high = jnp.minimum(bounds_ref[2 * g + 1], start + size)
+
+        @pl.when(low < high)
+        def _():
+            index = start + lax.broadcasted_iota(jnp.int32, (1, size), 1)
+            hold[...] = jnp.where((index >= low) & (index < high), trust_ref[g], hold[...])
+
+    w = w_ref[...]
+    ratio = first_ref[...] / (jnp.sqrt(second_ref[...]) + ADAM_EPS) + DECAY_W * w
+    new = w - LEARN_RATE * hold[...] * ratio
+    new_ref[...] = new
+    low_ref[...] = new.astype(BF)
+
+
+def update(bounds, trust, master, first, second):
+    shard = master.shape[1]
+    size = CHUNK * LANES
+    groups = bounds.shape[0] // 2
+    block = pl.BlockSpec((1, size), lambda i: (0, i))
+    smem = pl.BlockSpec(memory_space=pltpu.SMEM)
+    return pl.pallas_call(
+        functools.partial(update_kernel, groups, shard),
+        grid=(pl.cdiv(shard, size),),
+        out_shape=(jax.ShapeDtypeStruct((1, shard), F32), jax.ShapeDtypeStruct((1, shard), BF)),
+        in_specs=[smem, smem, block, block, block],
+        out_specs=(block, block),
+        scratch_shapes=[pltpu.VMEM((1, size), F32)],
+        compiler_params=pltpu.CompilerParams(vmem_limit_bytes=40 << 20),
+        name="update",
+    )(bounds, trust, master, first, second)
+
+
+def norms_kernel(n, m, own_ref, out_ref, across, along, part, ssem, rsem, ssem2, rsem2):
+    d = lax.axis_index("dp")
+    t = lax.axis_index("tensor")
+    barrier = pltpu.get_barrier_semaphore()
+    for k in range(1, m):
+        pl.semaphore_signal(barrier, inc=1, device_id=(d, lax.rem(t + k, m)), device_id_type=MESH)
+
+    @pl.loop(1, n)
+    def _(k):
+        pl.semaphore_signal(barrier, inc=1, device_id=(lax.rem(d + k, n), t), device_id_type=MESH)
+
+    pl.semaphore_wait(barrier, n + m - 2)
+
+    def over_tensor(k):
+        return pltpu.make_async_remote_copy(
+            src_ref=own_ref,
+            dst_ref=across.at[k - 1],
+            send_sem=ssem.at[k - 1],
+            recv_sem=rsem.at[k - 1],
+            device_id=(d, lax.rem(t + k, m)),
+            device_id_type=MESH,
+        )
+
+    def over_dp(k):
+        return pltpu.make_async_remote_copy(
+            src_ref=part,
+            dst_ref=along.at[k - 1],
+            send_sem=ssem2.at[k - 1],
+            recv_sem=rsem2.at[k - 1],
+            device_id=(lax.rem(d + k, n), t),
+            device_id_type=MESH,
+        )
+
+    for k in range(1, m):
+        over_tensor(k).start()
+    total_ = own_ref[...]
+    for k in range(1, m):
+        over_tensor(k).wait_recv()
+    for k in range(1, m):
+        total_ = total_ + across[k - 1]
+    part[...] = total_
+
+    @pl.loop(1, n)
+    def _(k):
+        over_dp(k).start()
+
+    @pl.loop(1, n)
+    def _(k):
+        over_dp(k).wait_recv()
+
+    def add(k, acc):
+        return acc + along[k - 1]
+
+    out_ref[...] = lax.fori_loop(1, n, add, part[...])
+    for k in range(1, m):
+        over_tensor(k).wait_send()
+
+    @pl.loop(1, n)
+    def _(k):
+        over_dp(k).wait_send()
+
+
+def sum_everywhere(values, n, m):
+    vm = pl.BlockSpec(memory_space=pltpu.VMEM)
+    dma = pltpu.SemaphoreType.DMA
+    tile = pltpu.VMEM((8, LANES), F32)
+    return pl.pallas_call(
+        functools.partial(norms_kernel, n, m),
+        out_shape=jax.ShapeDtypeStruct((8, LANES), F32),
+        in_specs=[vm],
+        out_specs=vm,
+        scratch_shapes=[
+            pltpu.VMEM((m - 1, 8, LANES), F32),
+            pltpu.VMEM((n - 1, 8, LANES), F32),
+            tile,
+            dma((m - 1,)),
+            dma((m - 1,)),
+            dma((n - 1,)),
+            dma((n - 1,)),
+        ],
+        compiler_params=pltpu.CompilerParams(collective_id=2, has_side_effects=True),
+        name="sum_everywhere",
+    )(values)
+
+
+def per_device(n, m, tokens, cotangent, lengths, master, moment_one, moment_two):
     d = lax.axis_index("dp")
     shard = master.shape[1]
     lines = shard // LANES
-    own = master[0].astype(BF)
-    base = d * shard
+    lines3 = master.reshape(lines, 1, LANES)
+    base = d * lines
+    mid = LEAD + FIRST
     small_own = jnp.concatenate(
-        [
-            window(own, -base, GAIN_ROWS * LANES),
-            window(own, (LEAD + FIRST) * LANES - base, SMALL_ROWS * LANES),
-        ]
+        [window(lines3, -base, GAIN_ROWS), window(lines3, mid - base, SMALL_ROWS)]
     )
-    small_flat = lax.psum(small_own, "dp")
-    gains = lax.all_gather(small_flat[: GAIN_ROWS * LANES].reshape(4, DG), "tensor", axis=1, tiled=True)
+    small_flat = lax.psum(small_own.reshape(-1, LANES).astype(BF), "dp")
+    gains = lax.all_gather(small_flat[:GAIN_ROWS].reshape(4, DG), "tensor", axis=1, tiled=True)
     gains = gains.astype(F32)
     small = {}
-    at = GAIN_ROWS * LANES
+    at = GAIN_ROWS
     for name, shape in SMALL:
-        count = math.prod(shape)
+        count = math.prod(shape) // LANES
         small[name] = small_flat[at : at + count].reshape(shape)
         at += count
-    weights = ring_gather(stack_own(own, n), n)
+    weights = ring_gather(stack_own(lines3, n), n)
     w = {}
     for name, rows in BIG:
         w[name] = weights[BIG_OFF[name] : BIG_OFF[name] + rows]
@@ -768,72 +1007,53 @@
     pos = lax.broadcasted_iota(jnp.int32, (tokens.shape[0] // SLOT, SLOT), 1)
     valid = (pos < lengths[:, None]).astype(F32).reshape(-1, 1)
     grad = cotangent.astype(F32) * valid
-    out, grad_in, slab, small_grads = layer(x, grad, w, small, gains, n)
-
-    small_sum = lax.psum(small_grads.astype(BF), "dp").astype(F32)
+    out, grad_in, operands, small_grads = layer(x, grad, w, small, gains, n)
+    small_sum = lax.psum(small_grads, "dp").astype(F32).reshape(-1, 1, LANES)
+    laid = ring_reduce(*operands, n, lines)
+
+    before, after = extents(n, lines)
     slab_lines = BIG_ROWS * LINES // n
-    before, after = extents(n, lines)
-    flat = slab.astype(F32).reshape(-1)
-    tail = lax.ppermute(slab.reshape(-1)[-after * LANES :], "dp", shift_perm(n, 1)).astype(F32)
-    head = lax.ppermute(slab.reshape(-1)[: before * LANES], "dp", shift_perm(n, -1)).astype(F32)
-    pad = jnp.zeros((2 * SMALL_ROWS * LANES,), F32)
-    ext = jnp.concatenate([pad, tail, flat, head, pad])
-    first_at = (2 * SMALL_ROWS + after) * LANES + base - LEAD * LANES - d * slab_lines * LANES
-    limit = ext.shape[0] - shard
-    one = lax.dynamic_slice_in_dim(ext, jnp.clip(first_at, 0, limit), shard, 0)
-    two = lax.dynamic_slice_in_dim(ext, jnp.clip(first_at - SMALL_ROWS * LANES, 0, limit), shard, 0)
-    index = base + jnp.arange(shard, dtype=jnp.int32)
-    mid = (LEAD + FIRST) * LANES
-    end = mid + SMALL_ROWS * LANES
-    grad_shard = jnp.where(index < mid, one, two)
-    grad_shard = jnp.where(
-        index < LEAD * LANES,
-        window(small_sum[: LEAD * LANES], base, shard),
-        jnp.where((index >= mid) & (index < end), window(small_sum[LEAD * LANES :], base - mid, shard), grad_shard),
-    )
-    used = end + (BIG_ROWS * LINES - FIRST) * LANES
-    grad_shard = jnp.where(index < used, grad_shard, 0.0)
-
-    weights_old = master[0]
-    first = BETA_ONE * moment_one[0] + (1.0 - BETA_ONE) * grad_shard
-    second = BETA_TWO * moment_two[0] + (1.0 - BETA_TWO) * grad_shard * grad_shard
-    trust_ratio = first / (jnp.sqrt(second) + ADAM_EPS) + DECAY_W * weights_old
-    bounds = group_bounds()
-    pieces = []
-    for lower_end, upper_end in bounds:
-        within = (index >= lower_end) & (index < upper_end)
-        pieces.append(
-            jnp.stack(
-                [
-                    jnp.sum(jnp.where(within, weights_old * weights_old, 0.0)),
-                    jnp.sum(jnp.where(within, trust_ratio * trust_ratio, 0.0)),
-                ]
-            )
-        )
-    squares = lax.psum(jnp.stack(pieces), ("dp", "tensor"))
-    trust_factor = jnp.sqrt(squares[:, 0] + TRUST_EPSILON) * lax.rsqrt(squares[:, 1] + TRUST_EPSILON)
-    column_trust = jnp.zeros((shard,), F32)
-    for g, (lower_end, upper_end) in enumerate(bounds):
-        within = (index >= lower_end) & (index < upper_end)
-        column_trust = jnp.where(within, trust_factor[g], column_trust)
-    master_new = weights_old - LEARN_RATE * column_trust * trust_ratio
-    return (
-        out,
-        grad_in,
-        master_new[None, :],
-        first[None, :],
-        second[None, :],
-        master_new.astype(BF)[None, :],
-        grad_shard[None, :],
-        jnp.sqrt(squares),
-    )
+
+    def local(row):
+        return row * LINES + LEAD + jnp.where(row >= FIRST // LINES, SMALL_ROWS, 0) - base
+
+    begin = local(d * (BIG_ROWS // n))
+    close = local((d + 1) * (BIG_ROWS // n) - 1) + LINES
+    from_prev = lax.ppermute(laid[SLACK + lines : SLACK + lines + after], "dp", shift_perm(n, 1))
+    from_next = lax.ppermute(laid[SLACK - before : SLACK], "dp", shift_perm(n, -1))
+    line = lax.broadcasted_iota(jnp.int32, (after, 1, 1), 0)
+    top = jnp.where(line < begin, from_prev, laid[SLACK : SLACK + after])
+    line = lax.broadcasted_iota(jnp.int32, (before, 1, 1), 0) + (lines - before)
+    bottom = jnp.where(line >= close, from_next, laid[SLACK + lines - before : SLACK + lines])
+    laid = laid.at[SLACK : SLACK + after].set(top)
+    laid = laid.at[SLACK + lines - before : SLACK + lines].set(bottom)
+
+    def place(laid, values, at):
+        count = values.shape[0]
+        return lax.dynamic_update_slice_in_dim(laid, values, SLACK + jnp.clip(at - base, -count, lines), 0)
+
+    laid = place(laid, small_sum[GAIN_ROWS:], mid)
+    laid = place(laid, small_sum[:GAIN_ROWS], 0)
+    used = LEAD + SMALL_ROWS + BIG_ROWS * LINES
+    rest = lines * n - used
+    if rest:
+        laid = place(laid, jnp.zeros((rest, 1, LANES), F32), used)
+
+    bounds = jnp.asarray([v for pair in group_bounds() for v in pair], jnp.int32)
+    first, second, grad_shard, sums = moments(bounds, laid, master, moment_one, moment_two)
+    count = sums.shape[0]
+    tile = jnp.pad(sums, (0, 8 * LANES - count)).reshape(8, LANES)
+    squares = sum_everywhere(tile, n, m).reshape(-1)[:count].reshape(-1, 2)
+    trust = jnp.sqrt(squares[:, 0] + TRUST_EPSILON) * lax.rsqrt(squares[:, 1] + TRUST_EPSILON)
+    master_new, low = update(bounds, trust, master, first, second)
+    return (out, grad_in, master_new, first, second, low, grad_shard, jnp.sqrt(squares))
 
 
 def solution(mesh):
     row = P("dp", None)
     flat = P("tensor", "dp")
     return jax.shard_map(
-        functools.partial(per_device, mesh.shape["dp"]),
+        functools.partial(per_device, mesh.shape["dp"], mesh.shape["tensor"]),
         mesh=mesh,
         in_specs=(row, row, P("dp"), flat, flat, flat),
         out_specs=(row, row, flat, flat, flat, flat, flat, P()),

time: 2540 us -> 1940 us (0.76)
  other arithmetic: 646 us -> 192 us
  local copies, waits for them, and re-layouts: 519 us -> 112 us
  Pallas kernels: 941 us -> 1100 us
  waiting for transfers between devices: 248 us -> 395 us
  blocking collectives: 47 us -> 5.67 us
    broadcast_in_dim x9 -> x2, local copies, waits for them, and re-layouts: 261 us -> 0.25 us  [window(): room = jnp.zeros((3 * size,) + values.shape[1:], values.dtype)]
    pallas_call x1 -> x5, Pallas kernels: 446 us -> 614 us  [the longest x1 447 us: ring_reduce(): pl.pallas_call(functools.partial(reduce_kernel, n, shard_lines), out_shap...]
    reduce_sum x2 -> x0, other arithmetic: 131 us -> none  [the longest x1 91.3 us: per_device(): jnp.sum(jnp.where(within, trust_ratio * trust_ratio, 0.0))]
    mul x1 -> x0, other arithmetic: 126 us -> none  [per_device(): BETA_TWO * moment_two[0] + (1.0 - BETA_TWO) * grad_shard * grad_shard]
    unnamed x20 -> x13, other arithmetic: 251 us -> 131 us
    psum x7, waiting for transfers between devices: 120 us -> 211 us  [total(): return lax.psum(partial_out.astype(BF), 'tensor').astype(F32)]
    unnamed x240 -> x151, local copies, waits for them, and re-layouts: 127 us -> 38.9 us
    psum x2, waiting for transfers between devices: 67.9 us -> 125 us  [the longest x1 68.6 us: per_device(): small_flat = lax.psum(small_own.reshape(-1, LANES).astype(BF), 'dp')]
  transfers between devices with their start and end apart: 15 -> 15, of which waited for: 8 -> 11; matrix products, arithmetic and copies ran while one was open for 21% -> 5% of each run, Pallas kernels for 18% -> 0%
where the time goes in v2:
time: 1940 us; the launch traced here: 1930 us
  Pallas kernels  1100 us (57%)
  waiting for transfers between devices  395 us (20%)
  other arithmetic  192 us (10%)
  local copies, waits for them, and re-layouts  112 us (6%)
  matrix products  92.2 us (5%)
    pallas_call x1, Pallas kernels, ring_reduce(): pl.pallas_call(functools.partial(reduce_kernel, n, shard_lines), out_shap...  447 us
    pallas_call x1, Pallas kernels, ring_gather(): pl.pallas_call(functools.partial(gather_kernel, n, subs), out_shape=jax.S...  438 us
    psum x7, waiting for transfers between devices, total(): return lax.psum(partial_out.astype(BF), 'tensor').astype(F32)  211 us
    unnamed x13, other arithmetic  131 us
    pallas_call x1, Pallas kernels, moments(): pl.pallas_call(functools.partial(moments_kernel, groups, shard), grid=(pl...  93 us
    psum x1, waiting for transfers between devices, per_device(): small_flat = lax.psum(small_own.reshape(-1, LANES).astype(BF), 'dp')  68.6 us
    pallas_call x1, Pallas kernels, update(): pl.pallas_call(functools.partial(update_kernel, groups, shard), grid=(pl....  57.5 us
    psum x1, waiting for transfers between devices, per_device(): small_sum = lax.psum(small_grads, 'dp').astype(F32).reshape(-1, 1, LANES)  56.6 us
  transfers between devices with their start and end apart: 15, of which 11 were waited for; matrix products, arithmetic and copies ran while one was open for 5% of the time, Pallas kernels for 0%

profile of v2, /device:TPU:2, one launch (start us, length us, event | category | flops | bytes accessed | tf_op | source)
XLA Modules:
  0.0 1929.6 jit_solution(2946125187333958361)
XLA Ops:
  7.2 113.9 %reduce.4 = bf16[2923648]{0:T(1024)(128)(2,1)} reduce(f32[1,2923648]{1,0:T(1,128)} %w_ref.3, f32[]{:T(128)} %constant.167), dimensions={0}, to_apply=%param.14.reduce_sub_computation | reduce | bytes 17541892 | tf_op args[3]
  138.7 68.6 %all-reduce.20.cloned.1.call-done = bf16[2504,128]{1,0:T(8,128)(2,1)} async-done(((bf16[2504,128]{1,0:T(8,128)(2,1)}), bf16[2504,128]{1,0:T(8,128)(2,1)}) %all-reduce.20.cloned.1.call-update) | async-done | bytes 641040 | tf_op jit(solution)/shard_map/psum | solution.py:992
  234.1 437.8 %ring_gather.1 = bf16[11264,2048]{1,0:T(8,128)(2,1)} custom-call(bf16[1408,2048]{1,0:T(8,128)(2,1)S(1)} %stack_own.1.own_ref), custom_call_target="tpu_custom_call" | custom-call | flops 1000000000 | bytes 1500000000 | tf_op jit(solution)/shard_map/ring_gather/pallas_call | solution.py:191
  684.6 29.7 %all-reduce.22.cloned.1.call-done = bf16[256,160]{1,0:T(8,128)(2,1)} async-done(((bf16[256,160]{1,0:T(8,128)(2,1)}), bf16[256,160]{1,0:T(8,128)(2,1)}) %all-reduce.22.cloned.1.call-update) | async-done | bytes 81936 | tf_op jit(solution)/shard_map/psum | solution.py:623
  717.4 11.3 scan_forward.1
  735.5 34.1 %all-reduce.24.cloned.1.call-done = bf16[256,2048]{1,0:T(8,128)(2,1)} async-done(((bf16[256,2048]{1,0:T(8,128)(2,1)}), bf16[256,2048]{1,0:T(8,128)(2,1)}) %all-reduce.24.cloned.1.call-update) | async-done | bytes 1048592 | tf_op jit(solution)/shard_map/psum | solution.py:566
  791.3 11.1 reshape.431
  802.4 8.6 copy.70
  811.0 10.3 all-reduce.26.cloned.1.call-done
  835.1 36.6 %all-reduce.28.cloned.1.call-done = bf16[256,2048]{1,0:T(8,128)(2,1)} async-done(((bf16[256,2048]{1,0:T(8,128)(2,1)}), bf16[256,2048]{1,0:T(8,128)(2,1)}) %all-reduce.28.cloned.1.call-update) | async-done | bytes 1048592 | tf_op jit(solution)/shard_map/psum | solution.py:566
  895.3 34.5 %all-reduce.30.cloned.1.call-done = bf16[256,2048]{1,0:T(8,128)(2,1)} async-done(((bf16[256,2048]{1,0:T(8,128)(2,1)}), bf16[256,2048]{1,0:T(8,128)(2,1)}) %all-reduce.30.cloned.1.call-update) | async-done | bytes 1048592 | tf_op jit(solution)/shard_map/psum | solution.py:566
  956.6 32.3 %all-reduce.32.cloned.1.call-done = bf16[256,2048]{1,0:T(8,128)(2,1)} async-done(((bf16[256,2048]{1,0:T(8,128)(2,1)}), bf16[256,2048]{1,0:T(8,128)(2,1)}) %all-reduce.32.cloned.1.call-update) | async-done | bytes 1048592 | tf_op jit(solution)/shard_map/psum | solution.py:566
  1015.9 11.1 reshape.434.qkv_ref
  1027.0 16.4 all-reduce.34.cloned.1.call-done
  1052.4 40.8 %scan_backward.1 = (bf16[256,1024]{1,0:T(8,128)(2,1)}, f32[256,1024]{1,0:T(8,128)}, bf16[256,256]{1,0:T(8,128)(2,1)}, f32[128,1024]{1,0:T(8,128)}, f32[1,1024]{1...) custom-call(bf16[256,128]{1,0:T(8,128)(2,1)} %slice.368.proj_ref, f32[256,32]{1,0:T(8,128)} %slice_convert_fusion.2.bc_ref, ...), custom_call_target="tpu_custom_call" | custom-call | tf_op jit(solution)/shard_map/scan_backward/pallas_call | solution.py:514
  1096.7 28.9 %all-reduce.36.cloned.1.call-done = bf16[256,160]{1,0:T(8,128)(2,1)} async-done(((bf16[256,160]{1,0:T(8,128)(2,1)}), bf16[256,160]{1,0:T(8,128)(2,1)}) %all-reduce.36.cloned.1.call-update) | async-done | bytes 81936 | tf_op jit(solution)/shard_map/psum | solution.py:681
  1148.9 46.3 %all-reduce.40.cloned.1.call-done = (bf16[256,2048]{1,0:T(8,128)(2,1)}, bf16[256,2048]{1,0:T(8,128)(2,1)}) async-done(((bf16[256,2048]{1,0:T(8,128)(2,1)}, bf16[256,2048]{1,0:T(8,128)(2,1)}), (bf16[256,2048]{1,0:T(8,128)(2,1)}, bf16[256,2048]{1,0:T(8,128)(2,1)})) %all-reduce.40.cloned.1.call-update) | async-done | bytes 2097168 | tf_op jit(solution)/shard_map/psum | solution.py:566
  1206.9 446.7 %ring_reduce.1 = f32[28985,1,128]{2,1,0:T(1,128)} custom-call(bf16[9728,256]{1,0:T(8,128)(2,1)} %copy.83.left_ref, bf16[7,256,2048]{2,1,0:T(8,128)(2,1)} %bitcast_dynamic-update-slice_fusion.right_refs, bf16[1536,2048]{1,0:T(8,128)(2,1)} %reshape.434.qkv_ref), custom_call_target="tpu_custom_call" | custom-call | flops 1000000000 | bytes 1500000000 | tf_op jit(solution)/shard_map/ring_reduce/pallas_call | solution.py:312
  1661.6 12.5 copy.139
  1679.5 56.6 %all-reduce.38.cloned.1.call-done = bf16[2504,128]{1,0:T(8,128)(2,1)} async-done(((bf16[2504,128]{1,0:T(8,128)(2,1)}), bf16[2504,128]{1,0:T(8,128)(2,1)}) %all-reduce.38.cloned.1.call-update) | async-done | bytes 641040 | tf_op jit(solution)/shard_map/psum | solution.py:1011
  1737.9 8.0 fusion.99
  1754.5 93.0 %moments.1 = (f32[1,2923648]{1,0:T(1,128)}, f32[1,2923648]{1,0:T(1,128)}, f32[1,2923648]{1,0:T(1,128)}, f32[38]{0:T(128)S(1)}) custom-call(s32[38]{0:T(128)S(1)} %copy-done.3, f32[1,3710080]{1,0:T(1,128)} %bitcast.146, f32[1,2923648]{1,0:T(1,128)S(1)} %copy-done.1, f32[1,2923648]{1,0:T(1,128)} %one_ref.1, f32[1,2923648]{1,0:T(1,128)} %two_ref.1), custom_call_target="tpu_custom_call" | custom-call | tf_op jit(solution)/shard_map/moments/pallas_call | solution.py:843
  1848.2 10.9 sum_everywhere.1
  1865.2 57.5 %update.1 = (f32[1,2923648]{1,0:T(1,128)}, bf16[1,2923648]{1,0:T(2,128)(2,1)}) custom-call(s32[38]{0:T(128)S(1)} %copy-done.3, f32[19]{0:T(128)S(1)} %fusion.124.trust_ref, f32[1,2923648]{1,0:T(1,128)S(1)} %copy-done.2, f32[1,2923648]{1,0:T(1,128)} %get-tuple-element.81.first_ref, f32[1,2923648]{1,0:T(1,128)} %get-tuple-element.82.second_ref), custom_call_target="tpu_custom_call" | custom-call | tf_op jit(solution)/shard_map/update/pallas_call | solution.py:885
  (321 shorter events, 256.6 us)
Async XLA Ops:
  7.2 200.1 %all-reduce.20.cloned.1.call-start = ((), (), s32[]{:S(2)}) async-start(), calls=%async_computation | async-start | bytes 1282048 | tf_op jit(solution)/shard_map/psum | solution.py:992
  125.9 588.5 %all-reduce.22.cloned.1.call-start = ((), (), s32[]{:S(2)}) async-start(), calls=%async_computation.1 | async-start | bytes 262144 | tf_op jit(solution)/shard_map/psum | solution.py:623
  126.9 9.5 collective-permute-start
  132.9 84.3 %collective-permute-start.1 = (f32[1878,1,128]{2,1,0:T(1,128)}, f32[1878,1,128]{2,1,0:T(1,128)}, u32[]{:S(2)}, u32[]{:S(2)}) collective-permute-start(f32[1878,1,128]{2,1,0:T(1,128)} %slice_bitcast_fusion), channel_id=1, source_target_pairs={{4,0},{8,4},{12,8},{16,12},{20,16},{24,20},{28,24},{5,1},{9,5},{13... | collective-permute-start | bytes 2884616 | tf_op jit(solution)/shard_map/ppermute | solution.py:771
  136.4 1058.9 %copy-start.62 = (f32[256]{0:T(256)}, f32[256]{0:T(256)S(1)}, u32[]{:S(2)}) copy-start(f32[256]{0:T(256)S(1)} %add_rsqrt_fusion.3) | copy-start | bytes 3076
  217.2 978.1 %copy-start.58 = (f32[1,2048]{1,0:T(1,128)}, f32[1,2048]{1,0:T(1,128)S(1)}, u32[]{:S(2)}) copy-start(f32[1,2048]{1,0:T(1,128)S(1)} %get-tuple-element.140) | copy-start | bytes 24580
  682.0 35.3 %copy-start.16 = (bf16[2,128,1024]{2,1,0:T(8,128)(2,1)}, bf16[2,128,1024]{2,1,0:T(8,128)(2,1)S(1)}, u32[]{:S(2)}) copy-start(bf16[2,128,1024]{2,1,0:T(8,128)(2,1)S(1)} %get-tuple-element.110) | copy-start | bytes 1572868
  683.1 86.5 %all-reduce.24.cloned.1.call-start = ((), (), s32[]{:S(2)}) async-start(), calls=%async_computation.2 | async-start | bytes 2097152 | tf_op jit(solution)/shard_map/psum | solution.py:566
  733.2 88.1 %all-reduce.26.cloned.1.call-start = ((), (), s32[]{:S(2)}) async-start(), calls=%async_computation.3 | async-start | bytes 2097152 | tf_op jit(solution)/shard_map/psum | solution.py:566
  784.4 87.3 %all-reduce.28.cloned.1.call-start = ((), (), s32[]{:S(2)}) async-start(), calls=%async_computation.4 | async-start | bytes 2097152 | tf_op jit(solution)/shard_map/psum | solution.py:566
  834.7 95.1 %all-reduce.30.cloned.1.call-start = ((), (), s32[]{:S(2)}) async-start(), calls=%async_computation.5 | async-start | bytes 2097152 | tf_op jit(solution)/shard_map/psum | solution.py:566
  892.9 96.0 %all-reduce.32.cloned.1.call-start = ((), (), s32[]{:S(2)}) async-start(), calls=%async_computation.6 | async-start | bytes 2097152 | tf_op jit(solution)/shard_map/psum | solution.py:566
  952.0 91.4 %all-reduce.34.cloned.1.call-start = ((), (), s32[]{:S(2)}) async-start(), calls=%async_computation.7 | async-start | bytes 2097152 | tf_op jit(solution)/shard_map/psum | solution.py:566
  1006.5 119.1 %all-reduce.36.cloned.1.call-start = ((), (), s32[]{:S(2)}) async-start(), calls=%async_computation.8 | async-start | bytes 262144 | tf_op jit(solution)/shard_map/psum | solution.py:681
  1052.4 73.2 %copy-start.24 = (f32[256,1024]{1,0:T(8,128)S(1)}, f32[256,1024]{1,0:T(8,128)}, u32[]{:S(2)}) copy-start(f32[256,1024]{1,0:T(8,128)} %copy-done.23) | copy-start | bytes 3145732
  1093.2 102.1 %all-reduce.40.cloned.1.call-start = ((), (), s32[]{:S(2)}) async-start(), calls=%async_computation.10 | async-start | bytes 4194304 | tf_op jit(solution)/shard_map/psum | solution.py:566
  1143.7 592.4 %all-reduce.38.cloned.1.call-start = ((), (), s32[]{:S(2)}) async-start(), calls=%async_computation.9 | async-start | bytes 1282048 | tf_op jit(solution)/shard_map/psum | solution.py:1011
  1147.7 50.4 %copy-start.61 = (f32[128,128]{1,0:T(8,128)S(1)}, f32[128,128]{1,0:T(8,128)}, u32[]{:S(2)}) copy-start(f32[128,128]{1,0:T(8,128)} %get-tuple-element.52) | copy-start | bytes 196612
  1147.7 50.4 %copy-start.38 = (bf16[1024,128]{1,0:T(8,128)(2,1)S(1)}, bf16[1024,128]{1,0:T(8,128)(2,1)}, u32[]{:S(2)}) copy-start(bf16[1024,128]{1,0:T(8,128)(2,1)} %convert_element_type.350) | copy-start | bytes 786436
  1654.9 83.0 %collective-permute-start.2 = (f32[1878,1,128]{2,1,0:T(1,128)S(1)}, f32[1878,1,128]{2,1,0:T(1,128)S(1)}, u32[]{:S(2)}, u32[]{:S(2)}) collective-permute-start(f32[1878,1,128]{2,1,0:T(1,128)S(1)} %slice.344), channel_id=1, source_target_pairs={{0,4},{4,8},{8,12},{12,16},{16,20},{20,24},{24,28},{1,5},{5,9},{9,... | collective-permute-start | bytes 2884616 | tf_op jit(solution)/shard_map/ppermute | solution.py:1022
  1661.5 16.0 copy-start.5
  1675.0 71.0 %collective-permute-start.3 = (f32[297,1,128]{2,1,0:T(1,128)S(1)}, f32[297,1,128]{2,1,0:T(1,128)S(1)}, u32[]{:S(2)}, u32[]{:S(2)}) collective-permute-start(f32[297,1,128]{2,1,0:T(1,128)S(1)} %slice.346), channel_id=1, source_target_pairs={{4,0},{8,4},{12,8},{16,12},{20,16},{24,20},{28,24},{5,1},{9,5},{13... | collective-permute-start | bytes 456200 | tf_op jit(solution)/shard_map/ppermute | solution.py:1023
  1679.5 58.4 %copy-start.64 = (pred[1878]{0:T(1024)(128)(4,1)S(1)}, pred[1878]{0:T(1024)(128)(4,1)}, u32[]{:S(2)}) copy-start(pred[1878]{0:T(1024)(128)(4,1)} %iota_compare_fusion) | copy-start | bytes 5638
  1679.5 66.5 %copy-start.66 = (pred[297]{0:T(512)(128)(4,1)S(1)}, pred[297]{0:T(512)(128)(4,1)}, u32[]{:S(2)}) copy-start(pred[297]{0:T(512)(128)(4,1)} %add_compare_fusion) | copy-start | bytes 895
  (62 other events, 235.5 us)
Sparse Core Ops, SparseCore 0:
  126.0 81.2 all-reduce.19
  683.3 31.0 all-reduce.21
  733.3 36.2 all-reduce.23
  784.6 36.7 all-reduce.25
  834.8 36.8 all-reduce.27
  893.0 36.7 all-reduce.29
  952.1 36.7 all-reduce.31
  1006.6 36.7 all-reduce.33
  1093.3 32.2 all-reduce.35
  1143.8 51.3 all-reduce.39
  1661.6 74.4 all-reduce.37

commit v3 on v2

--- a/solution.py
+++ b/solution.py
@@ -329,6 +329,172 @@
     )(left_t, rights, qkv_grad)
 
 
+def pair_kernel(parts, x_ref, out_ref, from_mate, chip, from_far, s1, r1, s2, r2, s3, r3):
+    d = lax.axis_index("dp")
+    t = lax.axis_index("tensor")
+    core = lax.rem(t, 2)
+    mate = t + 1 - 2 * core
+    far = lax.rem(t + 2, 4)
+    half = x_ref.shape[0] // 2
+    q = half // parts
+    barrier = pltpu.get_barrier_semaphore()
+    for peer in (mate, far):
+        pl.semaphore_signal(barrier, inc=1, device_id=(d, peer), device_id_type=MESH)
+    pl.semaphore_wait(barrier, 2)
+
+    def mine(k):
+        return pl.ds(pl.multiple_of(core * half + k * q, 16), q)
+
+    def theirs(k):
+        return pl.ds(pl.multiple_of((1 - core) * half + k * q, 16), q)
+
+    def send(src, dst, ssem, rsem, k, peer):
+        return pltpu.make_async_remote_copy(
+            src_ref=src,
+            dst_ref=dst,
+            send_sem=ssem.at[k],
+            recv_sem=rsem.at[k],
+            device_id=(d, peer),
+            device_id_type=MESH,
+        )
+
+    def one(k):
+        here = pl.ds(k * q, q)
+        return send(x_ref.at[theirs(k)], from_mate.at[here], s1, r1, k, mate)
+
+    def two(k):
+        here = pl.ds(k * q, q)
+        return send(chip.at[here], from_far.at[here], s2, r2, k, far)
+
+    def three(k):
+        return send(out_ref.at[mine(k)], out_ref.at[mine(k)], s3, r3, k, mate)
+
+    for k in range(parts):
+        one(k).start()
+    for k in range(parts):
+        here = slice(k * q, (k + 1) * q)
+        one(k).wait_recv()
+        chip[here, :] = (x_ref[mine(k), :].astype(F32) + from_mate[here, :].astype(F32)).astype(BF)
+        two(k).start()
+    for k in range(parts):
+        here = slice(k * q, (k + 1) * q)
+        two(k).wait_recv()
+        out_ref[mine(k), :] = (chip[here, :].astype(F32) + from_far[here, :].astype(F32)).astype(BF)
+        three(k).start()
+    for k in range(parts):
+        three(k).wait_recv()
+    for k in range(parts):
+        one(k).wait_send()
+        two(k).wait_send()
+        three(k).wait_send()
+
+
+def sum_tensor(value):
+    rows, cols = value.shape
+    parts = 4 if cols >= 1024 else 1
+    vm = pl.BlockSpec(memory_space=pltpu.VMEM)
+    dma = pltpu.SemaphoreType.DMA
+    part = pltpu.VMEM((rows // 2, cols), BF)
+    return pl.pallas_call(
+        functools.partial(pair_kernel, parts),
+        out_shape=jax.ShapeDtypeStruct((rows, cols), BF),
+        in_specs=[vm],
+        out_specs=vm,
+        scratch_shapes=[part, part, part] + [dma((parts,))] * 6,
+        compiler_params=pltpu.CompilerParams(
+            collective_id=3 if cols >= 1024 else 4, has_side_effects=True
+        ),
+        name="sum_tensor",
+    )(value)
+
+
+def sum_proj(value):
+    cols = value.shape[1]
+    padded = jnp.pad(value, ((0, 0), (0, -cols % LANES)))
+    return sum_tensor(padded)[:, :cols]
+
+
+def spread_kernel(n, x_ref, out_ref, got, s1, r1, s2, r2):
+    d = lax.axis_index("dp")
+    t = lax.axis_index("tensor")
+    q = x_ref.shape[0] // n
+    barrier = pltpu.get_barrier_semaphore()
+
+    def peer(k):
+        return lax.rem(d + k, n)
+
+    @pl.loop(1, n)
+    def _(k):
+        pl.semaphore_signal(barrier, inc=1, device_id=(peer(k), t), device_id_type=MESH)
+
+    pl.semaphore_wait(barrier, n - 1)
+
+    def rows(e):
+        return pl.ds(pl.multiple_of(e * q, 16), q)
+
+    def one(k):
+        return pltpu.make_async_remote_copy(
+            src_ref=x_ref.at[rows(peer(k))],
+            dst_ref=got.at[k - 1],
+            send_sem=s1.at[k - 1],
+            recv_sem=r1.at[k - 1],
+            device_id=(peer(k), t),
+            device_id_type=MESH,
+        )
+
+    def two(k):
+        return pltpu.make_async_remote_copy(
+            src_ref=out_ref.at[rows(d)],
+            dst_ref=out_ref.at[rows(d)],
+            send_sem=s2.at[k - 1],
+            recv_sem=r2.at[k - 1],
+            device_id=(peer(k), t),
+            device_id_type=MESH,
+        )
+
+    @pl.loop(1, n)
+    def _(k):
+        one(k).start()
+
+    @pl.loop(1, n)
+    def _(k):
+        one(k).wait_recv()
+
+    def add(k, acc):
+        return acc + got[k - 1].astype(F32)
+
+    out_ref[rows(d), :] = lax.fori_loop(1, n, add, x_ref[rows(d), :].astype(F32)).astype(BF)
+
+    @pl.loop(1, n)
+    def _(k):
+        two(k).start()
+
+    @pl.loop(1, n)
+    def _(k):
+        two(k).wait_recv()
+
+    @pl.loop(1, n)
+    def _(k):
+        one(k).wait_send()
+        two(k).wait_send()
+
+
+def sum_dp(value, n):
+    count = value.shape[0]
+    padded = jnp.pad(value, ((0, -count % (16 * n)), (0, 0)))
+    vm = pl.BlockSpec(memory_space=pltpu.VMEM)
+    dma = pltpu.SemaphoreType.DMA((n - 1,))
+    return pl.pallas_call(
+        functools.partial(spread_kernel, n),
+        out_shape=jax.ShapeDtypeStruct(padded.shape, BF),
+        in_specs=[vm],
+        out_specs=vm,
+        scratch_shapes=[pltpu.VMEM((n - 1, padded.shape[0] // n, LANES), BF), dma, dma, dma, dma],
+        compiler_params=pltpu.CompilerParams(collective_id=5, has_side_effects=True),
+        name="sum_dp",
+    )(padded)[:count]
+
+
 def spread(ref, value):
     rows = value.shape[0]
     for j in range(EI // LANES):
@@ -563,7 +729,7 @@
 
 
 def total(partial_out):
-    return lax.psum(partial_out.astype(BF), "tensor").astype(F32)
+    return sum_tensor(partial_out.astype(BF)).astype(F32)
 
 
 def shift_down(v, by):
@@ -620,7 +786,7 @@
     for j in range(CONV):
         pre_conv = pre_conv + conv_w[j] * shift_down(mix_x, CONV - 1 - j)
     unit = silu(pre_conv).astype(BF).reshape(rows, EI)
-    proj = lax.psum(mat_nn(unit, small["w_x"]).astype(BF), "tensor")
+    proj = sum_proj(mat_nn(unit, small["w_x"]).astype(BF))
     bc = proj[:, DTR:].astype(F32)
     scan_args = (
         proj[:, :DTR],
@@ -678,7 +844,7 @@
     gb1 = g1.astype(BF)
     ggated = mat_nt(gb1, w["w_out"])
     gz, gunit, gproj, g_dt, g_bias, g_skip, g_alog = scan_backward(*scan_args, ggated)
-    gproj = lax.psum(gproj[:, : DTR + 2 * NSTATE], "tensor")
+    gproj = sum_tensor(gproj)[:, : DTR + 2 * NSTATE]
     g_wx = mat_tn(unit, gproj)
     gu = gunit + mat_nt(gproj, small["w_x"])
     sig = jax.nn.sigmoid(pre_conv)
@@ -699,8 +865,9 @@
     g_gain = lax.dynamic_slice_in_dim(jnp.stack([gg1, gg2, gg3, gg4]), start, DG, 1)
     pieces = [g_gain, g_conv_w, g_conv_b, g_bias, g_skip, g_alog, g_wx, g_dt]
     small_grads = jnp.concatenate([p.reshape(-1, LANES).astype(BF) for p in pieces])
-    small_grads, left_t = lax.optimization_barrier((small_grads, left_t))
-    return x4.astype(BF), g0, (left_t, rights, g_qkv), small_grads
+    small_sum = sum_dp(small_grads, n)
+    g0, small_sum, left_t = lax.optimization_barrier((g0, small_sum, left_t))
+    return x4.astype(BF), g0, (left_t, rights, g_qkv), small_sum
 
 
 def extents(n, shard_rows):
@@ -794,10 +961,22 @@
     return room[size : 2 * size]
 
 
+STRIP = 8192
+
+
+def lone_group(groups, bounds_ref, start, stop):
+    def look(g, found):
+        holds = jnp.logical_and(bounds_ref[2 * g] <= start, bounds_ref[2 * g + 1] >= stop)
+        return jnp.where(holds, g, found)
+
+    return lax.fori_loop(0, groups, look, jnp.int32(-1))
+
+
 def moments_kernel(groups, shard, bounds_ref, grad_ref, w_ref, one_ref, two_ref,
                    first_ref, second_ref, grad_out, sums_ref, hold):
     i = pl.program_id(0)
     size = CHUNK * LANES
+    lanes = STRIP // 8
 
     @pl.when(i == 0)
     def _():
@@ -805,31 +984,63 @@
         def _(g):
             sums_ref[g] = 0.0
 
-    grad = grad_ref[...]
-    w = w_ref[...]
-    first = BETA_ONE * one_ref[...] + (1.0 - BETA_ONE) * grad
-    second = BETA_TWO * two_ref[...] + (1.0 - BETA_TWO) * grad * grad
-    first_ref[...] = first
-    second_ref[...] = second
-    grad_out[...] = grad
-    hold[...] = first / (jnp.sqrt(second) + ADAM_EPS) + DECAY_W * w
+    def strip(k, carry):
+        here = pl.ds(pl.multiple_of(k * STRIP, STRIP), STRIP)
+        grad = grad_ref[:, here]
+        w = w_ref[:, here]
+        first = BETA_ONE * one_ref[:, here] + (1.0 - BETA_ONE) * grad
+        second = BETA_TWO * two_ref[:, here] + (1.0 - BETA_TWO) * grad * grad
+        ratio = first / (jnp.sqrt(second) + ADAM_EPS) + DECAY_W * w
+        first_ref[:, here] = first
+        second_ref[:, here] = second
+        grad_out[:, here] = grad
+        hold[:, here] = ratio
+        wsq, rsq = carry
+        for j in range(8):
+            part = slice(j * lanes, (j + 1) * lanes)
+            wsq = wsq + w[:, part] * w[:, part]
+            rsq = rsq + ratio[:, part] * ratio[:, part]
+        return wsq, rsq
+
+    zero = jnp.zeros((1, lanes), F32)
+    wsq, rsq = lax.fori_loop(0, size // STRIP, strip, (zero, zero))
     d = lax.axis_index("dp")
     start = d * shard + i * size
-    stop = jnp.minimum(start + size, (d + 1) * shard)
-
-    @pl.loop(0, groups)
-    def _(g):
-        low = jnp.maximum(bounds_ref[2 * g], start)
-        high = jnp.minimum(bounds_ref[2 * g + 1], stop)
-
-        @pl.when(low < high)
-        def _():
-            index = start + lax.broadcasted_iota(jnp.int32, (1, size), 1)
-            inside = (index >= low) & (index < high)
-            wv = w_ref[...]
-            rv = hold[...]
-            sums_ref[2 * g] = sums_ref[2 * g] + jnp.sum(jnp.where(inside, wv * wv, 0.0))
-            sums_ref[2 * g + 1] = sums_ref[2 * g + 1] + jnp.sum(jnp.where(inside, rv * rv, 0.0))
+    limit = (d + 1) * shard
+    alone = lone_group(groups, bounds_ref, start, start + size)
+    alone = jnp.where(start + size <= limit, alone, -1)
+
+    @pl.when(alone >= 0)
+    def _():
+        sums_ref[2 * alone] = sums_ref[2 * alone] + jnp.sum(wsq)
+        sums_ref[2 * alone + 1] = sums_ref[2 * alone + 1] + jnp.sum(rsq)
+
+    @pl.when(alone < 0)
+    def _():
+        @pl.loop(0, groups)
+        def _(g):
+            low = jnp.maximum(bounds_ref[2 * g], start)
+            high = jnp.minimum(bounds_ref[2 * g + 1], jnp.minimum(start + size, limit))
+
+            @pl.when(low < high)
+            def _():
+                def masked(k, carry):
+                    at = pl.multiple_of(k * lanes, lanes)
+                    here = pl.ds(at, lanes)
+                    index = start + at + lax.broadcasted_iota(jnp.int32, (1, lanes), 1)
+                    inside = (index >= low) & (index < high)
+                    wv = w_ref[:, here]
+                    rv = hold[:, here]
+                    return (
+                        carry[0] + jnp.where(inside, wv * wv, 0.0),
+                        carry[1] + jnp.where(inside, rv * rv, 0.0),
+                    )
+
+                k0 = (low - start) // lanes
+                k1 = (high - start + lanes - 1) // lanes
+                wv, rv = lax.fori_loop(k0, k1, masked, (zero, zero))
+                sums_ref[2 * g] = sums_ref[2 * g] + jnp.sum(wv)
+                sums_ref[2 * g + 1] = sums_ref[2 * g + 1] + jnp.sum(rv)
 
 
 def moments(bounds, lines, master, one, two):
@@ -855,25 +1066,44 @@
 def update_kernel(groups, shard, bounds_ref, trust_ref, w_ref, first_ref, second_ref, new_ref, low_ref, hold):
     i = pl.program_id(0)
     size = CHUNK * LANES
-    d = lax.axis_index("dp")
-    start = d * shard + i * size
-    hold[...] = jnp.zeros_like(hold)
-
-    @pl.loop(0, groups)
-    def _(g):
-        low = jnp.maximum(bounds_ref[2 * g], start)
-        high = jnp.minimum(bounds_ref[2 * g + 1], start + size)
-
-        @pl.when(low < high)
-        def _():
-            index = start + lax.broadcasted_iota(jnp.int32, (1, size), 1)
-            hold[...] = jnp.where((index >= low) & (index < high), trust_ref[g], hold[...])
-
-    w = w_ref[...]
-    ratio = first_ref[...] / (jnp.sqrt(second_ref[...]) + ADAM_EPS) + DECAY_W * w
-    new = w - LEARN_RATE * hold[...] * ratio
-    new_ref[...] = new
-    low_ref[...] = new.astype(BF)
+    lanes = STRIP // 8
+    start = lax.axis_index("dp") * shard + i * size
+    alone = lone_group(groups, bounds_ref, start, start + size)
+
+    def step(trust_of):
+        @pl.loop(0, size // STRIP)
+        def _(k):
+            here = pl.ds(pl.multiple_of(k * STRIP, STRIP), STRIP)
+            w = w_ref[:, here]
+            ratio = first_ref[:, here] / (jnp.sqrt(second_ref[:, here]) + ADAM_EPS) + DECAY_W * w
+            new = w - LEARN_RATE * trust_of(here) * ratio
+            new_ref[:, here] = new
+            low_ref[:, here] = new.astype(BF)
+
+    @pl.when(alone >= 0)
+    def _():
+        trust = trust_ref[jnp.maximum(alone, 0)]
+        step(lambda here: trust)
+
+    @pl.when(alone < 0)
+    def _():
+        hold[...] = jnp.zeros_like(hold)
+
+        @pl.loop(0, groups)
+        def _(g):
+            low = jnp.maximum(bounds_ref[2 * g], start)
+            high = jnp.minimum(bounds_ref[2 * g + 1], start + size)
+
+            @pl.when(low < high)
+            def _():
+                @pl.loop((low - start) // lanes, (high - start + lanes - 1) // lanes)
+                def _(k):
+                    at = pl.multiple_of(k * lanes, lanes)
+                    here = pl.ds(at, lanes)
+                    index = start + at + lax.broadcasted_iota(jnp.int32, (1, lanes), 1)
+                    hold[:, here] = jnp.where((index >= low) & (index < high), trust_ref[g], hold[:, here])
+
+        step(lambda here: hold[:, here])
 
 
 def update(bounds, trust, master, first, second):
@@ -989,7 +1219,8 @@
     small_own = jnp.concatenate(
         [window(lines3, -base, GAIN_ROWS), window(lines3, mid - base, SMALL_ROWS)]
     )
-    small_flat = lax.psum(small_own.reshape(-1, LANES).astype(BF), "dp")
+    small_own = lax.optimization_barrier(small_own)
+    small_flat = sum_dp(small_own.reshape(-1, LANES).astype(BF), n)
     gains = lax.all_gather(small_flat[:GAIN_ROWS].reshape(4, DG), "tensor", axis=1, tiled=True)
     gains = gains.astype(F32)
     small = {}
@@ -1008,7 +1239,7 @@
     valid = (pos < lengths[:, None]).astype(F32).reshape(-1, 1)
     grad = cotangent.astype(F32) * valid
     out, grad_in, operands, small_grads = layer(x, grad, w, small, gains, n)
-    small_sum = lax.psum(small_grads, "dp").astype(F32).reshape(-1, 1, LANES)
+    small_sum = small_grads.astype(F32).reshape(-1, 1, LANES)
     laid = ring_reduce(*operands, n, lines)
 
     before, after = extents(n, lines)
@@ -1019,8 +1250,11 @@
 
     begin = local(d * (BIG_ROWS // n))
     close = local((d + 1) * (BIG_ROWS // n) - 1) + LINES
-    from_prev = lax.ppermute(laid[SLACK + lines : SLACK + lines + after], "dp", shift_perm(n, 1))
-    from_next = lax.ppermute(laid[SLACK - before : SLACK], "dp", shift_perm(n, -1))
+    tail, head, laid = lax.optimization_barrier(
+        (laid[SLACK + lines : SLACK + lines + after], laid[SLACK - before : SLACK], laid)
+    )
+    from_prev = lax.ppermute(tail, "dp", shift_perm(n, 1))
+    from_next = lax.ppermute(head, "dp", shift_perm(n, -1))
     line = lax.broadcasted_iota(jnp.int32, (after, 1, 1), 0)
     top = jnp.where(line < begin, from_prev, laid[SLACK : SLACK + after])
     line = lax.broadcasted_iota(jnp.int32, (before, 1, 1), 0) + (lines - before)

time: 1940 us -> 1600 us (0.82)
  waiting for transfers between devices: 395 us -> 8.71 us
  Pallas kernels: 1100 us -> 1280 us
  other arithmetic: 192 us -> 68.4 us
    psum x11 -> x0, waiting for transfers between devices: 394 us -> none  [the longest x7 211 us: total(): return lax.psum(partial_out.astype(BF), 'tensor').astype(F32)]
    pallas_call x0 -> x12, Pallas kernels: none -> 247 us  [the longest x10 168 us: sum_tensor(): pl.pallas_call(functools.partial(pair_kernel, parts), out_shape=jax.Shape...]
    unnamed x13, other arithmetic: 131 us -> 12 us
    pallas_call x1, Pallas kernels: 93 us -> 43.9 us  [moments(): pl.pallas_call(functools.partial(moments_kernel, groups, shard), grid=(pl...]
    unnamed x151 -> x201, local copies, waits for them, and re-layouts: 38.9 us -> 33.7 us
  transfers between devices with their start and end apart: 15 -> 4, of which waited for: 11 -> 1; matrix products, arithmetic and copies ran while one was open for 5% -> 3% of each run, Pallas kernels for 0% -> 3%
where the time goes in v3:
time: 1600 us; the launch traced here: 1590 us
  Pallas kernels  1280 us (80%)
  local copies, waits for them, and re-layouts  111 us (7%)
  matrix products  95.4 us (6%)
  other arithmetic  68.4 us (4%)
    pallas_call x1, Pallas kernels, ring_reduce(): pl.pallas_call(functools.partial(reduce_kernel, n, shard_lines), out_shap...  447 us
    pallas_call x1, Pallas kernels, ring_gather(): pl.pallas_call(functools.partial(gather_kernel, n, subs), out_shape=jax.S...  437 us
    pallas_call x10, Pallas kernels, sum_tensor(): pl.pallas_call(functools.partial(pair_kernel, parts), out_shape=jax.Shape...  168 us
    pallas_call x2, Pallas kernels, sum_dp(): pl.pallas_call(functools.partial(spread_kernel, n), out_shape=jax.ShapeDt...  79.7 us
    pallas_call x1, Pallas kernels, moments(): pl.pallas_call(functools.partial(moments_kernel, groups, shard), grid=(pl...  43.9 us
    dot_general x9, matrix products, mat_nt(): lax.dot_general(a, b, (((1,), (1,)), ((), ())), preferred_element_type=F32)  42.5 us
    pallas_call x1, Pallas kernels, scan_backward(): pl.pallas_call(functools.partial(adjoint_kernel, rows // SLOT), out_shape...  40.8 us
    dot_general x9, matrix products, mat_nn(): return jnp.dot(a, b, preferred_element_type=F32)  39.3 us
  transfers between devices with their start and end apart: 4, of which 1 were waited for; matrix products, arithmetic and copies ran while one was open for 3% of the time, Pallas kernels for 3%

profile of v3, /device:TPU:2, one launch (start us, length us, event | category | flops | bytes accessed | tf_op | source)
XLA Modules:
  0.0 1586.4 jit_solution(1541185218075709159)
XLA Ops:
  17.3 46.0 %sum_dp.2 = bf16[2560,128]{1,0:T(8,128)(2,1)} custom-call(bf16[2560,128]{1,0:T(8,128)(2,1)} %pad.46.x_ref), custom_call_target="tpu_custom_call" | custom-call | tf_op jit(solution)/shard_map/sum_dp/pallas_call | solution.py:487
  98.2 436.9 %ring_gather.1 = bf16[11264,2048]{1,0:T(8,128)(2,1)} custom-call(bf16[1408,2048]{1,0:T(8,128)(2,1)S(1)} %stack_own.1.own_ref), custom_call_target="tpu_custom_call" | custom-call | flops 1000000000 | bytes 1500000000 | tf_op jit(solution)/shard_map/ring_gather/pallas_call | solution.py:191
  546.3 8.1 sum_tensor.10
  564.0 11.5 scan_forward.1
  580.9 18.9 %sum_tensor.11 = bf16[256,2048]{1,0:T(8,128)(2,1)} custom-call(bf16[256,2048]{1,0:T(8,128)(2,1)} %fusion.29.x_ref), custom_call_target="tpu_custom_call" | custom-call | tf_op jit(solution)/shard_map/sum_tensor/pallas_call | solution.py:398
  614.6 18.9 %sum_tensor.12 = bf16[256,2048]{1,0:T(8,128)(2,1)} custom-call(bf16[256,2048]{1,0:T(8,128)(2,1)} %fusion.32.x_ref), custom_call_target="tpu_custom_call" | custom-call | tf_op jit(solution)/shard_map/sum_tensor/pallas_call | solution.py:398
  635.6 11.1 reshape.431
  646.7 8.6 copy.74
  672.2 19.0 %sum_tensor.13 = bf16[256,2048]{1,0:T(8,128)(2,1)} custom-call(bf16[256,2048]{1,0:T(8,128)(2,1)} %convolution_convert_fusion.1.x_ref), custom_call_target="tpu_custom_call" | custom-call | tf_op jit(solution)/shard_map/sum_tensor/pallas_call | solution.py:398
  706.4 18.9 %sum_tensor.14 = bf16[256,2048]{1,0:T(8,128)(2,1)} custom-call(bf16[256,2048]{1,0:T(8,128)(2,1)} %fusion.35.x_ref), custom_call_target="tpu_custom_call" | custom-call | tf_op jit(solution)/shard_map/sum_tensor/pallas_call | solution.py:398
  737.7 18.9 %sum_tensor.15 = bf16[256,2048]{1,0:T(8,128)(2,1)} custom-call(bf16[256,2048]{1,0:T(8,128)(2,1)} %fusion.44.x_ref), custom_call_target="tpu_custom_call" | custom-call | tf_op jit(solution)/shard_map/sum_tensor/pallas_call | solution.py:398
  782.6 18.9 %sum_tensor.16 = bf16[256,2048]{1,0:T(8,128)(2,1)} custom-call(bf16[256,2048]{1,0:T(8,128)(2,1)} %convolution_convert_fusion.2.x_ref), custom_call_target="tpu_custom_call" | custom-call | tf_op jit(solution)/shard_map/sum_tensor/pallas_call | solution.py:398
  818.2 19.0 %sum_tensor.17 = bf16[256,2048]{1,0:T(8,128)(2,1)} custom-call(bf16[256,2048]{1,0:T(8,128)(2,1)} %fusion.41.x_ref), custom_call_target="tpu_custom_call" | custom-call | tf_op jit(solution)/shard_map/sum_tensor/pallas_call | solution.py:398
  846.2 40.8 %scan_backward.1 = (bf16[256,1024]{1,0:T(8,128)(2,1)}, f32[256,1024]{1,0:T(8,128)}, bf16[256,256]{1,0:T(8,128)(2,1)}, f32[128,1024]{1,0:T(8,128)}, f32[1,1024]{1...) custom-call(bf16[256,128]{1,0:T(8,128)(2,1)} %slice.321.proj_ref, f32[256,32]{1,0:T(8,128)} %slice_convert_fusion.1.bc_ref, ...), custom_call_target="tpu_custom_call" | custom-call | tf_op jit(solution)/shard_map/scan_backward/pallas_call | solution.py:680
  887.0 8.1 sum_tensor.18
  909.1 19.0 %sum_tensor.19 = bf16[256,2048]{1,0:T(8,128)(2,1)} custom-call(bf16[256,2048]{1,0:T(8,128)(2,1)} %fusion.38.x_ref), custom_call_target="tpu_custom_call" | custom-call | tf_op jit(solution)/shard_map/sum_tensor/pallas_call | solution.py:398
  931.4 33.7 %sum_dp.3 = bf16[2560,128]{1,0:T(8,128)(2,1)} custom-call(bf16[2560,128]{1,0:T(8,128)(2,1)} %pad.54.x_ref), custom_call_target="tpu_custom_call" | custom-call | tf_op jit(solution)/shard_map/sum_dp/pallas_call | solution.py:487
  970.2 11.1 reshape.434.qkv_ref
  997.7 447.3 %ring_reduce.1 = f32[28985,1,128]{2,1,0:T(1,128)} custom-call(bf16[9728,256]{1,0:T(8,128)(2,1)} %copy.87.left_ref, bf16[7,256,2048]{2,1,0:T(8,128)(2,1)} %bitcast_dynamic-update-slice_fusion.right_refs, bf16[1536,2048]{1,0:T(8,128)(2,1)} %reshape.434.qkv_ref), custom_call_target="tpu_custom_call" | custom-call | flops 1000000000 | bytes 1500000000 | tf_op jit(solution)/shard_map/ring_reduce/pallas_call | solution.py:312
  1454.2 11.6 copy.132
  1465.8 8.7 collective-permute-done.2
  1486.7 43.9 %moments.1 = (f32[1,2923648]{1,0:T(1,128)}, f32[1,2923648]{1,0:T(1,128)}, f32[1,2923648]{1,0:T(1,128)}, f32[38]{0:T(128)S(1)}) custom-call(s32[38]{0:T(128)S(1)} %copy-done.2, f32[1,3710080]{1,0:T(1,128)} %bitcast.145, f32[1,2923648]{1,0:T(1,128)S(1)} %bitcast.144, f32[1,2923648]{1,0:T(1,128)} %one_ref.1, f32[1,2923648]{1,0:T(1,128)} %two_ref.1), custom_call_target="tpu_custom_call" | custom-call | tf_op jit(solution)/shard_map/moments/pallas_call | solution.py:1054
  1531.2 10.1 sum_everywhere.1
  1547.3 38.9 %update.1 = (f32[1,2923648]{1,0:T(1,128)}, bf16[1,2923648]{1,0:T(2,128)(2,1)}) custom-call(s32[38]{0:T(128)S(1)} %copy-done.2, f32[19]{0:T(128)S(1)} %fusion.126.trust_ref, f32[1,2923648]{1,0:T(1,128)S(1)} %copy-done.1, f32[1,2923648]{1,0:T(1,128)} %get-tuple-element.89.first_ref, f32[1,2923648]{1,0:T(1,128)} %get-tuple-element.90.second_ref), custom_call_target="tpu_custom_call" | custom-call | tf_op jit(solution)/shard_map/update/pallas_call | solution.py:1115
  (354 shorter events, 256.2 us)
Async XLA Ops:
  1.6 77.3 %collective-permute-start = (f32[297,1,128]{2,1,0:T(1,128)S(1)}, f32[297,1,128]{2,1,0:T(1,128)S(1)}, u32[]{:S(2)}, u32[]{:S(2)}) collective-permute-start(f32[297,1,128]{2,1,0:T(1,128)S(1)} %slice_bitcast_fusion.5), channel_id=1, source_target_pairs={{0,4},{4,8},{8,12},{12,16},{16,20},{20,24},{24,28},{1,5},{5,9},{9,... | collective-permute-start | bytes 456200 | tf_op jit(solution)/shard_map/ppermute | solution.py:939
  7.0 74.2 %collective-permute-start.1 = (f32[1878,1,128]{2,1,0:T(1,128)}, f32[1878,1,128]{2,1,0:T(1,128)}, u32[]{:S(2)}, u32[]{:S(2)}) collective-permute-start(f32[1878,1,128]{2,1,0:T(1,128)} %slice_bitcast_fusion), channel_id=1, source_target_pairs={{4,0},{8,4},{12,8},{16,12},{20,16},{24,20},{28,24},{5,1},{9,5},{13... | collective-permute-start | bytes 2884616 | tf_op jit(solution)/shard_map/ppermute | solution.py:938
  16.4 51.0 %copy-start.3 = (bf16[256,2048]{1,0:T(8,128)(2,1)S(1)}, bf16[256,2048]{1,0:T(8,128)(2,1)}, u32[]{:S(2)}) copy-start(bf16[256,2048]{1,0:T(8,128)(2,1)} %param.11) | copy-start | bytes 3145732
  17.3 58.9 %copy-start.89 = (s32[2]{0:T(128)S(1)}, s32[2]{0:T(128)}, u32[]{:S(2)}) copy-start(s32[2]{0:T(128)} %param.13) | copy-start | bytes 28
  78.2 467.0 %copy-start.32 = (bf16[1024,160]{1,0:T(8,128)(2,1)}, bf16[1024,160]{1,0:T(8,128)(2,1)S(1)}, u32[]{:S(2)}) copy-start(bf16[1024,160]{1,0:T(8,128)(2,1)S(1)} %reshape.429) | copy-start | bytes 983044
  98.1 436.9 %copy-start.54 = (f32[1,2048]{1,0:T(1,128)S(1)}, f32[1,2048]{1,0:T(1,128)}, u32[]{:S(2)}) copy-start(f32[1,2048]{1,0:T(1,128)} %copy-done.53) | copy-start | bytes 24580
  98.2 436.9 %copy-start.75 = (f32[256]{0:T(256)S(1)}, f32[256]{0:T(256)}, u32[]{:S(2)}) copy-start(f32[256]{0:T(256)} %copy-done.74) | copy-start | bytes 3076
  580.9 20.7 %copy-start.56 = (f32[1,2048]{1,0:T(1,128)S(1)}, f32[1,2048]{1,0:T(1,128)}, u32[]{:S(2)}) copy-start(f32[1,2048]{1,0:T(1,128)} %get-tuple-element.147) | copy-start | bytes 24580
  635.6 19.7 %copy-start.79 = (f32[256]{0:T(256)}, f32[256]{0:T(256)S(1)}, u32[]{:S(2)}) copy-start(f32[256]{0:T(256)S(1)} %add_rsqrt_fusion.1) | copy-start | bytes 3076
  818.2 19.0 %copy-start.57 = (f32[1,2048]{1,0:T(1,128)S(1)}, f32[1,2048]{1,0:T(1,128)}, u32[]{:S(2)}) copy-start(f32[1,2048]{1,0:T(1,128)} %get-tuple-element.147) | copy-start | bytes 24580
  818.2 19.0 %copy-start.78 = (f32[256]{0:T(256)S(1)}, f32[256]{0:T(256)}, u32[]{:S(2)}) copy-start(f32[256]{0:T(256)} %copy-done.77) | copy-start | bytes 3076
  846.2 48.9 %copy-start.17 = (bf16[2,128,1024]{2,1,0:T(8,128)(2,1)S(1)}, bf16[2,128,1024]{2,1,0:T(8,128)(2,1)}, u32[]{:S(2)}) copy-start(bf16[2,128,1024]{2,1,0:T(8,128)(2,1)} %copy-done.16) | copy-start | bytes 1572868
  846.2 50.1 %copy-start.25 = (f32[256,1024]{1,0:T(8,128)S(1)}, f32[256,1024]{1,0:T(8,128)}, u32[]{:S(2)}) copy-start(f32[256,1024]{1,0:T(8,128)} %copy-done.24) | copy-start | bytes 3145732
  846.2 50.1 %copy-start.33 = (bf16[1024,160]{1,0:T(8,128)(2,1)S(1)}, bf16[1024,160]{1,0:T(8,128)(2,1)}, u32[]{:S(2)}) copy-start(bf16[1024,160]{1,0:T(8,128)(2,1)} %copy-done.32) | copy-start | bytes 983044
  908.0 20.1 %copy-start.55 = (f32[1,2048]{1,0:T(1,128)S(1)}, f32[1,2048]{1,0:T(1,128)}, u32[]{:S(2)}) copy-start(f32[1,2048]{1,0:T(1,128)} %copy-done.53) | copy-start | bytes 24580
  908.0 20.1 %copy-start.76 = (f32[256]{0:T(256)S(1)}, f32[256]{0:T(256)}, u32[]{:S(2)}) copy-start(f32[256]{0:T(256)} %copy-done.74) | copy-start | bytes 3076
  909.1 21.1 %copy-start.73 = (f32[2048]{0:T(1024)S(1)}, f32[2048]{0:T(1024)}, u32[]{:S(2)}) copy-start(f32[2048]{0:T(1024)} %get-tuple-element.98) | copy-start | bytes 24580
  909.1 21.3 %copy-start.64 = (f32[128,128]{1,0:T(8,128)S(1)}, f32[128,128]{1,0:T(8,128)}, u32[]{:S(2)}) copy-start(f32[128,128]{1,0:T(8,128)} %get-tuple-element.56) | copy-start | bytes 196612
  930.5 36.6 %copy-start.15 = (f32[256,2048]{1,0:T(8,128)S(1)}, f32[256,2048]{1,0:T(8,128)}, u32[]{:S(2)}) copy-start(f32[256,2048]{1,0:T(8,128)} %copy-done.14) | copy-start | bytes 6291460
  1447.2 27.3 %collective-permute-start.2 = (f32[1878,1,128]{2,1,0:T(1,128)S(1)}, f32[1878,1,128]{2,1,0:T(1,128)S(1)}, u32[]{:S(2)}, u32[]{:S(2)}) collective-permute-start(f32[1878,1,128]{2,1,0:T(1,128)S(1)} %slice.358), channel_id=1, source_target_pairs={{0,4},{4,8},{8,12},{12,16},{16,20},{20,24},{24,28},{1,5},{5,9},{9,... | collective-permute-start | bytes 2884616 | tf_op jit(solution)/shard_map/ppermute | solution.py:1256
  1451.7 35.0 %slice-start = ((s8[11694592]{0:T(1024)(128)(4,1)}), s8[4194304]{0:T(1024)(128)(4,1)S(1)}, s32[]{:S(2)}) async-start(s8[11694592]{0:T(1024)(128)(4,1)} %bitcast.143), calls=%async_computation | async-start | bytes 8388608
  1451.8 34.9 %slice-start.1 = ((s8[11694592]{0:T(1024)(128)(4,1)}), s8[4194304]{0:T(1024)(128)(4,1)S(1)}, s32[]{:S(2)}) async-start(s8[11694592]{0:T(1024)(128)(4,1)} %bitcast.143), calls=%async_computation.1 | async-start | bytes 8388608
  1451.9 34.8 %slice-start.2 = ((s8[11694592]{0:T(1024)(128)(4,1)}), s8[3305984]{0:T(1024)(128)(4,1)S(1)}, s32[]{:S(2)}) async-start(s8[11694592]{0:T(1024)(128)(4,1)} %bitcast.143), calls=%async_computation.2 | async-start | bytes 6612992
  1451.9 30.6 %collective-permute-start.3 = (f32[297,1,128]{2,1,0:T(1,128)S(1)}, f32[297,1,128]{2,1,0:T(1,128)S(1)}, u32[]{:S(2)}, u32[]{:S(2)}) collective-permute-start(f32[297,1,128]{2,1,0:T(1,128)S(1)} %slice.359), channel_id=1, source_target_pairs={{4,0},{8,4},{12,8},{16,12},{20,16},{24,20},{28,24},{5,1},{9,5},{13... | collective-permute-start | bytes 456200 | tf_op jit(solution)/shard_map/ppermute | solution.py:1257
  (77 other events, 348.0 us)

commit v4 on v3

--- a/solution.py
+++ b/solution.py
@@ -493,6 +493,41 @@
         compiler_params=pltpu.CompilerParams(collective_id=5, has_side_effects=True),
         name="sum_dp",
     )(padded)[:count]
+
+
+def rows_kernel(src, dst, src_ref, out_ref, inn, out):
+    wide = src_ref.shape[1] // LANES
+    thin = out_ref.shape[1] // LANES
+    groups = src_ref.shape[0] // src
+    for b in range(wide):
+        inn[b] = src_ref[:, b * LANES : (b + 1) * LANES].astype(F32)
+    for q in range(src * wide):
+        a, b = divmod(q, wide)
+        j, c = divmod(q, thin)
+        out[c, pl.ds(j, groups, stride=dst), :] = inn[b, pl.ds(a, groups, stride=src), :]
+    for c in range(thin):
+        out_ref[:, c * LANES : (c + 1) * LANES] = out[c].astype(BF)
+
+
+def change_rows(value, start, count, width):
+    cols = value.shape[1]
+    unit = math.gcd(cols, width)
+    src, dst = width // unit, cols // unit
+    block = 32 * src
+    first = start // block
+    return pl.pallas_call(
+        functools.partial(rows_kernel, src, dst),
+        grid=(count // block,),
+        out_shape=jax.ShapeDtypeStruct((count * cols // width, width), BF),
+        in_specs=[pl.BlockSpec((block, cols), lambda i: (i + first, 0))],
+        out_specs=pl.BlockSpec((32 * dst, width), lambda i: (i, 0)),
+        scratch_shapes=[
+            pltpu.VMEM((cols // LANES, block, LANES), F32),
+            pltpu.VMEM((width // LANES, 32 * dst, LANES), F32),
+        ],
+        compiler_params=pltpu.CompilerParams(vmem_limit_bytes=24 << 20),
+        name="change_rows",
+    )(value)
 
 
 def spread(ref, value):
@@ -860,7 +895,8 @@
 
     left_t = jnp.concatenate([h1, gated, h2, act1, attended, h4, act2], axis=1).T
     rights = jnp.stack([gmixed, gb1, gp1, gb2, gb3, gp2, gb4])
-    g_qkv = mat_tn(h3, gpk).astype(BF).reshape(-1, D)
+    g_qkv = mat_tn(h3, gpk).astype(BF)
+    g_qkv = change_rows(g_qkv, 0, D, D)
     start = lax.axis_index("tensor") * DG
     g_gain = lax.dynamic_slice_in_dim(jnp.stack([gg1, gg2, gg3, gg4]), start, DG, 1)
     pieces = [g_gain, g_conv_w, g_conv_b, g_bias, g_skip, g_alog, g_wx, g_dt]
@@ -1220,7 +1256,9 @@
         [window(lines3, -base, GAIN_ROWS), window(lines3, mid - base, SMALL_ROWS)]
     )
     small_own = lax.optimization_barrier(small_own)
-    small_flat = sum_dp(small_own.reshape(-1, LANES).astype(BF), n)
+    small_flat = lax.psum(small_own.reshape(-1, LANES).astype(BF), "dp")
+    weights = ring_gather(stack_own(lines3, n), n)
+    weights, small_flat = lax.optimization_barrier((weights, small_flat))
     gains = lax.all_gather(small_flat[:GAIN_ROWS].reshape(4, DG), "tensor", axis=1, tiled=True)
     gains = gains.astype(F32)
     small = {}
@@ -1229,11 +1267,10 @@
         count = math.prod(shape) // LANES
         small[name] = small_flat[at : at + count].reshape(shape)
         at += count
-    weights = ring_gather(stack_own(lines3, n), n)
     w = {}
     for name, rows in BIG:
         w[name] = weights[BIG_OFF[name] : BIG_OFF[name] + rows]
-    w["w_qkv"] = w["w_qkv"].reshape(D, 3 * HW)
+    w["w_qkv"] = change_rows(weights, BIG_OFF["w_qkv"], dict(BIG)["w_qkv"], 3 * HW)
     x = tokens.astype(F32)
     pos = lax.broadcasted_iota(jnp.int32, (tokens.shape[0] // SLOT, SLOT), 1)
     valid = (pos < lengths[:, None]).astype(F32).reshape(-1, 1)

time: 1600 us -> 1700 us (1.062)
  other arithmetic: 68.4 us -> 189 us
  Pallas kernels: 1280 us -> 1260 us
  local copies, waits for them, and re-layouts: 111 us -> 91.4 us
    unnamed x13 -> x15, other arithmetic: 12 us -> 126 us
    pallas_call x2 -> x1, Pallas kernels: 79.7 us -> 33.8 us  [sum_dp(): pl.pallas_call(functools.partial(spread_kernel, n), out_shape=jax.ShapeDt...]
    reshape x2 -> x1, local copies, waits for them, and re-layouts: 22.2 us -> 3.27 us  [layer(): packed = mat_nn(h3, w['w_qkv']).reshape(m, SLOT, 3, hr, HEAD_DIM)]
    unnamed x201 -> x195, local copies, waits for them, and re-layouts: 33.7 us -> 40.2 us
  transfers between devices with their start and end apart: 4 -> 5, of which waited for: 1 -> 1; matrix products, arithmetic and copies ran while one was open for 3% -> 9% of each run, Pallas kernels for 3% -> 27%
where the time goes in v4:
time: 1700 us; the launch traced here: 1690 us
  Pallas kernels  1260 us (74%)
  other arithmetic  189 us (11%)
  matrix products  97.4 us (6%)
  local copies, waits for them, and re-layouts  91.4 us (5%)
    pallas_call x1, Pallas kernels, ring_gather(): pl.pallas_call(functools.partial(gather_kernel, n, subs), out_shape=jax.S...  448 us
    pallas_call x1, Pallas kernels, ring_reduce(): pl.pallas_call(functools.partial(reduce_kernel, n, shard_lines), out_shap...  447 us
    pallas_call x10, Pallas kernels, sum_tensor(): pl.pallas_call(functools.partial(pair_kernel, parts), out_shape=jax.Shape...  168 us
    unnamed x15, other arithmetic  126 us
    pallas_call x1, Pallas kernels, moments(): pl.pallas_call(functools.partial(moments_kernel, groups, shard), grid=(pl...  43.9 us
    dot_general x9, matrix products, mat_nt(): lax.dot_general(a, b, (((1,), (1,)), ((), ())), preferred_element_type=F32)  42.9 us
    pallas_call x1, Pallas kernels, scan_backward(): pl.pallas_call(functools.partial(adjoint_kernel, rows // SLOT), out_shape...  41.1 us
    dot_general x9, matrix products, mat_nn(): return jnp.dot(a, b, preferred_element_type=F32)  41.1 us
  transfers between devices with their start and end apart: 5, of which 1 were waited for; matrix products, arithmetic and copies ran while one was open for 9% of the time, Pallas kernels for 27%

profile of v4, /device:TPU:2, one launch (start us, length us, event | category | flops | bytes accessed | tf_op | source)
XLA Modules:
  0.0 1692.9 jit_solution(12060591002349551742)
XLA Ops:
  16.0 113.9 %reduce.4 = bf16[2923648]{0:T(1024)(128)(2,1)} reduce(f32[1,2923648]{1,0:T(1,128)} %w_ref.3, f32[]{:T(128)} %constant.173), dimensions={0}, to_apply=%param.14.reduce_sub_computation | reduce | bytes 17541892 | tf_op args[3]
  162.1 447.8 %ring_gather.1.src_ref = bf16[11264,2048]{1,0:T(8,128)(2,1)} custom-call(bf16[1408,2048]{1,0:T(8,128)(2,1)S(1)} %stack_own.1.own_ref), custom_call_target="tpu_custom_call" | custom-call | flops 1000000000 | bytes 1500000000 | tf_op jit(solution)/shard_map/ring_gather/pallas_call | solution.py:191
  615.0 16.3 all_gather.3
  642.9 8.1 sum_tensor.10
  655.2 10.3 change_rows.2
  669.1 11.2 scan_forward.1
  684.9 19.0 %sum_tensor.11 = bf16[256,2048]{1,0:T(8,128)(2,1)} custom-call(bf16[256,2048]{1,0:T(8,128)(2,1)} %fusion.29.x_ref), custom_call_target="tpu_custom_call" | custom-call | tf_op jit(solution)/shard_map/sum_tensor/pallas_call | solution.py:398
  719.5 18.9 %sum_tensor.12 = bf16[256,2048]{1,0:T(8,128)(2,1)} custom-call(bf16[256,2048]{1,0:T(8,128)(2,1)} %fusion.32.x_ref), custom_call_target="tpu_custom_call" | custom-call | tf_op jit(solution)/shard_map/sum_tensor/pallas_call | solution.py:398
  764.6 19.0 %sum_tensor.13 = bf16[256,2048]{1,0:T(8,128)(2,1)} custom-call(bf16[256,2048]{1,0:T(8,128)(2,1)} %convolution_convert_fusion.1.x_ref), custom_call_target="tpu_custom_call" | custom-call | tf_op jit(solution)/shard_map/sum_tensor/pallas_call | solution.py:398
  798.8 18.9 %sum_tensor.14 = bf16[256,2048]{1,0:T(8,128)(2,1)} custom-call(bf16[256,2048]{1,0:T(8,128)(2,1)} %fusion.35.x_ref), custom_call_target="tpu_custom_call" | custom-call | tf_op jit(solution)/shard_map/sum_tensor/pallas_call | solution.py:398
  830.1 18.9 %sum_tensor.15 = bf16[256,2048]{1,0:T(8,128)(2,1)} custom-call(bf16[256,2048]{1,0:T(8,128)(2,1)} %fusion.44.x_ref), custom_call_target="tpu_custom_call" | custom-call | tf_op jit(solution)/shard_map/sum_tensor/pallas_call | solution.py:398
  874.9 18.9 %sum_tensor.16 = bf16[256,2048]{1,0:T(8,128)(2,1)} custom-call(bf16[256,2048]{1,0:T(8,128)(2,1)} %convolution_convert_fusion.2.x_ref), custom_call_target="tpu_custom_call" | custom-call | tf_op jit(solution)/shard_map/sum_tensor/pallas_call | solution.py:398
  910.8 19.0 %sum_tensor.17 = bf16[256,2048]{1,0:T(8,128)(2,1)} custom-call(bf16[256,2048]{1,0:T(8,128)(2,1)} %fusion.41.x_ref), custom_call_target="tpu_custom_call" | custom-call | tf_op jit(solution)/shard_map/sum_tensor/pallas_call | solution.py:398
  939.3 41.1 %scan_backward.1 = (bf16[256,1024]{1,0:T(8,128)(2,1)}, f32[256,1024]{1,0:T(8,128)}, bf16[256,256]{1,0:T(8,128)(2,1)}, f32[128,1024]{1,0:T(8,128)}, f32[1,1024]{1...) custom-call(bf16[256,128]{1,0:T(8,128)(2,1)} %slice.309.proj_ref, f32[256,32]{1,0:T(8,128)} %slice_convert_fusion.bc_ref, ...), custom_call_target="tpu_custom_call" | custom-call | tf_op jit(solution)/shard_map/scan_backward/pallas_call | solution.py:715
  980.5 8.1 sum_tensor.18
  1005.6 19.0 %sum_tensor.19 = bf16[256,2048]{1,0:T(8,128)(2,1)} custom-call(bf16[256,2048]{1,0:T(8,128)(2,1)} %fusion.38.x_ref), custom_call_target="tpu_custom_call" | custom-call | tf_op jit(solution)/shard_map/sum_tensor/pallas_call | solution.py:398
  1034.1 33.8 %sum_dp.1 = bf16[2560,128]{1,0:T(8,128)(2,1)} custom-call(bf16[2560,128]{1,0:T(8,128)(2,1)} %pad.50.x_ref), custom_call_target="tpu_custom_call" | custom-call | tf_op jit(solution)/shard_map/sum_dp/pallas_call | solution.py:487
  1079.8 8.0 copy.90.left_ref
  1096.2 447.4 %ring_reduce.1 = f32[28985,1,128]{2,1,0:T(1,128)} custom-call(bf16[9728,256]{1,0:T(8,128)(2,1)} %copy.90.left_ref, bf16[7,256,2048]{2,1,0:T(8,128)(2,1)} %bitcast_dynamic-update-slice_fusion.right_refs, bf16[1536,2048]{1,0:T(8,128)(2,1)} %copy-done.2), custom_call_target="tpu_custom_call" | custom-call | flops 1000000000 | bytes 1500000000 | tf_op jit(solution)/shard_map/ring_reduce/pallas_call | solution.py:312
  1552.8 11.6 copy.147
  1564.4 8.8 collective-permute-done.2
  1585.4 43.9 %moments.1 = (f32[1,2923648]{1,0:T(1,128)}, f32[1,2923648]{1,0:T(1,128)}, f32[1,2923648]{1,0:T(1,128)}, f32[38]{0:T(128)S(1)}) custom-call(s32[38]{0:T(128)S(1)} %copy-done.4, f32[1,3710080]{1,0:T(1,128)} %bitcast.135, f32[1,2923648]{1,0:T(1,128)S(1)} %bitcast.130, f32[1,2923648]{1,0:T(1,128)} %one_ref.1, f32[1,2923648]{1,0:T(1,128)} %two_ref.1), custom_call_target="tpu_custom_call" | custom-call | tf_op jit(solution)/shard_map/moments/pallas_call | solution.py:1090
  1629.9 11.0 sum_everywhere.1
  1647.0 38.9 %update.1 = (f32[1,2923648]{1,0:T(1,128)}, bf16[1,2923648]{1,0:T(2,128)(2,1)}) custom-call(s32[38]{0:T(128)S(1)} %copy-done.4, f32[19]{0:T(128)S(1)} %fusion.127.trust_ref, f32[1,2923648]{1,0:T(1,128)S(1)} %copy-done.1, f32[1,2923648]{1,0:T(1,128)} %get-tuple-element.93.first_ref, f32[1,2923648]{1,0:T(1,128)} %get-tuple-element.94.second_ref), custom_call_target="tpu_custom_call" | custom-call | tf_op jit(solution)/shard_map/update/pallas_call | solution.py:1151
  (351 shorter events, 265.5 us)
Async XLA Ops:
  7.2 602.8 %all-reduce.11.cloned.1.call-start = ((), (), s32[]{:S(2)}) async-start(), calls=%async_computation | async-start | bytes 1282048 | tf_op jit(solution)/shard_map/psum | solution.py:1259
  8.1 134.7 %collective-permute-start = (f32[297,1,128]{2,1,0:T(1,128)S(1)}, f32[297,1,128]{2,1,0:T(1,128)S(1)}, u32[]{:S(2)}, u32[]{:S(2)}) collective-permute-start(f32[297,1,128]{2,1,0:T(1,128)S(1)} %slice_bitcast_fusion.3), channel_id=1, source_target_pairs={{0,4},{4,8},{8,12},{12,16},{16,20},{20,24},{24,28},{1,5},{5,9},{9,... | collective-permute-start | bytes 456200 | tf_op jit(solution)/shard_map/ppermute | solution.py:975
  13.6 131.6 %collective-permute-start.1 = (f32[1878,1,128]{2,1,0:T(1,128)}, f32[1878,1,128]{2,1,0:T(1,128)}, u32[]{:S(2)}, u32[]{:S(2)}) collective-permute-start(f32[1878,1,128]{2,1,0:T(1,128)} %slice_bitcast_fusion), channel_id=1, source_target_pairs={{4,0},{8,4},{12,8},{16,12},{20,16},{24,20},{28,24},{5,1},{9,5},{13... | collective-permute-start | bytes 2884616 | tf_op jit(solution)/shard_map/ppermute | solution.py:974
  139.5 514.4 %copy-start.73 = (f32[256]{0:T(256)}, f32[256]{0:T(256)S(1)}, u32[]{:S(2)}) copy-start(f32[256]{0:T(256)S(1)} %add_rsqrt_fusion.3) | copy-start | bytes 3076
  632.0 80.3 %copy-start.53 = (f32[1,2048]{1,0:T(1,128)}, f32[1,2048]{1,0:T(1,128)S(1)}, u32[]{:S(2)}) copy-start(f32[1,2048]{1,0:T(1,128)S(1)} %get-tuple-element.151) | copy-start | bytes 24580
  684.9 20.8 %copy-start.27 = (bf16[256,1024]{1,0:T(8,128)(2,1)S(1)}, bf16[256,1024]{1,0:T(8,128)(2,1)}, u32[]{:S(2)}) copy-start(bf16[256,1024]{1,0:T(8,128)(2,1)} %scan_forward.1) | copy-start | bytes 1572868
  798.8 19.0 %copy-start.80 = (f32[256]{0:T(256)S(1)}, f32[256]{0:T(256)}, u32[]{:S(2)}) copy-start(f32[256]{0:T(256)} %fusion.134) | copy-start | bytes 3076
  830.1 19.0 %copy-start.56 = (f32[1,2048]{1,0:T(1,128)S(1)}, f32[1,2048]{1,0:T(1,128)}, u32[]{:S(2)}) copy-start(f32[1,2048]{1,0:T(1,128)} %get-tuple-element.149) | copy-start | bytes 24580
  830.1 19.0 %copy-start.78 = (f32[256]{0:T(256)S(1)}, f32[256]{0:T(256)}, u32[]{:S(2)}) copy-start(f32[256]{0:T(256)} %copy-done.77) | copy-start | bytes 3076
  910.8 19.0 %copy-start.7 = (bf16[256,2048]{1,0:T(8,128)(2,1)S(1)}, bf16[256,2048]{1,0:T(8,128)(2,1)}, u32[]{:S(2)}) copy-start(bf16[256,2048]{1,0:T(8,128)(2,1)} %sum_tensor.11) | copy-start | bytes 3145732
  910.8 19.0 %copy-start.54 = (f32[1,2048]{1,0:T(1,128)S(1)}, f32[1,2048]{1,0:T(1,128)}, u32[]{:S(2)}) copy-start(f32[1,2048]{1,0:T(1,128)} %copy-done.53) | copy-start | bytes 24580
  910.8 19.0 %copy-start.76 = (f32[256]{0:T(256)S(1)}, f32[256]{0:T(256)}, u32[]{:S(2)}) copy-start(f32[256]{0:T(256)} %copy-done.75) | copy-start | bytes 3076
  939.3 49.2 %copy-start.19 = (bf16[2,128,1024]{2,1,0:T(8,128)(2,1)S(1)}, bf16[2,128,1024]{2,1,0:T(8,128)(2,1)}, u32[]{:S(2)}) copy-start(bf16[2,128,1024]{2,1,0:T(8,128)(2,1)} %copy-done.18) | copy-start | bytes 1572868
  939.3 50.5 %copy-start.25 = (f32[256,1024]{1,0:T(8,128)S(1)}, f32[256,1024]{1,0:T(8,128)}, u32[]{:S(2)}) copy-start(f32[256,1024]{1,0:T(8,128)} %copy-done.24) | copy-start | bytes 3145732
  939.3 50.5 %copy-start.33 = (bf16[1024,160]{1,0:T(8,128)(2,1)S(1)}, bf16[1024,160]{1,0:T(8,128)(2,1)}, u32[]{:S(2)}) copy-start(bf16[1024,160]{1,0:T(8,128)(2,1)} %copy-done.32) | copy-start | bytes 983044
  1005.6 21.8 %copy-start.68 = (f32[2048]{0:T(1024)S(1)}, f32[2048]{0:T(1024)}, u32[]{:S(2)}) copy-start(f32[2048]{0:T(1024)} %get-tuple-element.102) | copy-start | bytes 24580
  1005.6 26.5 %copy-start.59 = (f32[128,128]{1,0:T(8,128)S(1)}, f32[128,128]{1,0:T(8,128)}, u32[]{:S(2)}) copy-start(f32[128,128]{1,0:T(8,128)} %get-tuple-element.60) | copy-start | bytes 196612
  1024.6 49.2 %slice-start.3 = ((s8[6291456]{0:T(1024)(128)(4,1)}), s8[2097152]{0:T(1024)(128)(4,1)S(1)}, s32[]{:S(2)}) async-start(s8[6291456]{0:T(1024)(128)(4,1)} %bitcast.131), calls=%async_computation.4 | async-start | bytes 4194304
  1032.2 37.8 %copy-start.74 = (f32[256]{0:T(256)S(1)}, f32[256]{0:T(256)}, u32[]{:S(2)}) copy-start(f32[256]{0:T(256)} %copy-done.73) | copy-start | bytes 3076
  1545.9 27.3 %collective-permute-start.2 = (f32[1878,1,128]{2,1,0:T(1,128)S(1)}, f32[1878,1,128]{2,1,0:T(1,128)S(1)}, u32[]{:S(2)}, u32[]{:S(2)}) collective-permute-start(f32[1878,1,128]{2,1,0:T(1,128)S(1)} %slice.345), channel_id=1, source_target_pairs={{0,4},{4,8},{8,12},{12,16},{16,20},{20,24},{24,28},{1,5},{5,9},{9,... | collective-permute-start | bytes 2884616 | tf_op jit(solution)/shard_map/ppermute | solution.py:1293
  1550.4 35.0 %slice-start = ((s8[11694592]{0:T(1024)(128)(4,1)}), s8[4194304]{0:T(1024)(128)(4,1)S(1)}, s32[]{:S(2)}) async-start(s8[11694592]{0:T(1024)(128)(4,1)} %bitcast.129), calls=%async_computation.1 | async-start | bytes 8388608
  1550.5 34.9 %slice-start.1 = ((s8[11694592]{0:T(1024)(128)(4,1)}), s8[4194304]{0:T(1024)(128)(4,1)S(1)}, s32[]{:S(2)}) async-start(s8[11694592]{0:T(1024)(128)(4,1)} %bitcast.129), calls=%async_computation.2 | async-start | bytes 8388608
  1550.5 34.9 %slice-start.2 = ((s8[11694592]{0:T(1024)(128)(4,1)}), s8[3305984]{0:T(1024)(128)(4,1)S(1)}, s32[]{:S(2)}) async-start(s8[11694592]{0:T(1024)(128)(4,1)} %bitcast.129), calls=%async_computation.3 | async-start | bytes 6612992
  1550.5 30.7 %collective-permute-start.3 = (f32[297,1,128]{2,1,0:T(1,128)S(1)}, f32[297,1,128]{2,1,0:T(1,128)S(1)}, u32[]{:S(2)}, u32[]{:S(2)}) collective-permute-start(f32[297,1,128]{2,1,0:T(1,128)S(1)} %slice.346), channel_id=1, source_target_pairs={{4,0},{8,4},{12,8},{16,12},{20,16},{24,20},{28,24},{5,1},{9,5},{13... | collective-permute-start | bytes 456200 | tf_op jit(solution)/shard_map/ppermute | solution.py:1294
  (74 other events, 270.1 us)
Sparse Core Ops, SparseCore 0:
  139.3 80.6 all-reduce.10

commit v5 on v4

--- a/solution.py
+++ b/solution.py
@@ -412,87 +412,6 @@
     cols = value.shape[1]
     padded = jnp.pad(value, ((0, 0), (0, -cols % LANES)))
     return sum_tensor(padded)[:, :cols]
-
-
-def spread_kernel(n, x_ref, out_ref, got, s1, r1, s2, r2):
-    d = lax.axis_index("dp")
-    t = lax.axis_index("tensor")
-    q = x_ref.shape[0] // n
-    barrier = pltpu.get_barrier_semaphore()
-
-    def peer(k):
-        return lax.rem(d + k, n)
-
-    @pl.loop(1, n)
-    def _(k):
-        pl.semaphore_signal(barrier, inc=1, device_id=(peer(k), t), device_id_type=MESH)
-
-    pl.semaphore_wait(barrier, n - 1)
-
-    def rows(e):
-        return pl.ds(pl.multiple_of(e * q, 16), q)
-
-    def one(k):
-        return pltpu.make_async_remote_copy(
-            src_ref=x_ref.at[rows(peer(k))],
-            dst_ref=got.at[k - 1],
-            send_sem=s1.at[k - 1],
-            recv_sem=r1.at[k - 1],
-            device_id=(peer(k), t),
-            device_id_type=MESH,
-        )
-
-    def two(k):
-        return pltpu.make_async_remote_copy(
-            src_ref=out_ref.at[rows(d)],
-            dst_ref=out_ref.at[rows(d)],
-            send_sem=s2.at[k - 1],
-            recv_sem=r2.at[k - 1],
-            device_id=(peer(k), t),
-            device_id_type=MESH,
-        )
-
-    @pl.loop(1, n)
-    def _(k):
-        one(k).start()
-
-    @pl.loop(1, n)
-    def _(k):
-        one(k).wait_recv()
-
-    def add(k, acc):
-        return acc + got[k - 1].astype(F32)
-
-    out_ref[rows(d), :] = lax.fori_loop(1, n, add, x_ref[rows(d), :].astype(F32)).astype(BF)
-
-    @pl.loop(1, n)
-    def _(k):
-        two(k).start()
-
-    @pl.loop(1, n)
-    def _(k):
-        two(k).wait_recv()
-
-    @pl.loop(1, n)
-    def _(k):
-        one(k).wait_send()
-        two(k).wait_send()
-
-
-def sum_dp(value, n):
-    count = value.shape[0]
-    padded = jnp.pad(value, ((0, -count % (16 * n)), (0, 0)))
-    vm = pl.BlockSpec(memory_space=pltpu.VMEM)
-    dma = pltpu.SemaphoreType.DMA((n - 1,))
-    return pl.pallas_call(
-        functools.partial(spread_kernel, n),
-        out_shape=jax.ShapeDtypeStruct(padded.shape, BF),
-        in_specs=[vm],
-        out_specs=vm,
-        scratch_shapes=[pltpu.VMEM((n - 1, padded.shape[0] // n, LANES), BF), dma, dma, dma, dma],
-        compiler_params=pltpu.CompilerParams(collective_id=5, has_side_effects=True),
-        name="sum_dp",
-    )(padded)[:count]
 
 
 def rows_kernel(src, dst, src_ref, out_ref, inn, out):
@@ -901,9 +820,8 @@
     g_gain = lax.dynamic_slice_in_dim(jnp.stack([gg1, gg2, gg3, gg4]), start, DG, 1)
     pieces = [g_gain, g_conv_w, g_conv_b, g_bias, g_skip, g_alog, g_wx, g_dt]
     small_grads = jnp.concatenate([p.reshape(-1, LANES).astype(BF) for p in pieces])
-    small_sum = sum_dp(small_grads, n)
-    g0, small_sum, left_t = lax.optimization_barrier((g0, small_sum, left_t))
-    return x4.astype(BF), g0, (left_t, rights, g_qkv), small_sum
+    g0, small_grads, left_t = lax.optimization_barrier((g0, small_grads, left_t))
+    return x4.astype(BF), g0, (left_t, rights, g_qkv), small_grads
 
 
 def extents(n, shard_rows):
@@ -988,6 +906,21 @@
     )(top, lines3, bottom)
 
 
+def low_kernel(x_ref, out_ref):
+    out_ref[...] = x_ref[:, 0, :].astype(BF)
+
+
+def to_low(value):
+    vm = pl.BlockSpec(memory_space=pltpu.VMEM)
+    return pl.pallas_call(
+        low_kernel,
+        out_shape=jax.ShapeDtypeStruct((value.shape[0], LANES), BF),
+        in_specs=[vm],
+        out_specs=vm,
+        name="to_low",
+    )(value)
+
+
 def window(values, shift, size):
     length = values.shape[0]
     s = jnp.clip(shift, 0, length - size)
@@ -1255,8 +1188,7 @@
     small_own = jnp.concatenate(
         [window(lines3, -base, GAIN_ROWS), window(lines3, mid - base, SMALL_ROWS)]
     )
-    small_own = lax.optimization_barrier(small_own)
-    small_flat = lax.psum(small_own.reshape(-1, LANES).astype(BF), "dp")
+    small_flat = lax.psum(to_low(small_own), "dp")
     weights = ring_gather(stack_own(lines3, n), n)
     weights, small_flat = lax.optimization_barrier((weights, small_flat))
     gains = lax.all_gather(small_flat[:GAIN_ROWS].reshape(4, DG), "tensor", axis=1, tiled=True)
@@ -1276,8 +1208,10 @@
     valid = (pos < lengths[:, None]).astype(F32).reshape(-1, 1)
     grad = cotangent.astype(F32) * valid
     out, grad_in, operands, small_grads = layer(x, grad, w, small, gains, n)
-    small_sum = small_grads.astype(F32).reshape(-1, 1, LANES)
+    small_sum = lax.psum(small_grads, "dp")
     laid = ring_reduce(*operands, n, lines)
+    laid, small_sum = lax.optimization_barrier((laid, small_sum))
+    small_sum = small_sum.astype(F32).reshape(-1, 1, LANES)
 
     before, after = extents(n, lines)
     slab_lines = BIG_ROWS * LINES // n

time: 1700 us -> 1560 us (0.918)
  other arithmetic: 189 us -> 77 us
  Pallas kernels: 1260 us -> 1240 us
    unnamed x15 -> x14, other arithmetic: 126 us -> 14.4 us
    pallas_call x1, Pallas kernels: 33.8 us -> 3.42 us  [to_low(): pl.pallas_call(low_kernel, out_shape=jax.ShapeDtypeStruct((value.shape[0]...]
    unnamed x195 -> x199, local copies, waits for them, and re-layouts: 40.2 us -> 40.7 us
  transfers between devices with their start and end apart: 5 -> 6, of which waited for: 1 -> 2; matrix products, arithmetic and copies ran while one was open for 9% -> 4% of each run, Pallas kernels for 27% -> 59%
where the time goes in v5:
time: 1560 us; the launch traced here: 1550 us
  Pallas kernels  1240 us (79%)
  matrix products  97.5 us (6%)
  local copies, waits for them, and re-layouts  84.9 us (5%)
  other arithmetic  77 us (5%)
  waiting for transfers between devices  20.4 us (1%)
  between operations  15.7 us (1%)
    pallas_call x1, Pallas kernels, ring_reduce(): pl.pallas_call(functools.partial(reduce_kernel, n, shard_lines), out_shap...  456 us
    pallas_call x1, Pallas kernels, ring_gather(): pl.pallas_call(functools.partial(gather_kernel, n, subs), out_shape=jax.S...  443 us
    pallas_call x10, Pallas kernels, sum_tensor(): pl.pallas_call(functools.partial(pair_kernel, parts), out_shape=jax.Shape...  168 us
    pallas_call x1, Pallas kernels, moments(): pl.pallas_call(functools.partial(moments_kernel, groups, shard), grid=(pl...  43.9 us
    dot_general x9, matrix products, mat_nt(): lax.dot_general(a, b, (((1,), (1,)), ((), ())), preferred_element_type=F32)  43.1 us
    dot_general x9, matrix products, mat_nn(): return jnp.dot(a, b, preferred_element_type=F32)  41.1 us
    pallas_call x1, Pallas kernels, scan_backward(): pl.pallas_call(functools.partial(adjoint_kernel, rows // SLOT), out_shape...  40.9 us
    unnamed x199, local copies, waits for them, and re-layouts  40.7 us
  transfers between devices with their start and end apart: 6, of which 2 were waited for; matrix products, arithmetic and copies ran while one was open for 4% of the time, Pallas kernels for 59%

profile of v5, /device:TPU:2, one launch (start us, length us, event | category | flops | bytes accessed | tf_op | source)
XLA Modules:
  0.0 1548.6 jit_solution(8289172054111143968)
XLA Ops:
  33.0 10.3 collective-permute-done.1
  43.3 10.0 pad_maximum_fusion.bottom_ref
  63.2 443.0 %ring_gather.1.src_ref = bf16[11264,2048]{1,0:T(8,128)(2,1)} custom-call(bf16[1408,2048]{1,0:T(8,128)(2,1)S(1)} %stack_own.1.own_ref), custom_call_target="tpu_custom_call" | custom-call | flops 1000000000 | bytes 1500000000 | tf_op jit(solution)/shard_map/ring_gather/pallas_call | solution.py:191
  529.6 8.1 sum_tensor.10
  541.9 10.3 change_rows.2
  555.7 11.3 scan_forward.1
  571.6 19.0 %sum_tensor.11 = bf16[256,2048]{1,0:T(8,128)(2,1)} custom-call(bf16[256,2048]{1,0:T(8,128)(2,1)} %fusion.29.x_ref), custom_call_target="tpu_custom_call" | custom-call | tf_op jit(solution)/shard_map/sum_tensor/pallas_call | solution.py:398
  606.1 18.9 %sum_tensor.12 = bf16[256,2048]{1,0:T(8,128)(2,1)} custom-call(bf16[256,2048]{1,0:T(8,128)(2,1)} %fusion.32.x_ref), custom_call_target="tpu_custom_call" | custom-call | tf_op jit(solution)/shard_map/sum_tensor/pallas_call | solution.py:398
  651.0 18.9 %sum_tensor.13 = bf16[256,2048]{1,0:T(8,128)(2,1)} custom-call(bf16[256,2048]{1,0:T(8,128)(2,1)} %convolution_convert_fusion.1.x_ref), custom_call_target="tpu_custom_call" | custom-call | tf_op jit(solution)/shard_map/sum_tensor/pallas_call | solution.py:398
  685.2 18.9 %sum_tensor.14 = bf16[256,2048]{1,0:T(8,128)(2,1)} custom-call(bf16[256,2048]{1,0:T(8,128)(2,1)} %fusion.35.x_ref), custom_call_target="tpu_custom_call" | custom-call | tf_op jit(solution)/shard_map/sum_tensor/pallas_call | solution.py:398
  716.5 18.9 %sum_tensor.15 = bf16[256,2048]{1,0:T(8,128)(2,1)} custom-call(bf16[256,2048]{1,0:T(8,128)(2,1)} %fusion.44.x_ref), custom_call_target="tpu_custom_call" | custom-call | tf_op jit(solution)/shard_map/sum_tensor/pallas_call | solution.py:398
  761.4 18.9 %sum_tensor.16 = bf16[256,2048]{1,0:T(8,128)(2,1)} custom-call(bf16[256,2048]{1,0:T(8,128)(2,1)} %convolution_convert_fusion.2.x_ref), custom_call_target="tpu_custom_call" | custom-call | tf_op jit(solution)/shard_map/sum_tensor/pallas_call | solution.py:398
  796.8 19.0 %sum_tensor.17 = bf16[256,2048]{1,0:T(8,128)(2,1)} custom-call(bf16[256,2048]{1,0:T(8,128)(2,1)} %fusion.41.x_ref), custom_call_target="tpu_custom_call" | custom-call | tf_op jit(solution)/shard_map/sum_tensor/pallas_call | solution.py:398
  824.9 40.9 %scan_backward.1 = (bf16[256,1024]{1,0:T(8,128)(2,1)}, f32[256,1024]{1,0:T(8,128)}, bf16[256,256]{1,0:T(8,128)(2,1)}, f32[128,1024]{1,0:T(8,128)}, f32[1,1024]{1...) custom-call(bf16[256,128]{1,0:T(8,128)(2,1)} %slice.306.proj_ref, f32[256,32]{1,0:T(8,128)} %slice_convert_fusion.bc_ref, ...), custom_call_target="tpu_custom_call" | custom-call | tf_op jit(solution)/shard_map/scan_backward/pallas_call | solution.py:634
  865.8 8.1 sum_tensor.18
  890.3 19.1 %sum_tensor.19 = bf16[256,2048]{1,0:T(8,128)(2,1)} custom-call(bf16[256,2048]{1,0:T(8,128)(2,1)} %fusion.38.x_ref), custom_call_target="tpu_custom_call" | custom-call | tf_op jit(solution)/shard_map/sum_tensor/pallas_call | solution.py:398
  933.7 8.0 copy.86.left_ref
  942.9 455.9 %ring_reduce.1 = f32[28985,1,128]{2,1,0:T(1,128)} custom-call(bf16[9728,256]{1,0:T(8,128)(2,1)} %copy.86.left_ref, bf16[7,256,2048]{2,1,0:T(8,128)(2,1)} %bitcast_dynamic-update-slice_fusion.right_refs, bf16[1536,2048]{1,0:T(8,128)(2,1)} %copy-done.2), custom_call_target="tpu_custom_call" | custom-call | flops 1000000000 | bytes 1500000000 | tf_op jit(solution)/shard_map/ring_reduce/pallas_call | solution.py:312
  1407.6 11.3 copy.144
  1418.9 10.1 collective-permute-done.2
  1429.0 8.0 fusion.100
  1441.2 43.9 %moments.1 = (f32[1,2923648]{1,0:T(1,128)}, f32[1,2923648]{1,0:T(1,128)}, f32[1,2923648]{1,0:T(1,128)}, f32[38]{0:T(128)S(1)}) custom-call(s32[38]{0:T(128)S(1)} %copy-done.4, f32[1,3710080]{1,0:T(1,128)} %bitcast.133, f32[1,2923648]{1,0:T(1,128)S(1)} %bitcast.128, f32[1,2923648]{1,0:T(1,128)} %one_ref.1, f32[1,2923648]{1,0:T(1,128)} %two_ref.1), custom_call_target="tpu_custom_call" | custom-call | tf_op jit(solution)/shard_map/moments/pallas_call | solution.py:1023
  1485.7 10.8 sum_everywhere.1
  1502.6 38.9 %update.1 = (f32[1,2923648]{1,0:T(1,128)}, bf16[1,2923648]{1,0:T(2,128)(2,1)}) custom-call(s32[38]{0:T(128)S(1)} %copy-done.4, f32[19]{0:T(128)S(1)} %fusion.127.trust_ref, f32[1,2923648]{1,0:T(1,128)S(1)} %copy-done.1, f32[1,2923648]{1,0:T(1,128)} %get-tuple-element.97.first_ref, f32[1,2923648]{1,0:T(1,128)} %get-tuple-element.98.second_ref), custom_call_target="tpu_custom_call" | custom-call | tf_op jit(solution)/shard_map/update/pallas_call | solution.py:1084
  (353 shorter events, 252.2 us)
Async XLA Ops:
  7.2 499.1 %all-reduce.11.cloned.1.call-start = ((), (), s32[]{:S(2)}) async-start(), calls=%async_computation | async-start | bytes 1282048 | tf_op jit(solution)/shard_map/psum | solution.py:1191
  8.1 22.5 %collective-permute-start = (f32[297,1,128]{2,1,0:T(1,128)S(1)}, f32[297,1,128]{2,1,0:T(1,128)S(1)}, u32[]{:S(2)}, u32[]{:S(2)}) collective-permute-start(f32[297,1,128]{2,1,0:T(1,128)S(1)} %slice_bitcast_fusion.3), channel_id=1, source_target_pairs={{0,4},{4,8},{8,12},{12,16},{16,20},{20,24},{24,28},{1,5},{5,9},{9,... | collective-permute-start | bytes 456200 | tf_op jit(solution)/shard_map/ppermute | solution.py:893
  13.6 29.7 %collective-permute-start.1 = (f32[1878,1,128]{2,1,0:T(1,128)}, f32[1878,1,128]{2,1,0:T(1,128)S(1)}, u32[]{:S(2)}, u32[]{:S(2)}) collective-permute-start(f32[1878,1,128]{2,1,0:T(1,128)} %slice_bitcast_fusion), channel_id=1, source_target_pairs={{4,0},{8,4},{12,8},{16,12},{20,16},{24,20},{28,24},{5,1},{9,5},{13... | collective-permute-start | bytes 2884616 | tf_op jit(solution)/shard_map/ppermute | solution.py:892
  26.9 1371.9 %all-reduce.13.cloned.1.call-start = ((), (), s32[]{:S(2)}) async-start(), calls=%async_computation.1 | async-start | bytes 1282048 | tf_op jit(solution)/shard_map/psum | solution.py:1211
  27.3 513.3 %copy-start.72 = (f32[256]{0:T(256)}, f32[256]{0:T(256)S(1)}, u32[]{:S(2)}) copy-start(f32[256]{0:T(256)S(1)} %add_rsqrt_fusion.3) | copy-start | bytes 3076
  517.7 81.3 %copy-start.54 = (f32[1,2048]{1,0:T(1,128)}, f32[1,2048]{1,0:T(1,128)S(1)}, u32[]{:S(2)}) copy-start(f32[1,2048]{1,0:T(1,128)S(1)} %get-tuple-element.155) | copy-start | bytes 24580
  571.5 20.7 %copy-start.27 = (bf16[256,1024]{1,0:T(8,128)(2,1)S(1)}, bf16[256,1024]{1,0:T(8,128)(2,1)}, u32[]{:S(2)}) copy-start(bf16[256,1024]{1,0:T(8,128)(2,1)} %scan_forward.1) | copy-start | bytes 1572868
  685.2 18.9 %copy-start.81 = (f32[256]{0:T(256)S(1)}, f32[256]{0:T(256)}, u32[]{:S(2)}) copy-start(f32[256]{0:T(256)} %fusion.134) | copy-start | bytes 3076
  716.5 19.0 %copy-start.57 = (f32[1,2048]{1,0:T(1,128)S(1)}, f32[1,2048]{1,0:T(1,128)}, u32[]{:S(2)}) copy-start(f32[1,2048]{1,0:T(1,128)} %get-tuple-element.153) | copy-start | bytes 24580
  716.5 19.0 %copy-start.77 = (f32[256]{0:T(256)S(1)}, f32[256]{0:T(256)}, u32[]{:S(2)}) copy-start(f32[256]{0:T(256)} %copy-done.76) | copy-start | bytes 3076
  796.8 19.0 %copy-start.7 = (bf16[256,2048]{1,0:T(8,128)(2,1)S(1)}, bf16[256,2048]{1,0:T(8,128)(2,1)}, u32[]{:S(2)}) copy-start(bf16[256,2048]{1,0:T(8,128)(2,1)} %sum_tensor.11) | copy-start | bytes 3145732
  796.8 19.0 %copy-start.55 = (f32[1,2048]{1,0:T(1,128)S(1)}, f32[1,2048]{1,0:T(1,128)}, u32[]{:S(2)}) copy-start(f32[1,2048]{1,0:T(1,128)} %copy-done.54) | copy-start | bytes 24580
  796.8 19.0 %copy-start.75 = (f32[256]{0:T(256)S(1)}, f32[256]{0:T(256)}, u32[]{:S(2)}) copy-start(f32[256]{0:T(256)} %copy-done.74) | copy-start | bytes 3076
  824.8 49.0 %copy-start.19 = (bf16[2,128,1024]{2,1,0:T(8,128)(2,1)S(1)}, bf16[2,128,1024]{2,1,0:T(8,128)(2,1)}, u32[]{:S(2)}) copy-start(bf16[2,128,1024]{2,1,0:T(8,128)(2,1)} %copy-done.18) | copy-start | bytes 1572868
  824.9 50.2 %copy-start.24 = (f32[256,1024]{1,0:T(8,128)S(1)}, f32[256,1024]{1,0:T(8,128)}, u32[]{:S(2)}) copy-start(f32[256,1024]{1,0:T(8,128)} %copy-done.23) | copy-start | bytes 3145732
  824.9 50.3 %copy-start.33 = (bf16[1024,160]{1,0:T(8,128)(2,1)S(1)}, bf16[1024,160]{1,0:T(8,128)(2,1)}, u32[]{:S(2)}) copy-start(bf16[1024,160]{1,0:T(8,128)(2,1)} %copy-done.32) | copy-start | bytes 983044
  888.6 20.9 %copy-start.73 = (f32[256]{0:T(256)S(1)}, f32[256]{0:T(256)}, u32[]{:S(2)}) copy-start(f32[256]{0:T(256)} %copy-done.72) | copy-start | bytes 3076
  890.3 21.2 %copy-start.69 = (f32[2048]{0:T(1024)S(1)}, f32[2048]{0:T(1024)}, u32[]{:S(2)}) copy-start(f32[2048]{0:T(1024)} %get-tuple-element.106) | copy-start | bytes 24580
  890.3 21.9 %copy-start.17 = (f32[256,2048]{1,0:T(8,128)S(1)}, f32[256,2048]{1,0:T(8,128)}, u32[]{:S(2)}) copy-start(f32[256,2048]{1,0:T(8,128)} %copy-done.16) | copy-start | bytes 6291460
  1401.1 27.9 %collective-permute-start.2 = (f32[1878,1,128]{2,1,0:T(1,128)S(1)}, f32[1878,1,128]{2,1,0:T(1,128)S(1)}, u32[]{:S(2)}, u32[]{:S(2)}) collective-permute-start(f32[1878,1,128]{2,1,0:T(1,128)S(1)} %slice.341), channel_id=1, source_target_pairs={{0,4},{4,8},{8,12},{12,16},{16,20},{20,24},{24,28},{1,5},{5,9},{9,... | collective-permute-start | bytes 2884616 | tf_op jit(solution)/shard_map/ppermute | solution.py:1227
  1404.7 36.5 %slice-start = ((s8[11694592]{0:T(1024)(128)(4,1)}), s8[4194304]{0:T(1024)(128)(4,1)S(1)}, s32[]{:S(2)}) async-start(s8[11694592]{0:T(1024)(128)(4,1)} %bitcast.127), calls=%async_computation.2 | async-start | bytes 8388608
  1404.8 36.4 %slice-start.1 = ((s8[11694592]{0:T(1024)(128)(4,1)}), s8[4194304]{0:T(1024)(128)(4,1)S(1)}, s32[]{:S(2)}) async-start(s8[11694592]{0:T(1024)(128)(4,1)} %bitcast.127), calls=%async_computation.3 | async-start | bytes 8388608
  1404.8 36.4 %slice-start.2 = ((s8[11694592]{0:T(1024)(128)(4,1)}), s8[3305984]{0:T(1024)(128)(4,1)S(1)}, s32[]{:S(2)}) async-start(s8[11694592]{0:T(1024)(128)(4,1)} %bitcast.127), calls=%async_computation.4 | async-start | bytes 6612992
  1404.9 32.2 %collective-permute-start.3 = (f32[297,1,128]{2,1,0:T(1,128)S(1)}, f32[297,1,128]{2,1,0:T(1,128)S(1)}, u32[]{:S(2)}, u32[]{:S(2)}) collective-permute-start(f32[297,1,128]{2,1,0:T(1,128)S(1)} %slice.342), channel_id=1, source_target_pairs={{4,0},{8,4},{12,8},{16,12},{20,16},{24,20},{28,24},{5,1},{9,5},{13... | collective-permute-start | bytes 456200 | tf_op jit(solution)/shard_map/ppermute | solution.py:1228
  (77 other events, 300.0 us)
Sparse Core Ops, SparseCore 0:
  27.1 80.2 all-reduce.10
  920.0 76.9 all-reduce.12

commit v6 on v5

--- a/solution.py
+++ b/solution.py
@@ -391,7 +391,7 @@
 
 def sum_tensor(value):
     rows, cols = value.shape
-    parts = 4 if cols >= 1024 else 1
+    parts = 8 if cols >= 1024 else 1
     vm = pl.BlockSpec(memory_space=pltpu.VMEM)
     dma = pltpu.SemaphoreType.DMA
     part = pltpu.VMEM((rows // 2, cols), BF)
@@ -768,8 +768,9 @@
     attended = attended.reshape(rows, HW).astype(BF)
     x3 = x2 + total(mat_nn(attended, w["w_o"]))
     h4 = (rms_parts(x3, 0)[1] * gains[3]).astype(BF)
-    branch, pre2, act2 = ffn_forward(h4, w["w_gu2"], w["w_down2"])
-    x4 = x3 + branch
+    pre2 = mat_nn(h4, w["w_gu2"])
+    act2 = (silu(pre2[:, :FI]) * pre2[:, FI:]).astype(BF)
+    last = mat_nn(act2, w["w_down2"]).astype(BF)
 
     gb4 = grad_out.astype(BF)
     gh, gp2 = ffn_backward(pre2, w["w_gu2"], w["w_down2"], gb4)
@@ -820,8 +821,8 @@
     g_gain = lax.dynamic_slice_in_dim(jnp.stack([gg1, gg2, gg3, gg4]), start, DG, 1)
     pieces = [g_gain, g_conv_w, g_conv_b, g_bias, g_skip, g_alog, g_wx, g_dt]
     small_grads = jnp.concatenate([p.reshape(-1, LANES).astype(BF) for p in pieces])
-    g0, small_grads, left_t = lax.optimization_barrier((g0, small_grads, left_t))
-    return x4.astype(BF), g0, (left_t, rights, g_qkv), small_grads
+    g0, small_grads, last, left_t = lax.optimization_barrier((g0, small_grads, last, left_t))
+    return x3, last, g0, (left_t, rights, g_qkv), small_grads
 
 
 def extents(n, shard_rows):
@@ -1207,10 +1208,12 @@
     pos = lax.broadcasted_iota(jnp.int32, (tokens.shape[0] // SLOT, SLOT), 1)
     valid = (pos < lengths[:, None]).astype(F32).reshape(-1, 1)
     grad = cotangent.astype(F32) * valid
-    out, grad_in, operands, small_grads = layer(x, grad, w, small, gains, n)
+    x3, last, grad_in, operands, small_grads = layer(x, grad, w, small, gains, n)
     small_sum = lax.psum(small_grads, "dp")
     laid = ring_reduce(*operands, n, lines)
-    laid, small_sum = lax.optimization_barrier((laid, small_sum))
+    branch = lax.psum(last, "tensor")
+    laid, small_sum, branch = lax.optimization_barrier((laid, small_sum, branch))
+    out = (x3 + branch.astype(F32)).astype(BF)
     small_sum = small_sum.astype(F32).reshape(-1, 1, LANES)
 
     before, after = extents(n, lines)

time: 1560 us -> 1560 us (level)
    pallas_call x10 -> x9, Pallas kernels: 168 us -> 149 us  [sum_tensor(): pl.pallas_call(functools.partial(pair_kernel, parts), out_shape=jax.Shape...]
    unnamed x199 -> x205, local copies, waits for them, and re-layouts: 40.7 us -> 48.2 us
  transfers between devices with their start and end apart: 6 -> 7, of which waited for: 2 -> 2; matrix products, arithmetic and copies ran while one was open for 4% -> 4% of each run, Pallas kernels for 59% -> 59%
where the time goes in v6:
time: 1560 us; the launch traced here: 1550 us
  Pallas kernels  1230 us (79%)
  matrix products  101 us (6%)
  local copies, waits for them, and re-layouts  91.7 us (6%)
  other arithmetic  76.4 us (5%)
  blocking collectives  16.5 us (1%)
    pallas_call x1, Pallas kernels, ring_reduce(): pl.pallas_call(functools.partial(reduce_kernel, n, shard_lines), out_shap...  465 us
    pallas_call x1, Pallas kernels, ring_gather(): pl.pallas_call(functools.partial(gather_kernel, n, subs), out_shape=jax.S...  443 us
    pallas_call x9, Pallas kernels, sum_tensor(): pl.pallas_call(functools.partial(pair_kernel, parts), out_shape=jax.Shape...  149 us
    unnamed x205, local copies, waits for them, and re-layouts  48.2 us
    dot_general x9, matrix products, mat_nt(): lax.dot_general(a, b, (((1,), (1,)), ((), ())), preferred_element_type=F32)  45.1 us
    pallas_call x1, Pallas kernels, moments(): pl.pallas_call(functools.partial(moments_kernel, groups, shard), grid=(pl...  43.9 us
    dot_general x9, matrix products, mat_nn(): return jnp.dot(a, b, preferred_element_type=F32)  41.8 us
    pallas_call x1, Pallas kernels, scan_backward(): pl.pallas_call(functools.partial(adjoint_kernel, rows // SLOT), out_shape...  40.8 us
  transfers between devices with their start and end apart: 7, of which 2 were waited for; matrix products, arithmetic and copies ran while one was open for 4% of the time, Pallas kernels for 59%

profile of v6, /device:TPU:2, one launch (start us, length us, event | category | flops | bytes accessed | tf_op | source)
XLA Modules:
  0.0 1553.5 jit_solution(12909721645384080346)
XLA Ops:
  33.9 9.4 collective-permute-done.1
  43.3 10.0 pad_maximum_fusion.bottom_ref
  63.3 443.0 %ring_gather.1.src_ref = bf16[11264,2048]{1,0:T(8,128)(2,1)} custom-call(bf16[1408,2048]{1,0:T(8,128)(2,1)S(1)} %stack_own.1.own_ref), custom_call_target="tpu_custom_call" | custom-call | flops 1000000000 | bytes 1500000000 | tf_op jit(solution)/shard_map/ring_gather/pallas_call | solution.py:191
  509.0 16.5 %all_gather.3 = bf16[4,2048]{1,0:T(4,128)(2,1)S(1)} all-gather(bf16[4,512]{1,0:T(4,128)(2,1)S(1)} %reshape.411), channel_id=1, replica_groups=mesh['dp'=8,'tensor'=4] {'tensor'}, dimensions={1}, use_global_device_ids=true | all-gather | bytes 20480 | tf_op jit(solution)/shard_map/all_gather | solution.py:1195
  537.5 8.1 sum_tensor.9
  550.0 10.3 change_rows.2
  563.8 11.2 scan_forward.1
  580.5 19.0 %sum_tensor.10 = bf16[256,2048]{1,0:T(8,128)(2,1)} custom-call(bf16[256,2048]{1,0:T(8,128)(2,1)} %fusion.29.x_ref), custom_call_target="tpu_custom_call" | custom-call | tf_op jit(solution)/shard_map/sum_tensor/pallas_call | solution.py:398
  614.2 18.9 %sum_tensor.11 = bf16[256,2048]{1,0:T(8,128)(2,1)} custom-call(bf16[256,2048]{1,0:T(8,128)(2,1)} %fusion.32.x_ref), custom_call_target="tpu_custom_call" | custom-call | tf_op jit(solution)/shard_map/sum_tensor/pallas_call | solution.py:398
  657.5 19.0 %sum_tensor.12 = bf16[256,2048]{1,0:T(8,128)(2,1)} custom-call(bf16[256,2048]{1,0:T(8,128)(2,1)} %convolution_convert_fusion.1.x_ref), custom_call_target="tpu_custom_call" | custom-call | tf_op jit(solution)/shard_map/sum_tensor/pallas_call | solution.py:398
  690.3 6.8 fusion.44.x_ref
  697.1 19.0 %sum_tensor.13 = bf16[256,2048]{1,0:T(8,128)(2,1)} custom-call(bf16[256,2048]{1,0:T(8,128)(2,1)} %fusion.44.x_ref), custom_call_target="tpu_custom_call" | custom-call | tf_op jit(solution)/shard_map/sum_tensor/pallas_call | solution.py:398
  740.0 18.9 %sum_tensor.14 = bf16[256,2048]{1,0:T(8,128)(2,1)} custom-call(bf16[256,2048]{1,0:T(8,128)(2,1)} %convolution_convert_fusion.2.x_ref), custom_call_target="tpu_custom_call" | custom-call | tf_op jit(solution)/shard_map/sum_tensor/pallas_call | solution.py:398
  775.1 18.9 %sum_tensor.15 = bf16[256,2048]{1,0:T(8,128)(2,1)} custom-call(bf16[256,2048]{1,0:T(8,128)(2,1)} %fusion.41.x_ref), custom_call_target="tpu_custom_call" | custom-call | tf_op jit(solution)/shard_map/sum_tensor/pallas_call | solution.py:398
  805.0 40.8 %scan_backward.1 = (bf16[256,1024]{1,0:T(8,128)(2,1)}, f32[256,1024]{1,0:T(8,128)}, bf16[256,256]{1,0:T(8,128)(2,1)}, f32[128,1024]{1,0:T(8,128)}, f32[1,1024]{1...) custom-call(bf16[256,128]{1,0:T(8,128)(2,1)} %slice.306.proj_ref, f32[256,32]{1,0:T(8,128)} %slice_convert_fusion.bc_ref, ...), custom_call_target="tpu_custom_call" | custom-call | tf_op jit(solution)/shard_map/scan_backward/pallas_call | solution.py:634
  845.7 8.1 sum_tensor.16
  873.5 19.1 %sum_tensor.17 = bf16[256,2048]{1,0:T(8,128)(2,1)} custom-call(bf16[256,2048]{1,0:T(8,128)(2,1)} %fusion.38.x_ref), custom_call_target="tpu_custom_call" | custom-call | tf_op jit(solution)/shard_map/sum_tensor/pallas_call | solution.py:398
  920.7 7.9 copy.86.left_ref
  938.7 465.1 %ring_reduce.1 = f32[28985,1,128]{2,1,0:T(1,128)} custom-call(bf16[9728,256]{1,0:T(8,128)(2,1)} %copy.86.left_ref, bf16[7,256,2048]{2,1,0:T(8,128)(2,1)} %bitcast_dynamic-update-slice_fusion.right_refs, bf16[1536,2048]{1,0:T(8,128)(2,1)} %copy-done.3), custom_call_target="tpu_custom_call" | custom-call | flops 1000000000 | bytes 1500000000 | tf_op jit(solution)/shard_map/ring_reduce/pallas_call | solution.py:312
  1409.7 15.2 copy.145
  1434.2 8.0 fusion.100
  1446.4 43.9 %moments.1 = (f32[1,2923648]{1,0:T(1,128)}, f32[1,2923648]{1,0:T(1,128)}, f32[1,2923648]{1,0:T(1,128)}, f32[38]{0:T(128)S(1)}) custom-call(s32[38]{0:T(128)S(1)} %copy-done.5, f32[1,3710080]{1,0:T(1,128)} %bitcast.131, f32[1,2923648]{1,0:T(1,128)S(1)} %bitcast.128, f32[1,2923648]{1,0:T(1,128)} %one_ref.1, f32[1,2923648]{1,0:T(1,128)} %two_ref.1), custom_call_target="tpu_custom_call" | custom-call | tf_op jit(solution)/shard_map/moments/pallas_call | solution.py:1024
  1490.9 10.9 sum_everywhere.1
  1507.9 38.9 %update.1 = (f32[1,2923648]{1,0:T(1,128)}, bf16[1,2923648]{1,0:T(2,128)(2,1)}) custom-call(s32[38]{0:T(128)S(1)} %copy-done.5, f32[19]{0:T(128)S(1)} %fusion.127.trust_ref, f32[1,2923648]{1,0:T(1,128)S(1)} %copy-done.1, f32[1,2923648]{1,0:T(1,128)} %get-tuple-element.101.first_ref, f32[1,2923648]{1,0:T(1,128)} %get-tuple-element.102.second_ref), custom_call_target="tpu_custom_call" | custom-call | tf_op jit(solution)/shard_map/update/pallas_call | solution.py:1085
  (362 shorter events, 251.2 us)
Async XLA Ops:
  7.2 499.1 %all-reduce.12.cloned.1.call-start = ((), (), s32[]{:S(2)}) async-start(), calls=%async_computation | async-start | bytes 1282048 | tf_op jit(solution)/shard_map/psum | solution.py:1192
  8.1 23.1 %collective-permute-start = (f32[297,1,128]{2,1,0:T(1,128)S(1)}, f32[297,1,128]{2,1,0:T(1,128)}, u32[]{:S(2)}, u32[]{:S(2)}) collective-permute-start(f32[297,1,128]{2,1,0:T(1,128)S(1)} %slice_bitcast_fusion.3), channel_id=1, source_target_pairs={{0,4},{4,8},{8,12},{12,16},{16,20},{20,24},{24,28},{1,5},{5,9},{9,... | collective-permute-start | bytes 456200 | tf_op jit(solution)/shard_map/ppermute | solution.py:894
  13.6 29.7 %collective-permute-start.1 = (f32[1878,1,128]{2,1,0:T(1,128)}, f32[1878,1,128]{2,1,0:T(1,128)S(1)}, u32[]{:S(2)}, u32[]{:S(2)}) collective-permute-start(f32[1878,1,128]{2,1,0:T(1,128)} %slice_bitcast_fusion), channel_id=1, source_target_pairs={{4,0},{8,4},{12,8},{16,12},{20,16},{24,20},{28,24},{5,1},{9,5},{13... | collective-permute-start | bytes 2884616 | tf_op jit(solution)/shard_map/ppermute | solution.py:893
  27.6 1376.3 %all-reduce.16.cloned.1.call-start = ((), (), s32[]{:S(2)}) async-start(), calls=%async_computation.2 | async-start | bytes 2097152 | tf_op jit(solution)/shard_map/psum | solution.py:1214
  27.9 498.8 %copy-start.76 = (f32[256]{0:T(256)}, f32[256]{0:T(256)S(1)}, u32[]{:S(2)}) copy-start(f32[256]{0:T(256)S(1)} %add_rsqrt_fusion.3) | copy-start | bytes 3076
  525.4 7.1 copy-start.58
  525.5 81.6 %copy-start.60 = (f32[1,2048]{1,0:T(1,128)}, f32[1,2048]{1,0:T(1,128)S(1)}, u32[]{:S(2)}) copy-start(f32[1,2048]{1,0:T(1,128)S(1)} %get-tuple-element.157) | copy-start | bytes 24580
  536.4 23.9 %copy-start.22 = (bf16[2,128,1024]{2,1,0:T(8,128)(2,1)}, bf16[2,128,1024]{2,1,0:T(8,128)(2,1)S(1)}, u32[]{:S(2)}) copy-start(bf16[2,128,1024]{2,1,0:T(8,128)(2,1)S(1)} %get-tuple-element.128) | copy-start | bytes 1572868
  550.0 13.0 slice-start.6
  740.0 18.9 %copy-start.75 = (f32[256]{0:T(256)S(1)}, f32[256]{0:T(256)}, u32[]{:S(2)}) copy-start(f32[256]{0:T(256)} %copy-done.74) | copy-start | bytes 3076
  775.1 19.0 %copy-start.61 = (f32[1,2048]{1,0:T(1,128)S(1)}, f32[1,2048]{1,0:T(1,128)}, u32[]{:S(2)}) copy-start(f32[1,2048]{1,0:T(1,128)} %copy-done.60) | copy-start | bytes 24580
  775.1 19.0 %copy-start.82 = (f32[256]{0:T(256)S(1)}, f32[256]{0:T(256)}, u32[]{:S(2)}) copy-start(f32[256]{0:T(256)} %copy-done.81) | copy-start | bytes 3076
  868.8 23.8 %copy-start.59 = (f32[1,2048]{1,0:T(1,128)S(1)}, f32[1,2048]{1,0:T(1,128)}, u32[]{:S(2)}) copy-start(f32[1,2048]{1,0:T(1,128)} %copy-done.58) | copy-start | bytes 24580
  868.8 23.8 %copy-start.77 = (f32[256]{0:T(256)S(1)}, f32[256]{0:T(256)}, u32[]{:S(2)}) copy-start(f32[256]{0:T(256)} %copy-done.76) | copy-start | bytes 3076
  873.5 21.3 %copy-start.20 = (f32[256,2048]{1,0:T(8,128)S(1)}, f32[256,2048]{1,0:T(8,128)}, u32[]{:S(2)}) copy-start(f32[256,2048]{1,0:T(8,128)} %copy-done.19) | copy-start | bytes 6291460
  904.3 9.0 copy-start.21
  917.6 486.2 %all-reduce.14.cloned.1.call-start = ((), (), s32[]{:S(2)}) async-start(), calls=%async_computation.1 | async-start | bytes 1282048 | tf_op jit(solution)/shard_map/psum | solution.py:1212
  1406.1 28.1 %collective-permute-start.2 = (f32[1878,1,128]{2,1,0:T(1,128)S(1)}, f32[1878,1,128]{2,1,0:T(1,128)S(1)}, u32[]{:S(2)}, u32[]{:S(2)}) collective-permute-start(f32[1878,1,128]{2,1,0:T(1,128)S(1)} %slice.341), channel_id=1, source_target_pairs={{0,4},{4,8},{8,12},{12,16},{16,20},{20,24},{24,28},{1,5},{5,9},{9,... | collective-permute-start | bytes 2884616 | tf_op jit(solution)/shard_map/ppermute | solution.py:1230
  1409.6 36.8 %slice-start = ((s8[11694592]{0:T(1024)(128)(4,1)}), s8[4194304]{0:T(1024)(128)(4,1)S(1)}, s32[]{:S(2)}) async-start(s8[11694592]{0:T(1024)(128)(4,1)} %bitcast.127), calls=%async_computation.3 | async-start | bytes 8388608
  1409.7 17.8 %copy-start.10 = (f32[256,2048]{1,0:T(8,128)S(1)}, f32[256,2048]{1,0:T(8,128)}, u32[]{:S(2)}) copy-start(f32[256,2048]{1,0:T(8,128)} %copy-done.7) | copy-start | bytes 6291460
  1409.7 17.8 %copy-start.40 = (bf16[256,2048]{1,0:T(8,128)(2,1)S(1)}, bf16[256,2048]{1,0:T(8,128)(2,1)}, u32[]{:S(2)}) copy-start(bf16[256,2048]{1,0:T(8,128)(2,1)} %all-reduce.16.cloned.1.call-done) | copy-start | bytes 3145732
  1409.7 36.8 %slice-start.1 = ((s8[11694592]{0:T(1024)(128)(4,1)}), s8[4194304]{0:T(1024)(128)(4,1)S(1)}, s32[]{:S(2)}) async-start(s8[11694592]{0:T(1024)(128)(4,1)} %bitcast.127), calls=%async_computation.4 | async-start | bytes 8388608
  1409.7 36.7 %slice-start.2 = ((s8[11694592]{0:T(1024)(128)(4,1)}), s8[3305984]{0:T(1024)(128)(4,1)S(1)}, s32[]{:S(2)}) async-start(s8[11694592]{0:T(1024)(128)(4,1)} %bitcast.127), calls=%async_computation.5 | async-start | bytes 6612992
  1425.0 17.3 %collective-permute-start.3 = (f32[297,1,128]{2,1,0:T(1,128)S(1)}, f32[297,1,128]{2,1,0:T(1,128)S(1)}, u32[]{:S(2)}, u32[]{:S(2)}) collective-permute-start(f32[297,1,128]{2,1,0:T(1,128)S(1)} %slice.342), channel_id=1, source_target_pairs={{4,0},{8,4},{12,8},{16,12},{20,16},{24,20},{28,24},{5,1},{9,5},{13... | collective-permute-start | bytes 456200 | tf_op jit(solution)/shard_map/ppermute | solution.py:1231
  (82 other events, 262.2 us)
Sparse Core Ops, SparseCore 0:
  27.7 79.5 all-reduce.11
  917.7 36.0 all-reduce.15
  957.3 82.7 all-reduce.13

commit v7 on v6

--- a/solution.py
+++ b/solution.py
@@ -69,7 +69,7 @@
 LINES = D // LANES
 FIRST = BIG_OFF["w_out"] * LINES
 LEAD = GAIN_ROWS
-CHUNK = 1024
+CHUNK = 2048
 SLACK = -(-(SMALL_ROWS + GAIN_ROWS) // CHUNK) * CHUNK
 
 

time: 1560 us -> 1560 us (level)
  no operation moved by 1% of the time
where the time goes in v7:
time: 1560 us; the launch traced here: 1550 us
  Pallas kernels  1230 us (79%)
  local copies, waits for them, and re-layouts  101 us (6%)
  matrix products  101 us (6%)
  other arithmetic  76.4 us (5%)
  between operations  15.7 us (1%)
    pallas_call x1, Pallas kernels, ring_reduce(): pl.pallas_call(functools.partial(reduce_kernel, n, shard_lines), out_shap...  465 us
    pallas_call x1, Pallas kernels, ring_gather(): pl.pallas_call(functools.partial(gather_kernel, n, subs), out_shape=jax.S...  443 us
    pallas_call x9, Pallas kernels, sum_tensor(): pl.pallas_call(functools.partial(pair_kernel, parts), out_shape=jax.Shape...  149 us
    unnamed x205, local copies, waits for them, and re-layouts  49.1 us
    pallas_call x1, Pallas kernels, moments(): pl.pallas_call(functools.partial(moments_kernel, groups, shard), grid=(pl...  46.7 us
    dot_general x9, matrix products, mat_nt(): lax.dot_general(a, b, (((1,), (1,)), ((), ())), preferred_element_type=F32)  44.9 us
    dot_general x9, matrix products, mat_nn(): return jnp.dot(a, b, preferred_element_type=F32)  41.8 us
    pallas_call x1, Pallas kernels, scan_backward(): pl.pallas_call(functools.partial(adjoint_kernel, rows // SLOT), out_shape...  40.8 us
  transfers between devices with their start and end apart: 7, of which 2 were waited for; matrix products, arithmetic and copies ran while one was open for 4% of the time, Pallas kernels for 59%

profile of v7, /device:TPU:2, one launch (start us, length us, event | category | flops | bytes accessed | tf_op | source)
XLA Modules:
  0.0 1554.4 jit_solution(1703203198762346965)
XLA Ops:
  33.9 9.4 collective-permute-done.1
  43.3 10.0 pad_maximum_fusion.bottom_ref
  63.3 443.0 %ring_gather.1.src_ref = bf16[11264,2048]{1,0:T(8,128)(2,1)} custom-call(bf16[1408,2048]{1,0:T(8,128)(2,1)S(1)} %stack_own.1.own_ref), custom_call_target="tpu_custom_call" | custom-call | flops 1000000000 | bytes 1500000000 | tf_op jit(solution)/shard_map/ring_gather/pallas_call | solution.py:191
  526.5 8.1 sum_tensor.9
  539.0 10.3 change_rows.2
  552.8 11.2 scan_forward.1
  569.5 19.0 %sum_tensor.10 = bf16[256,2048]{1,0:T(8,128)(2,1)} custom-call(bf16[256,2048]{1,0:T(8,128)(2,1)} %fusion.29.x_ref), custom_call_target="tpu_custom_call" | custom-call | tf_op jit(solution)/shard_map/sum_tensor/pallas_call | solution.py:398
  603.2 18.9 %sum_tensor.11 = bf16[256,2048]{1,0:T(8,128)(2,1)} custom-call(bf16[256,2048]{1,0:T(8,128)(2,1)} %fusion.32.x_ref), custom_call_target="tpu_custom_call" | custom-call | tf_op jit(solution)/shard_map/sum_tensor/pallas_call | solution.py:398
  630.8 11.4 reshape.416
  654.6 19.0 %sum_tensor.12 = bf16[256,2048]{1,0:T(8,128)(2,1)} custom-call(bf16[256,2048]{1,0:T(8,128)(2,1)} %convolution_convert_fusion.1.x_ref), custom_call_target="tpu_custom_call" | custom-call | tf_op jit(solution)/shard_map/sum_tensor/pallas_call | solution.py:398
  687.4 6.8 fusion.44.x_ref
  694.2 19.0 %sum_tensor.13 = bf16[256,2048]{1,0:T(8,128)(2,1)} custom-call(bf16[256,2048]{1,0:T(8,128)(2,1)} %fusion.44.x_ref), custom_call_target="tpu_custom_call" | custom-call | tf_op jit(solution)/shard_map/sum_tensor/pallas_call | solution.py:398
  737.4 18.9 %sum_tensor.14 = bf16[256,2048]{1,0:T(8,128)(2,1)} custom-call(bf16[256,2048]{1,0:T(8,128)(2,1)} %convolution_convert_fusion.2.x_ref), custom_call_target="tpu_custom_call" | custom-call | tf_op jit(solution)/shard_map/sum_tensor/pallas_call | solution.py:398
  772.5 18.9 %sum_tensor.15 = bf16[256,2048]{1,0:T(8,128)(2,1)} custom-call(bf16[256,2048]{1,0:T(8,128)(2,1)} %fusion.41.x_ref), custom_call_target="tpu_custom_call" | custom-call | tf_op jit(solution)/shard_map/sum_tensor/pallas_call | solution.py:398
  802.2 40.8 %scan_backward.1 = (bf16[256,1024]{1,0:T(8,128)(2,1)}, f32[256,1024]{1,0:T(8,128)}, bf16[256,256]{1,0:T(8,128)(2,1)}, f32[128,1024]{1,0:T(8,128)}, f32[1,1024]{1...) custom-call(bf16[256,128]{1,0:T(8,128)(2,1)} %slice.306.proj_ref, f32[256,32]{1,0:T(8,128)} %slice_convert_fusion.bc_ref, ...), custom_call_target="tpu_custom_call" | custom-call | tf_op jit(solution)/shard_map/scan_backward/pallas_call | solution.py:634
  842.9 8.1 sum_tensor.16
  870.7 19.1 %sum_tensor.17 = bf16[256,2048]{1,0:T(8,128)(2,1)} custom-call(bf16[256,2048]{1,0:T(8,128)(2,1)} %fusion.38.x_ref), custom_call_target="tpu_custom_call" | custom-call | tf_op jit(solution)/shard_map/sum_tensor/pallas_call | solution.py:398
  917.9 7.9 copy.86.left_ref
  935.9 465.1 %ring_reduce.1 = f32[31033,1,128]{2,1,0:T(1,128)} custom-call(bf16[9728,256]{1,0:T(8,128)(2,1)} %copy.86.left_ref, bf16[7,256,2048]{2,1,0:T(8,128)(2,1)} %bitcast_dynamic-update-slice_fusion.right_refs, bf16[1536,2048]{1,0:T(8,128)(2,1)} %copy-done.3), custom_call_target="tpu_custom_call" | custom-call | flops 1000000000 | bytes 1500000000 | tf_op jit(solution)/shard_map/ring_reduce/pallas_call | solution.py:312
  1406.9 16.1 %copy.145 = f32[31033,1,128]{2,1,0:T(1,128)} copy(f32[31033,1,128]{2,1,0:T(1,128)} %ring_reduce.1) | data formatting | bytes 31777792
  1431.4 8.0 fusion.100
  1443.7 46.7 %moments.1 = (f32[1,2923648]{1,0:T(1,128)}, f32[1,2923648]{1,0:T(1,128)}, f32[1,2923648]{1,0:T(1,128)}, f32[38]{0:T(128)S(1)}) custom-call(s32[38]{0:T(128)S(1)} %copy-done.5, f32[1,3972224]{1,0:T(1,128)} %bitcast.131, f32[1,2923648]{1,0:T(1,128)S(1)} %bitcast.128, f32[1,2923648]{1,0:T(1,128)} %one_ref.1, f32[1,2923648]{1,0:T(1,128)} %two_ref.1), custom_call_target="tpu_custom_call" | custom-call | tf_op jit(solution)/shard_map/moments/pallas_call | solution.py:1024
  1491.0 11.0 sum_everywhere.1
  1508.1 39.4 %update.1 = (f32[1,2923648]{1,0:T(1,128)}, bf16[1,2923648]{1,0:T(2,128)(2,1)}) custom-call(s32[38]{0:T(128)S(1)} %copy-done.5, f32[19]{0:T(128)S(1)} %fusion.127.trust_ref, f32[1,2923648]{1,0:T(1,128)S(1)} %copy-done.1, f32[1,2923648]{1,0:T(1,128)} %get-tuple-element.101.first_ref, f32[1,2923648]{1,0:T(1,128)} %get-tuple-element.102.second_ref), custom_call_target="tpu_custom_call" | custom-call | tf_op jit(solution)/shard_map/update/pallas_call | solution.py:1085
  (362 shorter events, 252.6 us)
Async XLA Ops:
  7.2 499.1 %all-reduce.12.cloned.1.call-start = ((), (), s32[]{:S(2)}) async-start(), calls=%async_computation | async-start | bytes 1282048 | tf_op jit(solution)/shard_map/psum | solution.py:1192
  8.1 23.1 %collective-permute-start = (f32[297,1,128]{2,1,0:T(1,128)S(1)}, f32[297,1,128]{2,1,0:T(1,128)}, u32[]{:S(2)}, u32[]{:S(2)}) collective-permute-start(f32[297,1,128]{2,1,0:T(1,128)S(1)} %slice_bitcast_fusion.3), channel_id=1, source_target_pairs={{0,4},{4,8},{8,12},{12,16},{16,20},{20,24},{24,28},{1,5},{5,9},{9,... | collective-permute-start | bytes 456200 | tf_op jit(solution)/shard_map/ppermute | solution.py:894
  13.6 29.7 %collective-permute-start.1 = (f32[1878,1,128]{2,1,0:T(1,128)}, f32[1878,1,128]{2,1,0:T(1,128)S(1)}, u32[]{:S(2)}, u32[]{:S(2)}) collective-permute-start(f32[1878,1,128]{2,1,0:T(1,128)} %slice_bitcast_fusion), channel_id=1, source_target_pairs={{4,0},{8,4},{12,8},{16,12},{20,16},{24,20},{28,24},{5,1},{9,5},{13... | collective-permute-start | bytes 2884616 | tf_op jit(solution)/shard_map/ppermute | solution.py:893
  27.6 1373.5 %all-reduce.16.cloned.1.call-start = ((), (), s32[]{:S(2)}) async-start(), calls=%async_computation.2 | async-start | bytes 2097152 | tf_op jit(solution)/shard_map/psum | solution.py:1214
  27.9 487.8 %copy-start.76 = (f32[256]{0:T(256)}, f32[256]{0:T(256)S(1)}, u32[]{:S(2)}) copy-start(f32[256]{0:T(256)S(1)} %add_rsqrt_fusion.3) | copy-start | bytes 3076
  514.4 7.1 copy-start.58
  514.5 81.6 %copy-start.60 = (f32[1,2048]{1,0:T(1,128)}, f32[1,2048]{1,0:T(1,128)S(1)}, u32[]{:S(2)}) copy-start(f32[1,2048]{1,0:T(1,128)S(1)} %get-tuple-element.157) | copy-start | bytes 24580
  525.4 23.9 %copy-start.22 = (bf16[2,128,1024]{2,1,0:T(8,128)(2,1)}, bf16[2,128,1024]{2,1,0:T(8,128)(2,1)S(1)}, u32[]{:S(2)}) copy-start(bf16[2,128,1024]{2,1,0:T(8,128)(2,1)S(1)} %get-tuple-element.128) | copy-start | bytes 1572868
  539.0 13.0 slice-start.6
  737.4 18.9 %copy-start.75 = (f32[256]{0:T(256)S(1)}, f32[256]{0:T(256)}, u32[]{:S(2)}) copy-start(f32[256]{0:T(256)} %copy-done.74) | copy-start | bytes 3076
  772.5 19.0 %copy-start.61 = (f32[1,2048]{1,0:T(1,128)S(1)}, f32[1,2048]{1,0:T(1,128)}, u32[]{:S(2)}) copy-start(f32[1,2048]{1,0:T(1,128)} %copy-done.60) | copy-start | bytes 24580
  772.5 19.0 %copy-start.82 = (f32[256]{0:T(256)S(1)}, f32[256]{0:T(256)}, u32[]{:S(2)}) copy-start(f32[256]{0:T(256)} %copy-done.81) | copy-start | bytes 3076
  866.0 23.8 %copy-start.59 = (f32[1,2048]{1,0:T(1,128)S(1)}, f32[1,2048]{1,0:T(1,128)}, u32[]{:S(2)}) copy-start(f32[1,2048]{1,0:T(1,128)} %copy-done.58) | copy-start | bytes 24580
  866.0 23.8 %copy-start.77 = (f32[256]{0:T(256)S(1)}, f32[256]{0:T(256)}, u32[]{:S(2)}) copy-start(f32[256]{0:T(256)} %copy-done.76) | copy-start | bytes 3076
  870.7 21.3 %copy-start.20 = (f32[256,2048]{1,0:T(8,128)S(1)}, f32[256,2048]{1,0:T(8,128)}, u32[]{:S(2)}) copy-start(f32[256,2048]{1,0:T(8,128)} %copy-done.19) | copy-start | bytes 6291460
  901.5 9.0 copy-start.21
  914.9 486.2 %all-reduce.14.cloned.1.call-start = ((), (), s32[]{:S(2)}) async-start(), calls=%async_computation.1 | async-start | bytes 1282048 | tf_op jit(solution)/shard_map/psum | solution.py:1212
  1403.3 28.1 %collective-permute-start.2 = (f32[1878,1,128]{2,1,0:T(1,128)S(1)}, f32[1878,1,128]{2,1,0:T(1,128)S(1)}, u32[]{:S(2)}, u32[]{:S(2)}) collective-permute-start(f32[1878,1,128]{2,1,0:T(1,128)S(1)} %slice.341), channel_id=1, source_target_pairs={{0,4},{4,8},{8,12},{12,16},{16,20},{20,24},{24,28},{1,5},{5,9},{9,... | collective-permute-start | bytes 2884616 | tf_op jit(solution)/shard_map/ppermute | solution.py:1230
  1406.9 36.8 %slice-start = ((s8[11694592]{0:T(1024)(128)(4,1)}), s8[4194304]{0:T(1024)(128)(4,1)S(1)}, s32[]{:S(2)}) async-start(s8[11694592]{0:T(1024)(128)(4,1)} %bitcast.127), calls=%async_computation.3 | async-start | bytes 8388608
  1406.9 18.7 %copy-start.10 = (f32[256,2048]{1,0:T(8,128)S(1)}, f32[256,2048]{1,0:T(8,128)}, u32[]{:S(2)}) copy-start(f32[256,2048]{1,0:T(8,128)} %copy-done.7) | copy-start | bytes 6291460
  1406.9 18.7 %copy-start.40 = (bf16[256,2048]{1,0:T(8,128)(2,1)S(1)}, bf16[256,2048]{1,0:T(8,128)(2,1)}, u32[]{:S(2)}) copy-start(bf16[256,2048]{1,0:T(8,128)(2,1)} %all-reduce.16.cloned.1.call-done) | copy-start | bytes 3145732
  1406.9 36.8 %slice-start.1 = ((s8[11694592]{0:T(1024)(128)(4,1)}), s8[4194304]{0:T(1024)(128)(4,1)S(1)}, s32[]{:S(2)}) async-start(s8[11694592]{0:T(1024)(128)(4,1)} %bitcast.127), calls=%async_computation.4 | async-start | bytes 8388608
  1406.9 36.8 %slice-start.2 = ((s8[11694592]{0:T(1024)(128)(4,1)}), s8[3305984]{0:T(1024)(128)(4,1)S(1)}, s32[]{:S(2)}) async-start(s8[11694592]{0:T(1024)(128)(4,1)} %bitcast.127), calls=%async_computation.5 | async-start | bytes 6612992
  1423.0 16.5 %collective-permute-start.3 = (f32[297,1,128]{2,1,0:T(1,128)S(1)}, f32[297,1,128]{2,1,0:T(1,128)S(1)}, u32[]{:S(2)}, u32[]{:S(2)}) collective-permute-start(f32[297,1,128]{2,1,0:T(1,128)S(1)} %slice.342), channel_id=1, source_target_pairs={{4,0},{8,4},{12,8},{16,12},{20,16},{24,20},{28,24},{5,1},{9,5},{13... | collective-permute-start | bytes 456200 | tf_op jit(solution)/shard_map/ppermute | solution.py:1231
  (82 other events, 263.0 us)
Sparse Core Ops, SparseCore 0:
  27.7 79.5 all-reduce.11
  915.0 36.0 all-reduce.15
  954.5 82.7 all-reduce.13
